TPU v7x, 32 devices: a whole 2x2x4 slice. The times are simulated.
32 devices in a mesh: dp: 8 (over y, x, core), tensor: 4 (over z).
Axes of the slice: x: 2, y: 2, z: 4, core: 2. Of those that a mesh axis runs over, the one named last changes fastest.
Arguments:
- tokens: bfloat16 [18432, 768], P(('dp', 'tensor')), may hold values from -6 to 6
- segment_ids: int32 [8, 2304], P('dp'), may hold values from 0 to 7, never falling along the last dimension, each value on 1 to 1152 neighbouring positions
- ln1_gain: float32 [768], replicated, may hold values from 0.5 to 1.5
- ln1_bias: float32 [768], replicated, may hold values from -3 to 3
- qkv_weight: bfloat16 [3, 768, 768], P(None, None, 'tensor'), may hold values from -0.21875 to 0.21875
- qv_bias: float32 [2, 768], P(None, 'tensor'), may hold values from -3 to 3
- proj_weight: bfloat16 [768, 768], P('tensor'), may hold values from -0.875 to 0.875
- proj_bias: float32 [768], replicated, may hold values from -1.75 to 1.75
- scale_one: float32 [768], replicated, may hold values from 0.3 to 1.5
- ln2_gain: float32 [768], replicated, may hold values from 0.5 to 1.5
- ln2_bias: float32 [768], replicated, may hold values from -3 to 3
- fc1_weight: bfloat16 [768, 3072], P(None, 'tensor'), may hold values from -0.21875 to 0.21875
- fc1_bias: float32 [3072], P('tensor'), may hold values from -3 to 3
- fc2_weight: bfloat16 [3072, 768], P('tensor'), may hold values from -0.15625 to 0.15625
- fc2_bias: float32 [768], replicated, may hold values from -1.75 to 1.75
- scale_two: float32 [768], replicated, may hold values from 0.3 to 1.5
- cotangent: bfloat16 [18432, 768], P(('dp', 'tensor')), may hold values from -6 to 6
Outputs:
- block_out: bfloat16 [18432, 768], P(('dp', 'tensor'))
- grad_tokens: float32 [18432, 768], P(('dp', 'tensor'))
- grad_ln1_gain: float32 [768], replicated
- grad_ln1_bias: float32 [768], replicated
- grad_qkv_weight: float32 [3, 768, 768], P(None, None, 'tensor')
- grad_qv_bias: float32 [2, 768], P(None, 'tensor')
- grad_proj_weight: float32 [768, 768], P('tensor')
- grad_proj_bias: float32 [768], replicated
- grad_scale_one: float32 [768], replicated
- grad_ln2_gain: float32 [768], replicated
- grad_ln2_bias: float32 [768], replicated
- grad_fc1_weight: float32 [768, 3072], P(None, 'tensor')
- grad_fc1_bias: float32 [3072], P('tensor')
- grad_fc2_weight: float32 [3072, 768], P('tensor')
- grad_fc2_bias: float32 [768], replicated
- grad_scale_two: float32 [768], replicated
Inputs may be any that keep to these rules, and one draw needn't show every extreme that they name: `segment_ids`: within a sequence the ids never fall; every segment holds at most 1152 tokens, and some segment holds exactly 1152.
All inputs are finite; a program needn't handle non-finite values.
Results may differ from a plain program's by a relative error of at most 0.015.
Values may be sent and summed in bfloat16 or wider, within the bound.
A program may use at most 128 MiB of HBM per device.

v0:
```python
from functools import partial
import math

import jax, jax.numpy as jnp
from jax import lax
from jax.experimental import pallas as pl
from jax.experimental.pallas import tpu as pltpu

from jax.sharding import PartitionSpec as P

HEAD_DIM = 64
LANES = 128
MASKED = -(2.0**100)


def split_three(value):
    high = value.astype(jnp.bfloat16)
    rest = value - high.astype(jnp.float32)
    middle = rest.astype(jnp.bfloat16)
    low = (rest - middle.astype(jnp.float32)).astype(jnp.bfloat16)
    return (high, middle, low)


def join_heads(parts, low_half):
    tiles = []
    for at in range(0, len(parts), 2):
        if at + 1 < len(parts):
            tiles.append(jnp.where(low_half, parts[at], pltpu.roll(parts[at + 1], HEAD_DIM, 1)))
        else:
            tiles.append(parts[at])
    return tiles


def attend_kernel(key_block, bounds_ref, q_ref, k_ref, v_ref, out_ref, q_back_ref, peak_ref, acc_ref):
    step = pl.program_id(0)
    heads, count, _ = q_ref.shape
    peak_ref[...] = jnp.full_like(peak_ref, -3e38)
    acc_ref[...] = jnp.zeros_like(acc_ref)

    def visit(at, carry):
        keys = pl.ds(pl.multiple_of(at * key_block, key_block), key_block)
        for head in range(heads):
            scores = lax.dot_general(
                q_ref[head],
                k_ref[head, keys, :],
                (((1,), (1,)), ((), ())),
                preferred_element_type=jnp.float32,
            )
            old_peak = peak_ref[head]
            new_peak = jnp.maximum(old_peak, jnp.max(scores, axis=1, keepdims=True))
            weights = jnp.exp(scores - new_peak[:, :1]).astype(jnp.bfloat16)
            mixed = jnp.dot(weights, v_ref[head, keys, :], preferred_element_type=jnp.float32)
            acc_ref[head] = acc_ref[head] * jnp.exp(old_peak - new_peak) + mixed
            peak_ref[head] = new_peak
        return carry

    lax.fori_loop(bounds_ref[0, step], bounds_ref[1, step], visit, 0)
    lane = lax.broadcasted_iota(jnp.int32, (count, LANES), 1)
    low_half = lane < HEAD_DIM
    parts = []
    for head in range(heads):
        acc = acc_ref[head]
        total = acc[:, HEAD_DIM : HEAD_DIM + 1]
        parts.append(acc / total)
        log_total = -(peak_ref[head] + jnp.log(total))
        high, middle, low = split_three(log_total)
        kept = q_ref[head].astype(jnp.float32)
        kept = jnp.where(lane == HEAD_DIM + 8, high.astype(jnp.float32), kept)
        kept = jnp.where(lane == HEAD_DIM + 9, middle.astype(jnp.float32), kept)
        kept = jnp.where(lane == HEAD_DIM + 10, low.astype(jnp.float32), kept)
        q_back_ref[head] = kept.astype(jnp.bfloat16)
    for at, tile in enumerate(join_heads(parts, low_half)):
        wide = min(LANES, heads * HEAD_DIM - at * LANES)
        out_ref[:, at * LANES : at * LANES + wide] = tile[:, :wide].astype(jnp.bfloat16)


def attend(bounds, queries, keys, values, key_block):
    heads, seq_len, _ = queries.shape
    steps = bounds.shape[1]
    block = seq_len // steps
    q_spec = pl.BlockSpec((heads, block, LANES), lambda i, b: (0, i, 0))
    full = pl.BlockSpec((heads, seq_len, LANES), lambda i, b: (0, 0, 0))
    return pl.pallas_call(
        partial(attend_kernel, key_block),
        grid_spec=pltpu.PrefetchScalarGridSpec(
            num_scalar_prefetch=1,
            grid=(steps,),
            in_specs=[q_spec, full, full],
            out_specs=[pl.BlockSpec((block, heads * HEAD_DIM), lambda i, b: (i, 0)), q_spec],
            scratch_shapes=[
                pltpu.VMEM((heads, block, LANES), jnp.float32),
                pltpu.VMEM((heads, block, LANES), jnp.float32),
            ],
        ),
        out_shape=[
            jax.ShapeDtypeStruct((seq_len, heads * HEAD_DIM), jnp.bfloat16),
            jax.ShapeDtypeStruct((heads, seq_len, LANES), jnp.bfloat16),
        ],
        name="attend",
        cost_estimate=pl.CostEstimate(
            flops=4 * heads * seq_len * seq_len * LANES // 2, transcendentals=heads * seq_len * seq_len // 2,
            bytes_accessed=8 * heads * seq_len * LANES,
        ),
    )(bounds, queries, keys, values)


def attend_back_kernel(
    query_block, bounds_ref, q_ref, k_ref, v_ref, mixed_ref, grad_ref, out_ref, grad_heads_ref, dq_ref, dk_ref, dv_ref, k0_ref
):
    step = pl.program_id(0)
    heads, count, _ = k_ref.shape
    seq_len = q_ref.shape[1]
    blocks = seq_len // query_block

    @pl.when(step == 0)
    def _():
        dq_ref[...] = jnp.zeros_like(dq_ref)

        def prepare(at, carry):
            rows = pl.ds(pl.multiple_of(at * query_block, query_block), query_block)
            lane = lax.broadcasted_iota(jnp.int32, (query_block, LANES), 1)
            for head in range(heads):
                first = (head // 2) * LANES
                wide = min(LANES, heads * HEAD_DIM - first)
                grad = grad_ref[rows, first : first + wide].astype(jnp.float32)
                mixed = mixed_ref[rows, first : first + wide].astype(jnp.float32)
                if wide < LANES:
                    blank = jnp.zeros((query_block, LANES - wide), jnp.float32)
                    grad = jnp.concatenate([grad, blank], axis=1)
                    mixed = jnp.concatenate([mixed, blank], axis=1)
                if head % 2:
                    grad = pltpu.roll(grad, HEAD_DIM, 1)
                    mixed = pltpu.roll(mixed, HEAD_DIM, 1)
                inside = lane < HEAD_DIM
                shared = -jnp.sum(jnp.where(inside, grad * mixed, 0.0), axis=1, keepdims=True)
                high, middle, low = split_three(shared)
                grad = jnp.where(inside, grad, 0.0)
                grad = jnp.where(lane == HEAD_DIM, high.astype(jnp.float32), grad)
                grad = jnp.where(lane == HEAD_DIM + 1, middle.astype(jnp.float32), grad)
                grad = jnp.where(lane == HEAD_DIM + 2, low.astype(jnp.float32), grad)
                grad_heads_ref[head, rows, :] = grad.astype(jnp.bfloat16)
            return carry

        lax.fori_loop(0, blocks, prepare, 0)

    dk_ref[...] = jnp.zeros_like(dk_ref)
    dv_ref[...] = jnp.zeros_like(dv_ref)

    def visit(at, carry):
        rows = pl.ds(pl.multiple_of(at * query_block, query_block), query_block)
        for head in range(heads):
            queries = q_ref[head, rows, :]
            grads = grad_heads_ref[head, rows, :]
            keys = k_ref[head]
            contract = (((1,), (1,)), ((), ()))
            scores = lax.dot_general(keys, queries, contract, preferred_element_type=jnp.float32)
            probs = jnp.exp(scores)
            grad_probs = lax.dot_general(
                v_ref[head], grads, contract, preferred_element_type=jnp.float32
            )
            grad_scores = (probs * grad_probs).astype(jnp.bfloat16)
            dv_ref[head] += jnp.dot(
                probs.astype(jnp.bfloat16), grads, preferred_element_type=jnp.float32
            )
            dk_ref[head] += jnp.dot(grad_scores, queries, preferred_element_type=jnp.float32)
            dq_ref[head, rows, :] += lax.dot_general(
                grad_scores, keys, (((0,), (0,)), ((), ())), preferred_element_type=jnp.float32
            )
        return carry

    lax.fori_loop(bounds_ref[0, step], bounds_ref[1, step], visit, 0)
    lane = lax.broadcasted_iota(jnp.int32, (count, LANES), 1)
    low_half = lane < HEAD_DIM
    here = pl.ds(pl.multiple_of(step * count, count), count)
    k0_ref[here, :] = dk_ref[0]
    out_ref[here, 256:384] = jnp.where(
        low_half, dk_ref[1], pltpu.roll(dk_ref[2], HEAD_DIM, 1)
    ).astype(jnp.bfloat16)
    out_ref[here, 384:512] = jnp.where(
        low_half, dv_ref[0], pltpu.roll(dv_ref[1], HEAD_DIM, 1)
    ).astype(jnp.bfloat16)
    out_ref[here, 512:576] = dv_ref[2][:, :HEAD_DIM].astype(jnp.bfloat16)

    @pl.when(step == pl.num_programs(0) - 1)
    def _():
        def finish(at, carry):
            rows = pl.ds(pl.multiple_of(at * query_block, query_block), query_block)
            lane = lax.broadcasted_iota(jnp.int32, (query_block, LANES), 1)
            low_half = lane < HEAD_DIM
            scale = HEAD_DIM**-0.5
            out_ref[rows, 0:128] = (
                jnp.where(low_half, dq_ref[0, rows, :], pltpu.roll(dq_ref[1, rows, :], HEAD_DIM, 1))
                * scale
            ).astype(jnp.bfloat16)
            out_ref[rows, 128:256] = jnp.where(
                low_half, dq_ref[2, rows, :] * scale, pltpu.roll(k0_ref[rows, :], HEAD_DIM, 1)
            ).astype(jnp.bfloat16)
            return carry

        lax.fori_loop(0, blocks, finish, 0)


def attend_back(bounds, queries, keys, values, mixed, grads, query_block):
    heads, seq_len, _ = queries.shape
    steps = bounds.shape[1]
    block = seq_len // steps
    k_spec = pl.BlockSpec((heads, block, LANES), lambda i, b: (0, i, 0))
    full = pl.BlockSpec((heads, seq_len, LANES), lambda i, b: (0, 0, 0))
    flat = pl.BlockSpec((seq_len, heads * HEAD_DIM), lambda i, b: (0, 0))
    return pl.pallas_call(
        partial(attend_back_kernel, query_block),
        grid_spec=pltpu.PrefetchScalarGridSpec(
            num_scalar_prefetch=1,
            grid=(steps,),
            in_specs=[full, k_spec, k_spec, flat, flat],
            out_specs=pl.BlockSpec((seq_len, 3 * heads * HEAD_DIM), lambda i, b: (0, 0)),
            scratch_shapes=[
                pltpu.VMEM((heads, seq_len, LANES), jnp.bfloat16),
                pltpu.VMEM((heads, seq_len, LANES), jnp.float32),
                pltpu.VMEM((heads, block, LANES), jnp.float32),
                pltpu.VMEM((heads, block, LANES), jnp.float32),
                pltpu.VMEM((seq_len, LANES), jnp.float32),
            ],
        ),
        out_shape=jax.ShapeDtypeStruct((seq_len, 3 * heads * HEAD_DIM), jnp.bfloat16),
        name="attend_back",
        cost_estimate=pl.CostEstimate(
            flops=10 * heads * seq_len * seq_len * LANES // 2, transcendentals=heads * seq_len * seq_len // 2,
            bytes_accessed=12 * heads * seq_len * LANES,
        ),
    )(bounds, queries, keys, values, mixed, grads)


def visit_bounds(ids, steps, block):
    seq_len = ids.shape[0]
    count = seq_len // steps
    first = ids[::count][:steps]
    last = ids[count - 1 :: count]
    start = jnp.sum(ids[None, :] < first[:, None], axis=1, dtype=jnp.int32)
    end = jnp.sum(ids[None, :] <= last[:, None], axis=1, dtype=jnp.int32)
    return jnp.stack([start // block, (end + block - 1) // block])


MESH = pl.DeviceIdType.MESH
PIECES = 8
PIECE_BITS = 3


def contract_rows(left, right):
    return lax.dot_general(left, right, (((0,), (0,)), ((), ())), preferred_element_type=jnp.float32)


def times_transposed(left, right, precision=None):
    return lax.dot_general(
        left, right, (((1,), (1,)), ((), ())), preferred_element_type=jnp.float32, precision=precision
    )


def rounded_sum(left, right):
    return (left.astype(jnp.float32) + right.astype(jnp.float32)).astype(jnp.bfloat16)


def bit_of(index, bit):
    return lax.rem(index // (1 << bit), 2)


def partner_of(index, bit):
    return index + (1 - 2 * bit_of(index, bit)) * (1 << bit)


def greet(dp_bits, shards):
    barrier = pltpu.get_barrier_semaphore()
    member, here = lax.axis_index("dp"), lax.axis_index("tensor")
    peers = [{"dp": partner_of(member, bit)} for bit in range(dp_bits)]
    peers += [{"tensor": lax.rem(here + shift, shards)} for shift in range(1, shards)]
    for peer in peers:
        pl.semaphore_signal(barrier, inc=1, device_id=peer, device_id_type=MESH)
    pl.semaphore_wait(barrier, len(peers))


def finish_kernel(
    shards,
    dp_bits,
    grads_ref,
    rows_ref,
    weight_ref,
    gain_ref,
    shift_ref,
    vectors_ref,
    tokens_ref,
    hidden_ref,
    a_keep,
    a_got,
    b_keep,
    b_got,
    tokens_out,
    vectors_out,
    qkv_out,
    weights_out,
    part,
    from_left,
    from_right,
    q_wide,
    q_all,
    q_half,
    q_quarter,
    q_got_core,
    q_got_x,
    q_got_y,
    q_got_more,
    v_now,
    v_got,
    v_shards,
    a_sum,
    b_sum,
    a_second,
    b_second,
    pieces,
    pieces_more,
    z_got,
    send,
    recv,
):
    f32, bf16 = jnp.float32, jnp.bfloat16
    member, here = lax.axis_index("dp"), lax.axis_index("tensor")
    core, x_bit, y_bit = bit_of(member, 0), bit_of(member, 1), bit_of(member, 2)
    own_piece = core * 4 + x_bit * 2 + y_bit
    block = part.shape[1]
    width = part.shape[2]
    columns = grads_ref.shape[1]
    half_rows = weights_out.shape[1] // 2
    last = shards - 1
    slots = iter(range(send.shape[0]))
    pending = []

    def copy_to(src, dst, at, **peer):
        return pltpu.make_async_remote_copy(
            src_ref=src, dst_ref=dst, send_sem=send.at[at], recv_sem=recv.at[at], device_id=peer, device_id_type=MESH
        )

    def start_dp(src, dst, bit, keep=True):
        copy = copy_to(src, dst, next(slots), dp=partner_of(member, bit))
        copy.start()
        if keep:
            pending.append(copy)
        return copy

    greet(dp_bits, shards)

    def add_into(out, left, right):
        def step(at, carry):
            out[at] = rounded_sum(left[at], right[at])
            return carry

        lax.fori_loop(0, out.shape[0], step, 0)

    def sum_pairs(out, left, right):
        def step(at, carry):
            one, two = at // out.shape[1], lax.rem(at, out.shape[1])
            out[one, two] = rounded_sum(left[one, two], right[one, two])
            return carry

        lax.fori_loop(0, out.shape[0] * out.shape[1], step, 0)

    sum_pairs(a_sum, a_keep, a_got)
    sum_pairs(b_sum, b_keep, b_got)
    second_a = start_dp(a_sum.at[1 - y_bit], a_second, 2)
    second_b = start_dp(b_sum.at[1 - x_bit], b_second, 1)

    right_slots = [next(slots) for _ in range(shards)]
    left_slots = [next(slots) for _ in range(shards)]

    def to_right(owner):
        return copy_to(part.at[owner], from_left.at[owner], right_slots[owner], tensor=lax.rem(here + 1, shards))

    def to_left(owner):
        return copy_to(
            part.at[owner], from_right.at[owner], left_slots[owner], tensor=lax.rem(here + last, shards)
        )

    def add_arrived(owner, arrived):
        def step(at, carry):
            rows = pl.ds(pl.multiple_of(at * (block // 4), 16), block // 4)
            part[owner, rows, :] = rounded_sum(part[owner, rows, :], arrived[owner, rows, :])
            return carry

        lax.fori_loop(0, 4, step, 0)

    order = []
    for near in range((shards + 1) // 2):
        for owner in (last - near, near):
            if owner not in order:
                order.append(owner)
    for owner in order:
        product = times_transposed(grads_ref[owner * block : (owner + 1) * block, :], weight_ref[...])
        part[owner] = product.astype(bf16)
        if owner > 0:

            @pl.when(here == 0)
            def _():
                to_right(owner).start()

        if owner < last:

            @pl.when(here == last)
            def _():
                to_left(owner).start()

    def hop(time):
        for owner in range(shards):
            at = time - (last - owner)
            if 0 < at < owner:

                @pl.when(here == at)
                def _():
                    to_right(owner).wait_recv()
                    add_arrived(owner, from_left)
                    to_right(owner).start()

            at = last + owner - time
            if owner < at < last:

                @pl.when(here == at)
                def _():
                    to_left(owner).wait_recv()
                    add_arrived(owner, from_right)
                    to_left(owner).start()

    q_wide[...] = jnp.zeros_like(q_wide)

    def grow(at, carry):
        rows = pl.ds(pl.multiple_of(at * block, 16), block)
        q_wide[...] += contract_rows(rows_ref[rows, :], grads_ref[rows, :])
        return carry

    lax.fori_loop(0, shards, grow, 0)
    sums = jnp.dot(jnp.ones((8, grads_ref.shape[0]), bf16), grads_ref[...], preferred_element_type=f32)
    exact = lax.Precision.HIGHEST
    weight = weight_ref[...].astype(f32)
    shift_sum = times_transposed(sums, weight, exact)[0:1]
    gain_sum = times_transposed(jnp.ones((8, columns), f32), weight * q_wide[...], exact)[0:1]
    v_now[0] = vectors_ref[...]
    v_now[0, 0:1, :] = (gain_sum - shift_ref[...] * shift_sum) / gain_ref[...]
    v_now[0, 1:2, :] = shift_sum
    v_now[0, pl.ds(12 + here, 1), 0:columns] = sums[0:1]
    count = q_all.shape[1]
    for piece in range(PIECES):
        q_all[piece] = q_wide[piece * count : (piece + 1) * count, :].astype(bf16)

    def vector_stage(bit):
        return start_dp(v_now.at[bit], v_got.at[bit], bit)

    q_core = start_dp(q_all.at[pl.ds((1 - core) * 4, 4)], q_got_core, 0)
    v_copy = vector_stage(0)

    second_a.wait_recv()
    second_b.wait_recv()
    pairs = shards // 2
    for at in range(pairs):
        pieces[at] = rounded_sum(a_sum[y_bit, at], a_second[at])
        pieces[pairs + at] = rounded_sum(b_sum[x_bit, at], b_second[at])
    for bit in range(PIECE_BITS, dp_bits):
        extra = start_dp(pieces, pieces_more.at[bit - PIECE_BITS], bit, False)
        extra.wait_recv()
        extra.wait_send()
        add_into(pieces, pieces, pieces_more.at[bit - PIECE_BITS])
    z_copies = []
    for shift in range(1, shards):
        target = lax.rem(here + shift, shards)
        copy = copy_to(pieces.at[target], z_got.at[shift - 1], next(slots), tensor=target)
        copy.start()
        z_copies.append(copy)
    pending.extend(z_copies)

    q_core.wait_recv()
    for at in range(4):
        q_half[at] = rounded_sum(q_all[core * 4 + at], q_got_core[at])
    q_x = start_dp(q_half.at[pl.ds((1 - x_bit) * 2, 2)], q_got_x, 1)
    v_copy.wait_recv()
    v_now[1] = v_now[0] + v_got[0]
    v_copy = vector_stage(1)
    if last > 1:
        hop(1)
    q_x.wait_recv()
    for at in range(2):
        q_quarter[at] = rounded_sum(q_half[x_bit * 2 + at], q_got_x[at])
    q_y = start_dp(q_quarter.at[1 - y_bit], q_got_y, 2)
    v_copy.wait_recv()
    v_now[2] = v_now[1] + v_got[1]
    v_copy = vector_stage(2)
    q_y.wait_recv()
    qkv_out[own_piece] = rounded_sum(q_quarter[y_bit], q_got_y[...])
    v_copy.wait_recv()
    v_now[3] = v_now[2] + v_got[2]
    for bit in range(PIECE_BITS, dp_bits):
        extra = start_dp(qkv_out.at[own_piece], q_got_more.at[bit - PIECE_BITS], bit, False)
        v_copy = vector_stage(bit)
        extra.wait_recv()
        extra.wait_send()
        qkv_out[own_piece] = rounded_sum(qkv_out[own_piece], q_got_more[bit - PIECE_BITS])
        v_copy.wait_recv()
        v_now[bit + 1] = v_now[bit] + v_got[bit]
    v_shards[here] = v_now[dp_bits]
    for shift in range(1, shards):
        copy = copy_to(
            v_now.at[dp_bits], v_shards.at[here], next(slots), tensor=lax.rem(here + shift, shards)
        )
        copy.start()
        pending.append(copy)
    v_waits = pending[-last:]
    q_back = start_dp(qkv_out.at[own_piece], qkv_out.at[own_piece], 2)
    q_back.wait_recv()
    q_back = start_dp(
        qkv_out.at[pl.ds(core * 4 + x_bit * 2, 2)], qkv_out.at[pl.ds(core * 4 + x_bit * 2, 2)], 1
    )
    for time in range(2, last):
        hop(time)
    q_back.wait_recv()
    q_back = start_dp(qkv_out.at[pl.ds(core * 4, 4)], qkv_out.at[pl.ds(core * 4, 4)], 0)

    for copy in z_copies:
        copy.wait_recv()
    total = pieces[here].astype(f32)
    for shift in range(1, shards):
        total = total + z_got[shift - 1].astype(f32)
    weights_out[own_piece] = total.astype(bf16)

    def own_half(low, *index):
        rows = pl.ds(0 if low else half_rows, half_rows)
        return weights_out.at[index[0], rows]

    back_a = start_dp(own_half(True, own_piece), own_half(True, own_piece), 2)
    back_b = start_dp(own_half(False, own_piece), own_half(False, own_piece), 1)
    back_a.wait_recv()
    span = pl.ds(core * 4 + x_bit * 2, 2)
    back_a = start_dp(own_half(True, span), own_half(True, span), 1)
    back_b.wait_recv()
    back_c = [
        start_dp(own_half(False, core * 4 + 2 * at + y_bit), own_half(False, core * 4 + 2 * at + y_bit), 2)
        for at in range(2)
    ]
    back_a.wait_recv()
    for copy in back_c:
        copy.wait_recv()
    span = pl.ds(core * 4, 4)
    back_core = start_dp(weights_out.at[span], weights_out.at[span], 0)

    for copy in v_waits:
        copy.wait_recv()
    vectors_sum = v_shards[0]
    for at in range(1, shards):
        vectors_sum = vectors_sum + v_shards[at]
    vectors_out[...] = vectors_sum

    for owner in range(shards):

        @pl.when(here == owner)
        def _():
            if owner > 0:
                to_right(owner).wait_recv()
                add_arrived(owner, from_left)
            if owner < last:
                to_left(owner).wait_recv()
                add_arrived(owner, from_right)

    def close(at, carry):
        rows = pl.ds(pl.multiple_of(at * (block // 4), 16), block // 4)
        tokens = tokens_ref[rows, :].astype(f32)
        centred = tokens - jnp.mean(tokens, axis=1, keepdims=True)
        inverse = lax.rsqrt(jnp.mean(centred * centred, axis=1, keepdims=True) + eps_norm)
        unit = centred * inverse
        scaled = part[here, rows, :].astype(f32) * gain_ref[...]
        inner = (
            scaled
            - jnp.mean(scaled, axis=1, keepdims=True)
            - unit * jnp.mean(scaled * unit, axis=1, keepdims=True)
        )
        tokens_out[rows, :] = hidden_ref[rows, :] + inverse * inner
        return carry

    lax.fori_loop(0, 4, close, 0)
    q_back.wait_recv()
    back_core.wait_recv()
    for copy in pending:
        copy.wait_send()
    for owner in range(shards):

        @pl.when(here < owner)
        def _():
            to_right(owner).wait_send()

        @pl.when(here > owner)
        def _():
            to_left(owner).wait_send()


def finish(shards, members, grads, rows, weight, gain, shift, vectors, tokens, grad_hidden, a_keep, a_got, b_keep, b_got):
    dp_bits = members.bit_length() - 1
    assert members == 1 << dp_bits and dp_bits >= PIECE_BITS
    f32, bf16 = jnp.float32, jnp.bfloat16
    seq_len, columns = grads.shape
    block, width = tokens.shape
    piece_rows = a_keep.shape[2]
    count = width // PIECES
    more = max(1, dp_bits - PIECE_BITS)
    copies = 16 + 2 * shards + 2 * (shards - 1) + 3 * dp_bits
    vm = pltpu.VMEM
    return pl.pallas_call(
        partial(finish_kernel, shards, dp_bits),
        in_specs=[pl.BlockSpec(memory_space=vm)] * 12,
        out_specs=[pl.BlockSpec(memory_space=vm)] * 4,
        out_shape=[
            jax.ShapeDtypeStruct((block, width), f32),
            jax.ShapeDtypeStruct(vectors.shape, f32),
            jax.ShapeDtypeStruct((PIECES, count, columns), bf16),
            jax.ShapeDtypeStruct((PIECES, piece_rows, width), bf16),
        ],
        scratch_shapes=[
            vm((shards, block, width), bf16),
            vm((shards, block, width), bf16),
            vm((shards, block, width), bf16),
            vm((width, columns), f32),
            vm((PIECES, count, columns), bf16),
            vm((4, count, columns), bf16),
            vm((2, count, columns), bf16),
            vm((4, count, columns), bf16),
            vm((2, count, columns), bf16),
            vm((count, columns), bf16),
            vm((more, count, columns), bf16),
            vm((dp_bits + 1,) + vectors.shape, f32),
            vm((dp_bits,) + vectors.shape, f32),
            vm((shards,) + vectors.shape, f32),
            vm(a_keep.shape, bf16),
            vm(b_keep.shape, bf16),
            vm(a_keep.shape[1:], bf16),
            vm(b_keep.shape[1:], bf16),
            vm((shards, piece_rows, width), bf16),
            vm((more, shards, piece_rows, width), bf16),
            vm((shards - 1, piece_rows, width), bf16),
            pltpu.SemaphoreType.DMA((copies,)),
            pltpu.SemaphoreType.DMA((copies,)),
        ],
        compiler_params=pltpu.CompilerParams(
            collective_id=1, has_side_effects=True, vmem_limit_bytes=64 * 1024 * 1024 - 2048 * 1024
        ),
        name="finish",
        cost_estimate=pl.CostEstimate(
            flops=4 * seq_len * columns * width, transcendentals=0, bytes_accessed=40 * block * width
        ),
    )(grads, rows, weight, gain, shift, vectors, tokens, grad_hidden, a_keep, a_got, b_keep, b_got)


def start_kernel(
    shards,
    dp_bits,
    tokens_ref,
    ids_ref,
    gain_ref,
    shift_ref,
    qkv_ref,
    qv_bias_ref,
    fc1_ref,
    fc2_ref,
    proj_ref,
    fc1_bias_ref,
    normed_out,
    q_out,
    k_out,
    v_out,
    weights_out,
    bias_out,
    blocks,
    q_extra,
    k_extra,
    own,
    chain,
    send,
    recv,
    local,
):
    f32, bf16 = jnp.float32, jnp.bfloat16
    member, here = lax.axis_index("dp"), lax.axis_index("tensor")
    core, x_bit, y_bit = bit_of(member, 0), bit_of(member, 1), bit_of(member, 2)
    own_piece = core * 4 + x_bit * 2 + y_bit
    block, width = tokens_ref.shape
    heads = q_out.shape[0]
    seq_len = ids_ref.shape[1]
    last = shards - 1
    slots = iter(range(send.shape[0]))
    pending = []

    def copy_to(src, dst, at, **peer):
        return pltpu.make_async_remote_copy(
            src_ref=src, dst_ref=dst, send_sem=send.at[at], recv_sem=recv.at[at], device_id=peer, device_id_type=MESH
        )

    def start_dp(src, dst, bit):
        copy = copy_to(src, dst, next(slots), dp=partner_of(member, bit))
        copy.start()
        pending.append(copy)
        return copy

    fc1_rows, fc2_rows, proj_rows = (ref.shape[0] // PIECES for ref in (fc1_ref, fc2_ref, proj_ref))
    loads = []
    for at, (ref, first, count) in enumerate(
        ((fc1_ref, 0, fc1_rows), (fc2_ref, fc1_rows, fc2_rows))
    ):
        rows = pl.ds(pl.multiple_of(own_piece * count, 16), count)
        loads.append(pltpu.make_async_copy(ref.at[rows], own.at[first : first + count], local.at[at]))
        loads[-1].start()
    used = fc1_rows + fc2_rows
    rows = pl.ds(pl.multiple_of(own_piece * proj_rows, 8), proj_rows)
    own[used : used + proj_rows, :] = proj_ref[rows, :]
    used += proj_rows
    own[used:, :] = jnp.zeros((own.shape[0] - used, width), bf16)
    greet(dp_bits, shards)
    for load in loads:
        load.wait()

    chains = {}
    for name, first, rest in (("w", own, chain), ("t", tokens_ref, blocks)):
        chains[name] = (
            first,
            rest,
            [next(slots) for _ in range(shards)],
            [next(slots) for _ in range(shards)],
        )

    def hop_copy(name, owner, rightward, from_own):
        first, rest, right_slots, left_slots = chains[name]
        src = first if from_own else rest.at[owner]
        step = 1 if rightward else last
        at = (right_slots if rightward else left_slots)[owner]
        return copy_to(src, rest.at[owner], at, tensor=lax.rem(here + step, shards))

    def send_own(name, rightward):
        for owner in range(shards):
            if owner != (last if rightward else 0):

                @pl.when(here == owner)
                def _():
                    hop_copy(name, owner, rightward, True).start()

    def hop(name, time, then=None):
        for at in range(shards):
            for rightward, owner, end in ((True, at - time, last), (False, at + time, 0)):
                if 0 <= owner <= last:

                    @pl.when(here == at)
                    def _():
                        hop_copy(name, owner, rightward, False).wait_recv()
                        if at != end:
                            hop_copy(name, owner, rightward, False).start()
                            if then is not None and owner in (0, last):
                                hop_copy(then, at, rightward, True).start()

    send_own("w", True)
    send_own("w", False)

    @pl.when(here == 0)
    def _():
        hop_copy("t", 0, True, True).start()

    @pl.when(here == last)
    def _():
        hop_copy("t", last, False, True).start()

    bias_copies = []
    bias_out[here] = fc1_bias_ref[...]
    for shift in range(1, shards):
        copy = copy_to(
            fc1_bias_ref, bias_out.at[here], next(slots), tensor=lax.rem(here + shift, shards)
        )
        copy.start()
        bias_copies.append(copy)
    pending.extend(bias_copies)

    large = -MASKED
    segments = lax.broadcasted_iota(jnp.int32, (8, seq_len), 0)
    same = jnp.where(segments == ids_ref[...], 1.0, 0.0).astype(bf16)
    select = lax.broadcasted_iota(jnp.int32, (8, LANES), 1) - HEAD_DIM == lax.broadcasted_iota(
        jnp.int32, (8, LANES), 0
    )
    matched = contract_rows(same, jnp.where(select, 1.0, 0.0).astype(bf16))
    lane = lax.broadcasted_iota(jnp.int32, (seq_len, LANES), 1)
    segment_lane = (lane >= HEAD_DIM) & (lane < HEAD_DIM + 8)
    ones_lane = (lane >= HEAD_DIM + 8) & (lane < HEAD_DIM + 11)
    q_extra[...] = jnp.where(segment_lane, (matched - 1.0) * large, 0.0).astype(bf16)
    k_extra[...] = jnp.where(ones_lane, 1.0, matched).astype(bf16)
    low_half = lax.broadcasted_iota(jnp.int32, (block, LANES), 1) < HEAD_DIM
    v_lane = lax.broadcasted_iota(jnp.int32, (block, LANES), 1)
    v_extra = jnp.where((v_lane >= HEAD_DIM) & (v_lane < HEAD_DIM + 3), 1.0, 0.0).astype(bf16)

    def project_block(source, owner):
        tokens = source.astype(f32)
        centred = tokens - jnp.mean(tokens, axis=1, keepdims=True)
        inverse = lax.rsqrt(jnp.mean(centred * centred, axis=1, keepdims=True) + eps_norm)
        normed = (centred * inverse * gain_ref[...] + shift_ref[...]).astype(bf16)
        rows = pl.ds(pl.multiple_of(owner * block, 16), block)
        normed_out[rows, :] = normed
        for which, out in ((0, q_out), (1, k_out), (2, v_out)):
            product = jnp.dot(normed, qkv_ref[which], preferred_element_type=f32)
            if which != 1:
                product = product + qv_bias_ref[which // 2 : which // 2 + 1, :]
            if which == 0:
                product = product.astype(bf16).astype(f32) * HEAD_DIM**-0.5
            extra = v_extra if which == 2 else (q_extra if which == 0 else k_extra)[rows, :]
            for head in range(heads):
                first = (head // 2) * LANES
                tile = product[:, first : first + LANES]
                if tile.shape[1] < LANES:
                    blank = jnp.zeros((block, LANES - tile.shape[1]), f32)
                    tile = jnp.concatenate([tile, blank], axis=1)
                if head % 2:
                    tile = pltpu.roll(tile, HEAD_DIM, 1)
                out[head, rows, :] = jnp.where(low_half, tile, extra.astype(f32)).astype(bf16)

    project_block(tokens_ref[...], here)
    for time in range(1, shards):
        hop("w", time, "t")

    half = shards // 2
    out_a = [weights_out.at[own_piece, 0:half]]
    stores = []
    for owner in range(shards):
        at = 2 + owner

        @pl.when(here == owner)
        def _():
            pltpu.make_async_copy(own, weights_out.at[own_piece, owner], local.at[at]).start()

        @pl.when(here != owner)
        def _():
            pltpu.make_async_copy(chain.at[owner], weights_out.at[own_piece, owner], local.at[at]).start()

        stores.append(pltpu.make_async_copy(own, weights_out.at[own_piece, owner], local.at[at]))
    for store in stores:
        store.wait()

    def part(low, pieces):
        owners = pl.ds(0, half) if low else pl.ds(half, shards - half)
        return weights_out.at[pieces, owners]

    def gather_stage(low, pieces, bit):
        return [start_dp(part(low, at), part(low, at), bit) for at in pieces]

    def wait_all(copies):
        for copy in copies:
            copy.wait_recv()

    stage = gather_stage(True, [own_piece], 2) + gather_stage(False, [own_piece], 1)

    def arrived(time):
        for way in (-1, 1):
            owner = here + way * time

            @pl.when((owner >= 0) & (owner <= last))
            def _():
                project_block(blocks[owner], owner)

    for time in range(1, shards):
        hop("t", time)
        if time == 1:
            arrived(time)
            wait_all(stage)
            stage = gather_stage(True, [pl.ds(core * 4 + x_bit * 2, 2)], 1) + gather_stage(
                False, [core * 4 + 2 * at + y_bit for at in range(2)], 2
            )
        elif time == 2:
            arrived(time)
            wait_all(stage)
            stage = [start_dp(weights_out.at[pl.ds(core * 4, 4)], weights_out.at[pl.ds(core * 4, 4)], 0)]
        else:
            arrived(time)
    wait_all(stage)
    wait_all(bias_copies)
    for copy in pending:
        copy.wait_send()
    for name in chains:
        for at in range(shards):
            for owner in range(shards):
                if owner <= at < last:

                    @pl.when(here == at)
                    def _():
                        hop_copy(name, owner, True, False).wait_send()

                if owner >= at > 0:

                    @pl.when(here == at)
                    def _():
                        hop_copy(name, owner, False, False).wait_send()


def start(shards, members, tokens, ids, gain, shift, qkv, qv_bias, fc1, fc2, proj, fc1_bias):
    dp_bits = members.bit_length() - 1
    assert members == 1 << dp_bits and dp_bits >= PIECE_BITS and shards >= 3
    f32, bf16 = jnp.float32, jnp.bfloat16
    block, width = tokens.shape
    seq_len = block * shards
    heads = qkv.shape[2] // HEAD_DIM
    rows = -(-(fc1.shape[0] + fc2.shape[0] + proj.shape[0]) // PIECES // 16) * 16
    copies = 4 * shards + (shards - 1) + 6
    vm = pltpu.VMEM
    on_chip = pl.BlockSpec(memory_space=vm)
    anywhere = pl.BlockSpec(memory_space=pl.ANY)
    head_rows = jax.ShapeDtypeStruct((heads, seq_len, LANES), bf16)
    return pl.pallas_call(
        partial(start_kernel, shards, dp_bits),
        in_specs=[on_chip] * 6 + [anywhere] * 2 + [on_chip] * 2,
        out_specs=[on_chip] * 4 + [anywhere, on_chip],
        out_shape=[
            jax.ShapeDtypeStruct((seq_len, width), bf16),
            head_rows,
            head_rows,
            head_rows,
            jax.ShapeDtypeStruct((PIECES, shards, rows, width), bf16),
            jax.ShapeDtypeStruct((shards,) + fc1_bias.shape, f32),
        ],
        scratch_shapes=[
            vm((shards, block, width), bf16),
            vm((seq_len, LANES), bf16),
            vm((seq_len, LANES), bf16),
            vm((rows, width), bf16),
            vm((shards, rows, width), bf16),
            pltpu.SemaphoreType.DMA((copies,)),
            pltpu.SemaphoreType.DMA((copies,)),
            pltpu.SemaphoreType.DMA((2 + shards,)),
        ],
        compiler_params=pltpu.CompilerParams(collective_id=0, has_side_effects=True),
        name="start",
        cost_estimate=pl.CostEstimate(
            flops=6 * seq_len * width * heads * HEAD_DIM, transcendentals=0, bytes_accessed=40 * block * width
        ),
    )(tokens, ids, gain, shift, qkv, qv_bias, fc1, fc2, proj, fc1_bias)


CHUNK = 32


def middle_kernel(
    shards,
    dp_bits,
    mixed_ref,
    weights_ref,
    fc1_bias_ref,
    params_ref,
    tokens_ref,
    cotangent_ref,
    block_out,
    hidden_grad_out,
    mixed_grad_out,
    vectors_out,
    a_keep,
    a_away,
    b_keep,
    b_away,
    weights,
    attended,
    branch,
    hidden,
    normed,
    wide,
    total,
    active,
    slope,
    grad_pre,
    grad_mlp,
    grad_branch,
    grad_attended,
    got,
    send,
    recv,
    local,
):
    f32, bf16 = jnp.float32, jnp.bfloat16
    member, here = lax.axis_index("dp"), lax.axis_index("tensor")
    core, x_bit, y_bit = bit_of(member, 0), bit_of(member, 1), bit_of(member, 2)
    block, width = tokens_ref.shape
    columns = mixed_ref.shape[1]
    half = PIECES // 2
    fc_rows, proj_rows = width // PIECES, columns // PIECES
    proj_first = 2 * fc_rows
    slots = iter(range(send.shape[0]))
    proj_bias, scale_one, gain, shift, fc2_bias, scale_two = (
        params_ref[at : at + 1, :] for at in range(6)
    )

    def copy_to(src, dst, at, **peer):
        return pltpu.make_async_remote_copy(
            src_ref=src, dst_ref=dst, send_sem=send.at[at], recv_sem=recv.at[at], device_id=peer, device_id_type=MESH
        )

    loads = []
    for owner in range(shards):
        load = pltpu.make_async_copy(weights_ref.at[:, owner], weights.at[:, owner], local.at[owner])
        load.start()
        loads.append(load)
    greet(dp_bits, shards)

    def rows_of(owner):
        return pl.ds(pl.multiple_of(owner * block, 16), block)

    copies = []
    for way in range(1, shards):
        target = lax.rem(here + way, shards)
        copy = copy_to(mixed_ref.at[rows_of(target)], attended.at[here], next(slots), tensor=target)
        copy.start()
        copies.append(copy)
    attended[here] = mixed_ref[rows_of(here), :]
    for load in loads:
        load.wait()

    def fc1_of(owner):
        return weights[:, owner, :fc_rows, :].reshape(width, width)

    def fc2_of(owner):
        return weights[:, owner, fc_rows:proj_first, :].reshape(width, width)

    def proj_of(owner):
        return weights[:, owner, proj_first : proj_first + proj_rows, :].reshape(columns, width)

    def chunk(at):
        return pl.ds(pl.multiple_of(at * CHUNK, CHUNK), CHUNK)

    def each_chunk(body, init):
        return lax.fori_loop(0, block // CHUNK, body, init)

    def column_sum(value):
        return jnp.sum(value, axis=0, keepdims=True)

    def unit_of(value):
        centred = value - jnp.mean(value, axis=1, keepdims=True)
        inverse = lax.rsqrt(jnp.mean(centred * centred, axis=1, keepdims=True) + eps_norm)
        return centred * inverse, inverse

    for copy in copies:
        copy.wait_recv()
    product = jnp.dot(attended[0], proj_of(0), preferred_element_type=f32)
    for owner in range(1, shards):
        product += jnp.dot(attended[owner], proj_of(owner), preferred_element_type=f32)
    branch[...] = product

    def enter(at, carry):
        rows = chunk(at)
        value = branch[rows, :] + proj_bias
        branch[rows, :] = value
        value = tokens_ref[rows, :].astype(f32) + scale_one * value
        hidden[rows, :] = value
        unit, _ = unit_of(value)
        normed[rows, :] = (unit * gain + shift).astype(bf16)
        return carry

    each_chunk(enter, 0)

    def forward(owner, carry):
        wide[...] = jnp.dot(normed[...], fc1_of(owner), preferred_element_type=f32)
        bias = fc1_bias_ref[owner]

        def activate(at, carry):
            rows = chunk(at)
            value = wide[rows, :] + bias
            below = 0.5 * (1.0 + lax.erf(value * 0.5**0.5))
            active[owner, rows, :] = (value * below).astype(bf16)
            density = jnp.exp(value * value * -0.5) * (0.5 / math.pi) ** 0.5
            slope[owner, rows, :] = below + value * density
            return carry

        each_chunk(activate, 0)
        product = jnp.dot(active[owner], fc2_of(owner), preferred_element_type=f32)
        total[...] = jnp.where(owner == 0, product, total[...] + product)
        return carry

    lax.fori_loop(0, shards, forward, 0)
    empty = jnp.zeros((1, width), f32)

    def turn(at, sums):
        rows = chunk(at)
        value = total[rows, :] + fc2_bias
        block_out[rows, :] = (hidden[rows, :] + scale_two * value).astype(bf16)
        grad = cotangent_ref[rows, :].astype(f32)
        grad_mlp[rows, :] = (grad * scale_two).astype(bf16)
        return (
            sums[0] + column_sum(grad * value),
            sums[1] + column_sum(grad_mlp[rows, :].astype(f32)),
        )

    scale_two_sum, fc2_bias_sum = each_chunk(turn, (empty, empty))

    def backward(owner, carry):
        wide[...] = times_transposed(grad_mlp[...], fc2_of(owner))

        def slopes(at, sums):
            rows = chunk(at)
            value = (wide[rows, :] * slope[owner, rows, :]).astype(bf16)
            grad_pre[owner, rows, :] = value
            return sums + column_sum(value.astype(f32))

        vectors_out[pl.ds(8 + owner, 1), :] = each_chunk(slopes, empty)
        product = times_transposed(grad_pre[owner], fc1_of(owner))
        total[...] = jnp.where(owner == 0, product, total[...] + product)
        return carry

    lax.fori_loop(0, shards, backward, 0)

    def leave(at, sums):
        rows = chunk(at)
        grad = total[rows, :]
        unit, inverse = unit_of(hidden[rows, :])
        scaled = grad * gain
        inner = (
            scaled
            - jnp.mean(scaled, axis=1, keepdims=True)
            - unit * jnp.mean(scaled * unit, axis=1, keepdims=True)
        )
        value = cotangent_ref[rows, :].astype(f32) + inverse * inner
        hidden_grad_out[rows, :] = value
        rounded = (value * scale_one).astype(bf16)
        grad_branch[rows, :] = rounded
        return (
            sums[0] + column_sum(grad * unit),
            sums[1] + column_sum(grad),
            sums[2] + column_sum(value * branch[rows, :]),
            sums[3] + column_sum(rounded.astype(f32)),
        )

    gain_sum, shift_sum, scale_one_sum, proj_bias_sum = each_chunk(leave, (empty,) * 4)
    for at, value in enumerate(
        (empty, empty, proj_bias_sum, scale_one_sum, gain_sum, shift_sum, fc2_bias_sum, scale_two_sum)
    ):
        vectors_out[at : at + 1, :] = value
    vectors_out[12:, :] = jnp.zeros((vectors_out.shape[0] - 12, width), f32)

    back = []
    for way in (*range(1, shards), 0):
        target = lax.rem(here + way, shards)
        grad_attended[target] = times_transposed(grad_branch[...], proj_of(target)).astype(bf16)
        if way:
            copy = copy_to(grad_attended.at[target], mixed_grad_out.at[here], next(slots), tensor=target)
            copy.start()
            back.append(copy)
    mixed_grad_out[here] = grad_attended[here]

    first_slot = next(slots)

    def core_copy(owner):
        return pltpu.make_async_remote_copy(
            src_ref=weights.at[pl.ds((1 - core) * half, half), owner],
            dst_ref=got.at[:, owner],
            send_sem=send.at[first_slot + owner],
            recv_sem=recv.at[first_slot + owner],
            device_id={"dp": partner_of(member, 0)},
            device_id_type=MESH,
        )

    def weight_grads(owner, carry):
        for left, right, first, count in (
            (normed[...], grad_pre[owner], 0, fc_rows),
            (active[owner], grad_mlp[...], fc_rows, fc_rows),
            (attended[owner], grad_branch[...], proj_first, proj_rows),
        ):
            product = contract_rows(left, right).astype(bf16)
            weights[:, owner, first : first + count, :] = product.reshape(PIECES, count, width)
        core_copy(owner).start()
        return carry

    lax.fori_loop(0, shards, weight_grads, 0)
    pairs = shards // 2
    for owner in range(shards):
        core_copy(owner).wait_recv()
        if owner < pairs:
            for y in range(2):
                for out, x in ((a_keep, x_bit), (a_away, 1 - x_bit)):
                    out[y, owner] = rounded_sum(weights[core * half + x * 2 + y, owner], got[x * 2 + y, owner])
        else:
            for x in range(2):
                for out, y in ((b_keep, y_bit), (b_away, 1 - y_bit)):
                    out[x, owner - pairs] = rounded_sum(
                        weights[core * half + x * 2 + y, owner], got[x * 2 + y, owner]
                    )
    for copy in back:
        copy.wait_recv()
    for copy in copies + back:
        copy.wait_send()
    for owner in range(shards):
        core_copy(owner).wait_send()


def middle(shards, members, mixed, weights, fc1_bias, params, tokens, cotangent):
    dp_bits = members.bit_length() - 1
    f32, bf16 = jnp.float32, jnp.bfloat16
    block, width = tokens.shape
    columns = mixed.shape[1]
    rows = weights.shape[2]
    vm = pltpu.VMEM
    on_chip = pl.BlockSpec(memory_space=vm)
    quarter = jax.ShapeDtypeStruct((2, shards // 2, rows, width), bf16)
    copies = 2 * (shards - 1) + shards
    return pl.pallas_call(
        partial(middle_kernel, shards, dp_bits),
        in_specs=[on_chip, pl.BlockSpec(memory_space=pl.ANY)] + [on_chip] * 4,
        out_specs=[on_chip] * 8,
        out_shape=[
            jax.ShapeDtypeStruct((block, width), bf16),
            jax.ShapeDtypeStruct((block, width), f32),
            jax.ShapeDtypeStruct((shards, block, columns), bf16),
            jax.ShapeDtypeStruct((16, width), f32),
            quarter,
            quarter,
            quarter,
            quarter,
        ],
        scratch_shapes=[
            vm(weights.shape, bf16),
            vm((shards, block, columns), bf16),
            vm((block, width), f32),
            vm((block, width), f32),
            vm((block, width), bf16),
            vm((block, width), f32),
            vm((block, width), f32),
            vm((shards, block, width), bf16),
            vm((shards, block, width), f32),
            vm((shards, block, width), bf16),
            vm((block, width), bf16),
            vm((block, width), bf16),
            vm((shards, block, columns), bf16),
            vm((PIECES // 2, shards, rows, width), bf16),
            pltpu.SemaphoreType.DMA((copies,)),
            pltpu.SemaphoreType.DMA((copies,)),
            pltpu.SemaphoreType.DMA((shards,)),
        ],
        compiler_params=pltpu.CompilerParams(
            collective_id=2, has_side_effects=True, vmem_limit_bytes=62 * 1024 * 1024
        ),
        name="middle",
        cost_estimate=pl.CostEstimate(
            flops=12 * block * width * width * shards, transcendentals=0, bytes_accessed=40 * block * width
        ),
    )(mixed, weights, fc1_bias, params, tokens, cotangent)


eps_norm = 1e-06


def on_device(
    shards,
    members,
    tokens,
    segment_ids,
    ln1_gain,
    ln1_bias,
    qkv_weight,
    qv_bias,
    proj_weight,
    proj_bias,
    scale_one,
    ln2_gain,
    ln2_bias,
    fc1_weight,
    fc1_bias,
    fc2_weight,
    fc2_bias,
    scale_two,
    cotangent,
):
    f32, bf16 = jnp.float32, jnp.bfloat16
    seq_len = segment_ids.shape[1]
    rows_here, width = tokens.shape
    head_columns = qkv_weight.shape[2]
    heads = head_columns // HEAD_DIM
    hidden_here = fc1_weight.shape[1]
    ids = segment_ids[0]
    here = lax.axis_index("tensor")

    full_one, queries, keys, values, gathered, fc1_bias_full = start(
        shards,
        members,
        tokens,
        segment_ids,
        ln1_gain[None],
        ln1_bias[None],
        qkv_weight,
        qv_bias,
        fc1_weight,
        fc2_weight,
        proj_weight,
        fc1_bias[None],
    )
    bounds = visit_bounds(ids, 8, seq_len // 9)
    mixed, queries_back = attend(bounds, queries, keys, values, seq_len // 9)

    params = jnp.stack([proj_bias, scale_one, ln2_gain, ln2_bias, fc2_bias, scale_two])
    block_out, grad_hidden, grad_mixed, vectors, a_keep, a_away, b_keep, b_away = middle(
        shards, members, mixed, gathered, fc1_bias_full, params, tokens, cotangent
    )
    grad_mixed = grad_mixed.reshape(seq_len, head_columns)

    def swap(value, bit):
        return lax.ppermute(value, "dp", [(j, j ^ (1 << bit)) for j in range(members)])

    a_got, b_got = swap(a_away, 1), swap(b_away, 2)
    grad_heads = attend_back(
        bounds, queries_back, keys, values, mixed, grad_mixed, seq_len // 9
    )
    grad_tokens, totals, qkv_pieces, weight_pieces = finish(
        shards,
        members,
        grad_heads,
        full_one,
        qkv_weight.transpose(1, 0, 2).reshape(width, 3 * head_columns),
        ln1_gain[None],
        ln1_bias[None],
        vectors,
        tokens,
        grad_hidden,
        a_keep,
        a_got,
        b_keep,
        b_got,
    )
    grad_qkv_weight = (
        qkv_pieces.reshape(width, 3, head_columns).transpose(1, 0, 2).astype(f32)
    )
    fc_rows, proj_count = width // PIECES, head_columns // PIECES
    grad_fc1_weight = weight_pieces[:, :fc_rows].reshape(width, hidden_here).astype(f32)
    grad_fc2_weight = (
        weight_pieces[:, fc_rows : 2 * fc_rows].reshape(hidden_here, width).astype(f32)
    )
    grad_proj_weight = (
        weight_pieces[:, 2 * fc_rows : 2 * fc_rows + proj_count]
        .reshape(head_columns, width)
        .astype(f32)
    )
    vectors = totals
    grad_fc1_bias = lax.dynamic_index_in_dim(totals, 8 + here, 0, keepdims=False)
    qv_sums = lax.dynamic_index_in_dim(totals, 12 + here, 0, keepdims=False)
    grad_qv_bias = jnp.stack([qv_sums[:head_columns], qv_sums[2 * head_columns : 3 * head_columns]])
    return (
        block_out,
        grad_tokens,
        vectors[0],
        vectors[1],
        grad_qkv_weight,
        grad_qv_bias,
        grad_proj_weight,
        vectors[2],
        vectors[3],
        vectors[4],
        vectors[5],
        grad_fc1_weight,
        grad_fc1_bias,
        grad_fc2_weight,
        vectors[6],
        vectors[7],
    )


def solution(mesh):
    rows = P(("dp", "tensor"), None)
    columns = P(None, "tensor")
    return jax.shard_map(
        partial(on_device, mesh.shape["tensor"], mesh.shape["dp"]),
        mesh=mesh,
        in_specs=(
            rows,
            P("dp", None),
            P(),
            P(),
            P(None, None, "tensor"),
            columns,
            P("tensor", None),
            P(),
            P(),
            P(),
            P(),
            columns,
            P("tensor"),
            P("tensor", None),
            P(),
            P(),
            rows,
        ),
        out_specs=(
            rows,
            rows,
            P(),
            P(),
            P(None, None, "tensor"),
            columns,
            P("tensor", None),
            P(),
            P(),
            P(),
            P(),
            columns,
            P("tensor"),
            P("tensor", None),
            P(),
            P(),
        ),
        check_vma=False,
    )
```

profile of v0, /device:TPU:16, one launch (start us, length us, event | category | flops | bytes accessed | tf_op | source)
XLA Modules:
  0.0 425.4 jit_solution(3189365082486648632)
XLA Ops:
  0.7 0.8 reduce
  1.5 0.1 slice.47
  1.6 0.1 slice.48
  1.7 1.3 broadcast_in_dim.14.shift_ref
  2.9 1.3 broadcast_in_dim.6.gain_ref
  4.2 2.3 copy.39.qkv_ref
  6.5 0.6 broadcast_in_dim.15.fc1_bias_ref
  7.2 0.2 convert_reduce_fusion.1
  7.5 0.6 pad_add_fusion.bounds_ref
  8.1 87.6 %start.1 = (bf16[2304,768]{1,0:T(8,128)(2,1)}, bf16[3,2304,128]{2,1,0:T(8,128)(2,1)}, bf16[3,2304,128]{2,1,0:T(8,128)(2,1)}, bf16[3,2304,128]{2,1,0:T(8,128)(2,1...) custom-call(bf16[576,768]{1,0:T(8,128)(2,1)} %tokens_ref.5, s32[1,2304]{1,0:T(1,128)} %ids_ref.1, ...), custom_call_target="tpu_custom_call" | custom-call | flops 2038431744 | bytes 17694720 | tf_op jit(solution)/shard_map/start/pallas_call | solution.py:908
  95.6 43.7 %attend.1 = (bf16[2304,192]{1,0:T(8,128)(2,1)}, bf16[3,2304,128]{2,1,0:T(8,128)(2,1)}) custom-call(s32[2,8]{1,0:T(2,128)} %pad_add_fusion.bounds_ref, bf16[3,2304,128]{2,1,0:T(8,128)(2,1)} %get-tuple-element.36.q_ref, bf16[3,2304,128]{2,1,0:T(8,128)(2,1)} %get-tuple-element.37.k_ref, bf16[3,2304,128]{2,1,0:T(8,128)(2,1)} %get-tuple-element.38.v_ref), custom_call_target="tpu_custom_call" | custom-call | flops 4076863488 | bytes 7077888 | tf_op jit(solution)/shard_map/attend/pallas_call | solution.py:83
  139.3 0.6 stack.38.params_ref
  140.0 94.4 %middle.1 = (bf16[576,768]{1,0:T(8,128)(2,1)}, f32[576,768]{1,0:T(8,128)}, bf16[4,576,192]{2,1,0:T(8,128)(2,1)}, f32[16,768]{1,0:T(8,128)}, bf16[2,2,224,768]{3,...) custom-call(bf16[2304,192]{1,0:T(8,128)(2,1)} %get-tuple-element.39., ...), custom_call_target="tpu_custom_call" | custom-call | flops 16307453952 | bytes 17694720 | tf_op jit(solution)/shard_map/middle/pallas_call | solution.py:1199
  234.4 0.2 collective-permute-start
  234.6 0.0 collective-permute-start.1
  234.6 1.3 copy.40.weight_ref
  235.9 54.4 %attend_back.1.grads_ref = bf16[2304,576]{1,0:T(8,128)(2,1)} custom-call(s32[2,8]{1,0:T(2,128)} %pad_add_fusion.bounds_ref, bf16[3,2304,128]{2,1,0:T(8,128)(2,1)} %get-tuple-element.43.q_ref, bf16[3,2304,128]{2,1,0:T(8,128)(2,1)} %get-tuple-element.37.k_ref, bf16[3,2304,128]{2,1,0:T(8,128)(2,1)} %get-tuple-element.38.v_ref, ...), custom_call_target="tpu_custom_call" | custom-call | flops 10192158720 | bytes 10616832 | tf_op jit(solution)/shard_map/attend_back/pallas_call | solution.py:210
  290.3 0.0 collective-permute-done.a_got
  290.3 0.0 collective-permute-done.1.b_got
  290.4 118.8 %finish.1 = (f32[576,768]{1,0:T(8,128)}, f32[16,768]{1,0:T(8,128)}, bf16[8,96,576]{2,1,0:T(8,128)(2,1)}, bf16[8,224,768]{2,1,0:T(8,128)(2,1)}) custom-call(bf16[2304,576]{1,0:T(8,128)(2,1)} %attend_back.1.grads_ref, bf16[2304,768]{1,0:T(8,128)(2,1)} %get-tuple-element.45.rows_ref, bf16[768,576]{1,0:T(8,128)(2,1)} %copy.40.weight_ref, ...), custom_call_target="tpu_custom_call" | custom-call | flops 4076863488 | bytes 17694720 | tf_op jit(solution)/shard_map/finish/pallas_call | solution.py:608
  409.2 1.8 fusion
  411.0 1.0 slice.53
  412.0 1.7 bitcast_convert_fusion
  413.6 1.7 bitcast_convert_fusion.1
  415.3 2.0 copy.41
  417.3 2.0 reshape.164
  419.3 0.9 bitcast_convert_fusion.2
  420.2 1.7 slice_reduce_fusion
  421.9 0.8 constant_dynamic-slice_fusion
  422.7 0.6 pad_maximum_fusion
  423.3 0.9 copy.44
  424.2 1.2 copy.45
  (27 shorter events, 0.1 us)
Async XLA Ops:
  0.6 5.9 %copy-start.3 = (f32[768]{0:T(1024)S(1)}, f32[768]{0:T(1024)}, u32[]{:S(2)}) copy-start(f32[768]{0:T(1024)} %param.29) | copy-start | bytes 9220
  0.7 6.5 %copy-start.4 = (f32[768]{0:T(1024)S(1)}, f32[768]{0:T(1024)}, u32[]{:S(2)}) copy-start(f32[768]{0:T(1024)} %param.24) | copy-start | bytes 9220
  0.7 6.5 %copy-start.5 = (f32[768]{0:T(1024)S(1)}, f32[768]{0:T(1024)}, u32[]{:S(2)}) copy-start(f32[768]{0:T(1024)} %param.25) | copy-start | bytes 9220
  0.7 6.5 %copy-start.6 = (f32[768]{0:T(1024)S(1)}, f32[768]{0:T(1024)}, u32[]{:S(2)}) copy-start(f32[768]{0:T(1024)} %param.26) | copy-start | bytes 9220
  0.7 6.5 %copy-start.7 = (f32[768]{0:T(1024)S(1)}, f32[768]{0:T(1024)}, u32[]{:S(2)}) copy-start(f32[768]{0:T(1024)} %param.27) | copy-start | bytes 9220
  0.7 6.5 %copy-start.8 = (f32[768]{0:T(1024)S(1)}, f32[768]{0:T(1024)}, u32[]{:S(2)}) copy-start(f32[768]{0:T(1024)} %param.31) | copy-start | bytes 9220
  0.7 6.5 %copy-start.9 = (f32[768]{0:T(1024)S(1)}, f32[768]{0:T(1024)}, u32[]{:S(2)}) copy-start(f32[768]{0:T(1024)} %param.32) | copy-start | bytes 9220
  140.0 94.6 %copy-start = (bf16[3,768,192]{1,2,0:T(8,128)(2,1)S(1)}, bf16[3,768,192]{1,2,0:T(8,128)(2,1)}, u32[]{:S(2)}) copy-start(bf16[3,768,192]{1,2,0:T(8,128)(2,1)} %param.21) | copy-start | bytes 2654212
  234.4 56.0 %collective-permute-start = (bf16[2,2,224,768]{3,2,1,0:T(8,128)(2,1)}, bf16[2,2,224,768]{3,2,1,0:T(8,128)(2,1)}, u32[]{:S(2)}, u32[]{:S(2)}) collective-permute-start(bf16[2,2,224,768]{3,2,1,0:T(8,128)(2,1)} %get-tuple-element.49), channel_id=1, source_target_pairs={{0,8},{4,12},{8,0},{12,4},{16,24},{20,28},{24,16},{28,20},{1,9},{5... | collective-permute-start | bytes 4128776 | tf_op jit(solution)/shard_map/ppermute | solution.py:1299
  234.6 55.7 %collective-permute-start.1 = (bf16[2,2,224,768]{3,2,1,0:T(8,128)(2,1)}, bf16[2,2,224,768]{3,2,1,0:T(8,128)(2,1)}, u32[]{:S(2)}, u32[]{:S(2)}) collective-permute-start(bf16[2,2,224,768]{3,2,1,0:T(8,128)(2,1)} %get-tuple-element.51), channel_id=1, source_target_pairs={{0,16},{4,20},{8,24},{12,28},{16,0},{20,4},{24,8},{28,12},{1,17},{... | collective-permute-start | bytes 4128776 | tf_op jit(solution)/shard_map/ppermute | solution.py:1299
  417.3 6.0 %copy-start.2 = (bf16[576,768]{1,0:T(8,128)(2,1)S(1)}, bf16[576,768]{1,0:T(8,128)(2,1)}, u32[]{:S(2)}) copy-start(bf16[576,768]{1,0:T(8,128)(2,1)} %get-tuple-element.89) | copy-start | bytes 2654212
  419.3 4.9 %copy-start.1 = (f32[576,768]{1,0:T(8,128)S(1)}, f32[576,768]{1,0:T(8,128)}, u32[]{:S(2)}) copy-start(f32[576,768]{1,0:T(8,128)} %get-tuple-element.90) | copy-start | bytes 5308420
where the time goes:
time: 426 us; the launch traced here: 425 us
  Pallas kernels  399 us (94%)
  local copies, waits for them, and re-layouts  19.1 us (4%)
  other arithmetic  6.35 us (1%)
    pallas_call x1, Pallas kernels, finish(): pl.pallas_call(partial(finish_kernel, shards, dp_bits), in_specs=[pl.Bloc...  119 us
    pallas_call x1, Pallas kernels, middle(): pl.pallas_call(partial(middle_kernel, shards, dp_bits), in_specs=[on_chip...  94.4 us
    pallas_call x1, Pallas kernels, start(): pl.pallas_call(partial(start_kernel, shards, dp_bits), in_specs=[on_chip]...  87.6 us
    pallas_call x1, Pallas kernels, attend_back(): pl.pallas_call(partial(attend_back_kernel, query_block), grid_spec=pltpu....  54.4 us
    pallas_call x1, Pallas kernels, attend(): pl.pallas_call(partial(attend_kernel, key_block), grid_spec=pltpu.Prefetc...  43.7 us
  transfers between devices with their start and end apart: 2, of which 0 were waited for; matrix products, arithmetic and copies ran while one was open for 0% of the time, Pallas kernels for 13%

commit v1 on v0

--- a/solution.py
+++ b/solution.py
@@ -11,6 +11,16 @@
 HEAD_DIM = 64
 LANES = 128
 MASKED = -(2.0**100)
+
+
+def contract_rows(left, right):
+    return lax.dot_general(left, right, (((0,), (0,)), ((), ())), preferred_element_type=jnp.float32)
+
+
+def times_transposed(left, right, precision=None):
+    return lax.dot_general(
+        left, right, (((1,), (1,)), ((), ())), preferred_element_type=jnp.float32, precision=precision
+    )
 
 
 def split_three(value):
@@ -31,27 +41,30 @@
     return tiles
 
 
-def attend_kernel(key_block, bounds_ref, q_ref, k_ref, v_ref, out_ref, q_back_ref, peak_ref, acc_ref):
+def attend_kernel(
+    key_block, bounds_ref, q_ref, k_ref, v_ref, out_ref, q_back_ref, peak_ref, acc_ref, score_ref, weight_ref
+):
     step = pl.program_id(0)
     heads, count, _ = q_ref.shape
+    repeats = key_block // LANES
     peak_ref[...] = jnp.full_like(peak_ref, -3e38)
     acc_ref[...] = jnp.zeros_like(acc_ref)
 
     def visit(at, carry):
         keys = pl.ds(pl.multiple_of(at * key_block, key_block), key_block)
         for head in range(heads):
-            scores = lax.dot_general(
-                q_ref[head],
-                k_ref[head, keys, :],
-                (((1,), (1,)), ((), ())),
-                preferred_element_type=jnp.float32,
+            score_ref[head] = times_transposed(q_ref[head], k_ref[head, keys, :])
+        for head in range(heads):
+            old_peak = peak_ref[head]
+            new_peak = jnp.maximum(old_peak, jnp.max(score_ref[head], axis=1, keepdims=True))
+            peak_ref[head] = new_peak
+            spread = jnp.concatenate([new_peak] * repeats, axis=1)
+            weight_ref[head] = jnp.exp(score_ref[head] - spread).astype(jnp.bfloat16)
+            acc_ref[head] = acc_ref[head] * jnp.exp(old_peak - new_peak)
+        for head in range(heads):
+            acc_ref[head] += jnp.dot(
+                weight_ref[head], v_ref[head, keys, :], preferred_element_type=jnp.float32
             )
-            old_peak = peak_ref[head]
-            new_peak = jnp.maximum(old_peak, jnp.max(scores, axis=1, keepdims=True))
-            weights = jnp.exp(scores - new_peak[:, :1]).astype(jnp.bfloat16)
-            mixed = jnp.dot(weights, v_ref[head, keys, :], preferred_element_type=jnp.float32)
-            acc_ref[head] = acc_ref[head] * jnp.exp(old_peak - new_peak) + mixed
-            peak_ref[head] = new_peak
         return carry
 
     lax.fori_loop(bounds_ref[0, step], bounds_ref[1, step], visit, 0)
@@ -90,6 +103,8 @@
             scratch_shapes=[
                 pltpu.VMEM((heads, block, LANES), jnp.float32),
                 pltpu.VMEM((heads, block, LANES), jnp.float32),
+                pltpu.VMEM((heads, block, key_block), jnp.float32),
+                pltpu.VMEM((heads, block, key_block), jnp.bfloat16),
             ],
         ),
         out_shape=[
@@ -105,8 +120,23 @@
 
 
 def attend_back_kernel(
-    query_block, bounds_ref, q_ref, k_ref, v_ref, mixed_ref, grad_ref, out_ref, grad_heads_ref, dq_ref, dk_ref, dv_ref, k0_ref
+    query_block,
+    bounds_ref,
+    q_ref,
+    k_ref,
+    v_ref,
+    mixed_ref,
+    grad_ref,
+    out_ref,
+    grad_heads_ref,
+    dq_ref,
+    dk_ref,
+    dv_ref,
+    k0_ref,
+    prob_ref,
+    grad_score_ref,
 ):
+    f32, bf16 = jnp.float32, jnp.bfloat16
     step = pl.program_id(0)
     heads, count, _ = k_ref.shape
     seq_len = q_ref.shape[1]
@@ -115,30 +145,37 @@
     @pl.when(step == 0)
     def _():
         dq_ref[...] = jnp.zeros_like(dq_ref)
+        source = lax.broadcasted_iota(jnp.int32, (LANES, LANES), 0)
+        target = lax.broadcasted_iota(jnp.int32, (LANES, LANES), 1)
+        gathers = (target >= HEAD_DIM) & (target < HEAD_DIM + 3)
+        picks = []
+        for odd in range(2):
+            own = (source >= HEAD_DIM * odd) & (source < HEAD_DIM * (odd + 1))
+            summing = jnp.where(own & gathers, -1.0, 0.0).astype(bf16)
+            moving = jnp.where(own & (source - HEAD_DIM * odd == target), 1.0, 0.0).astype(bf16)
+            picks.append((summing, moving))
+        lane = lax.broadcasted_iota(jnp.int32, (query_block, LANES), 1)
 
         def prepare(at, carry):
             rows = pl.ds(pl.multiple_of(at * query_block, query_block), query_block)
-            lane = lax.broadcasted_iota(jnp.int32, (query_block, LANES), 1)
-            for head in range(heads):
-                first = (head // 2) * LANES
+            for first in range(0, heads * HEAD_DIM, LANES):
                 wide = min(LANES, heads * HEAD_DIM - first)
-                grad = grad_ref[rows, first : first + wide].astype(jnp.float32)
-                mixed = mixed_ref[rows, first : first + wide].astype(jnp.float32)
-                if wide < LANES:
-                    blank = jnp.zeros((query_block, LANES - wide), jnp.float32)
-                    grad = jnp.concatenate([grad, blank], axis=1)
-                    mixed = jnp.concatenate([mixed, blank], axis=1)
-                if head % 2:
-                    grad = pltpu.roll(grad, HEAD_DIM, 1)
-                    mixed = pltpu.roll(mixed, HEAD_DIM, 1)
-                inside = lane < HEAD_DIM
-                shared = -jnp.sum(jnp.where(inside, grad * mixed, 0.0), axis=1, keepdims=True)
-                high, middle, low = split_three(shared)
-                grad = jnp.where(inside, grad, 0.0)
-                grad = jnp.where(lane == HEAD_DIM, high.astype(jnp.float32), grad)
-                grad = jnp.where(lane == HEAD_DIM + 1, middle.astype(jnp.float32), grad)
-                grad = jnp.where(lane == HEAD_DIM + 2, low.astype(jnp.float32), grad)
-                grad_heads_ref[head, rows, :] = grad.astype(jnp.bfloat16)
+                grad = grad_ref[rows, first : first + wide]
+                mixed = mixed_ref[rows, first : first + wide]
+                product = grad.astype(f32) * mixed.astype(f32)
+                high = product.astype(bf16)
+                low = (product - high.astype(f32)).astype(bf16)
+                for odd in range(-(-wide // HEAD_DIM)):
+                    summing, moving = (pick[:wide] for pick in picks[odd])
+                    shared = jnp.dot(high, summing, preferred_element_type=f32) + jnp.dot(
+                        low, summing, preferred_element_type=f32
+                    )
+                    first_part, second_part, third_part = split_three(shared)
+                    moved = jnp.dot(grad, moving, preferred_element_type=f32)
+                    moved = jnp.where(lane == HEAD_DIM, first_part.astype(f32), moved)
+                    moved = jnp.where(lane == HEAD_DIM + 1, second_part.astype(f32), moved)
+                    moved = jnp.where(lane == HEAD_DIM + 2, third_part.astype(f32), moved)
+                    grad_heads_ref[first // HEAD_DIM + odd, rows, :] = moved.astype(bf16)
             return carry
 
         lax.fori_loop(0, blocks, prepare, 0)
@@ -149,55 +186,51 @@
     def visit(at, carry):
         rows = pl.ds(pl.multiple_of(at * query_block, query_block), query_block)
         for head in range(heads):
-            queries = q_ref[head, rows, :]
-            grads = grad_heads_ref[head, rows, :]
-            keys = k_ref[head]
-            contract = (((1,), (1,)), ((), ()))
-            scores = lax.dot_general(keys, queries, contract, preferred_element_type=jnp.float32)
-            probs = jnp.exp(scores)
-            grad_probs = lax.dot_general(
-                v_ref[head], grads, contract, preferred_element_type=jnp.float32
+            probs = jnp.exp(times_transposed(k_ref[head], q_ref[head, rows, :]))
+            grad_probs = times_transposed(v_ref[head], grad_heads_ref[head, rows, :])
+            prob_ref[head] = probs.astype(bf16)
+            grad_score_ref[head] = (probs * grad_probs).astype(bf16)
+        for head in range(heads):
+            dv_ref[head] += jnp.dot(
+                prob_ref[head], grad_heads_ref[head, rows, :], preferred_element_type=f32
             )
-            grad_scores = (probs * grad_probs).astype(jnp.bfloat16)
-            dv_ref[head] += jnp.dot(
-                probs.astype(jnp.bfloat16), grads, preferred_element_type=jnp.float32
+            dk_ref[head] += jnp.dot(
+                grad_score_ref[head], q_ref[head, rows, :], preferred_element_type=f32
             )
-            dk_ref[head] += jnp.dot(grad_scores, queries, preferred_element_type=jnp.float32)
-            dq_ref[head, rows, :] += lax.dot_general(
-                grad_scores, keys, (((0,), (0,)), ((), ())), preferred_element_type=jnp.float32
-            )
+            dq_ref[head, rows, :] += contract_rows(grad_score_ref[head], k_ref[head])
         return carry
 
     lax.fori_loop(bounds_ref[0, step], bounds_ref[1, step], visit, 0)
     lane = lax.broadcasted_iota(jnp.int32, (count, LANES), 1)
     low_half = lane < HEAD_DIM
     here = pl.ds(pl.multiple_of(step * count, count), count)
-    k0_ref[here, :] = dk_ref[0]
+    k0_ref[here, :] = dk_ref[0].astype(bf16)
     out_ref[here, 256:384] = jnp.where(
         low_half, dk_ref[1], pltpu.roll(dk_ref[2], HEAD_DIM, 1)
-    ).astype(jnp.bfloat16)
+    ).astype(bf16)
     out_ref[here, 384:512] = jnp.where(
         low_half, dv_ref[0], pltpu.roll(dv_ref[1], HEAD_DIM, 1)
-    ).astype(jnp.bfloat16)
-    out_ref[here, 512:576] = dv_ref[2][:, :HEAD_DIM].astype(jnp.bfloat16)
+    ).astype(bf16)
+    out_ref[here, 512:576] = dv_ref[2][:, :HEAD_DIM].astype(bf16)
 
     @pl.when(step == pl.num_programs(0) - 1)
     def _():
-        def finish(at, carry):
+        scale = HEAD_DIM**-0.5
+
+        def close(at, carry):
             rows = pl.ds(pl.multiple_of(at * query_block, query_block), query_block)
-            lane = lax.broadcasted_iota(jnp.int32, (query_block, LANES), 1)
-            low_half = lane < HEAD_DIM
-            scale = HEAD_DIM**-0.5
+            low_half = lax.broadcasted_iota(jnp.int32, (query_block, LANES), 1) < HEAD_DIM
+            second = pltpu.roll(dq_ref[1, rows, :], HEAD_DIM, 1)
             out_ref[rows, 0:128] = (
-                jnp.where(low_half, dq_ref[0, rows, :], pltpu.roll(dq_ref[1, rows, :], HEAD_DIM, 1))
-                * scale
-            ).astype(jnp.bfloat16)
+                jnp.where(low_half, dq_ref[0, rows, :], second) * scale
+            ).astype(bf16)
+            first_keys = pltpu.roll(k0_ref[rows, :].astype(f32), HEAD_DIM, 1)
             out_ref[rows, 128:256] = jnp.where(
-                low_half, dq_ref[2, rows, :] * scale, pltpu.roll(k0_ref[rows, :], HEAD_DIM, 1)
-            ).astype(jnp.bfloat16)
+                low_half, dq_ref[2, rows, :] * scale, first_keys
+            ).astype(bf16)
             return carry
 
-        lax.fori_loop(0, blocks, finish, 0)
+        lax.fori_loop(0, blocks, close, 0)
 
 
 def attend_back(bounds, queries, keys, values, mixed, grads, query_block):
@@ -219,7 +252,9 @@
                 pltpu.VMEM((heads, seq_len, LANES), jnp.float32),
                 pltpu.VMEM((heads, block, LANES), jnp.float32),
                 pltpu.VMEM((heads, block, LANES), jnp.float32),
-                pltpu.VMEM((seq_len, LANES), jnp.float32),
+                pltpu.VMEM((seq_len, LANES), jnp.bfloat16),
+                pltpu.VMEM((heads, block, query_block), jnp.bfloat16),
+                pltpu.VMEM((heads, block, query_block), jnp.bfloat16),
             ],
         ),
         out_shape=jax.ShapeDtypeStruct((seq_len, 3 * heads * HEAD_DIM), jnp.bfloat16),
@@ -231,29 +266,9 @@
     )(bounds, queries, keys, values, mixed, grads)
 
 
-def visit_bounds(ids, steps, block):
-    seq_len = ids.shape[0]
-    count = seq_len // steps
-    first = ids[::count][:steps]
-    last = ids[count - 1 :: count]
-    start = jnp.sum(ids[None, :] < first[:, None], axis=1, dtype=jnp.int32)
-    end = jnp.sum(ids[None, :] <= last[:, None], axis=1, dtype=jnp.int32)
-    return jnp.stack([start // block, (end + block - 1) // block])
-
-
 MESH = pl.DeviceIdType.MESH
 PIECES = 8
 PIECE_BITS = 3
-
-
-def contract_rows(left, right):
-    return lax.dot_general(left, right, (((0,), (0,)), ((), ())), preferred_element_type=jnp.float32)
-
-
-def times_transposed(left, right, precision=None):
-    return lax.dot_general(
-        left, right, (((1,), (1,)), ((), ())), preferred_element_type=jnp.float32, precision=precision
-    )
 
 
 def rounded_sum(left, right):
@@ -272,7 +287,7 @@
     barrier = pltpu.get_barrier_semaphore()
     member, here = lax.axis_index("dp"), lax.axis_index("tensor")
     peers = [{"dp": partner_of(member, bit)} for bit in range(dp_bits)]
-    peers += [{"tensor": lax.rem(here + shift, shards)} for shift in range(1, shards)]
+    peers += [{"tensor": lax.rem(here + way, shards)} for way in range(1, shards)]
     for peer in peers:
         pl.semaphore_signal(barrier, inc=1, device_id=peer, device_id_type=MESH)
     pl.semaphore_wait(barrier, len(peers))
@@ -330,6 +345,7 @@
     columns = grads_ref.shape[1]
     half_rows = weights_out.shape[1] // 2
     last = shards - 1
+    gain, shift = (ref[...].reshape(1, width) for ref in (gain_ref, shift_ref))
     slots = iter(range(send.shape[0]))
     pending = []
 
@@ -392,7 +408,9 @@
             if owner not in order:
                 order.append(owner)
     for owner in order:
-        product = times_transposed(grads_ref[owner * block : (owner + 1) * block, :], weight_ref[...])
+        product = jnp.dot(
+            grads_ref[owner * block : (owner + 1) * block, :], weight_ref[...], preferred_element_type=f32
+        )
         part[owner] = product.astype(bf16)
         if owner > 0:
 
@@ -430,17 +448,18 @@
 
     def grow(at, carry):
         rows = pl.ds(pl.multiple_of(at * block, 16), block)
-        q_wide[...] += contract_rows(rows_ref[rows, :], grads_ref[rows, :])
+        q_wide[...] += contract_rows(grads_ref[rows, :], rows_ref[rows, :])
         return carry
 
     lax.fori_loop(0, shards, grow, 0)
     sums = jnp.dot(jnp.ones((8, grads_ref.shape[0]), bf16), grads_ref[...], preferred_element_type=f32)
-    exact = lax.Precision.HIGHEST
     weight = weight_ref[...].astype(f32)
-    shift_sum = times_transposed(sums, weight, exact)[0:1]
-    gain_sum = times_transposed(jnp.ones((8, columns), f32), weight * q_wide[...], exact)[0:1]
+    shift_sum = jnp.dot(
+        sums, weight, preferred_element_type=f32, precision=lax.Precision.HIGHEST
+    )[0:1]
+    gain_sum = jnp.sum(weight * q_wide[...], axis=0, keepdims=True)
     v_now[0] = vectors_ref[...]
-    v_now[0, 0:1, :] = (gain_sum - shift_ref[...] * shift_sum) / gain_ref[...]
+    v_now[0, 0:1, :] = (gain_sum - shift * shift_sum) / gain
     v_now[0, 1:2, :] = shift_sum
     v_now[0, pl.ds(12 + here, 1), 0:columns] = sums[0:1]
     count = q_all.shape[1]
@@ -465,9 +484,9 @@
         extra.wait_send()
         add_into(pieces, pieces, pieces_more.at[bit - PIECE_BITS])
     z_copies = []
-    for shift in range(1, shards):
-        target = lax.rem(here + shift, shards)
-        copy = copy_to(pieces.at[target], z_got.at[shift - 1], next(slots), tensor=target)
+    for way in range(1, shards):
+        target = lax.rem(here + way, shards)
+        copy = copy_to(pieces.at[target], z_got.at[way - 1], next(slots), tensor=target)
         copy.start()
         z_copies.append(copy)
     pending.extend(z_copies)
@@ -501,9 +520,9 @@
         v_copy.wait_recv()
         v_now[bit + 1] = v_now[bit] + v_got[bit]
     v_shards[here] = v_now[dp_bits]
-    for shift in range(1, shards):
+    for way in range(1, shards):
         copy = copy_to(
-            v_now.at[dp_bits], v_shards.at[here], next(slots), tensor=lax.rem(here + shift, shards)
+            v_now.at[dp_bits], v_shards.at[here], next(slots), tensor=lax.rem(here + way, shards)
         )
         copy.start()
         pending.append(copy)
@@ -521,8 +540,8 @@
     for copy in z_copies:
         copy.wait_recv()
     total = pieces[here].astype(f32)
-    for shift in range(1, shards):
-        total = total + z_got[shift - 1].astype(f32)
+    for way in range(1, shards):
+        total = total + z_got[way - 1].astype(f32)
     weights_out[own_piece] = total.astype(bf16)
 
     def own_half(low, *index):
@@ -569,7 +588,7 @@
         centred = tokens - jnp.mean(tokens, axis=1, keepdims=True)
         inverse = lax.rsqrt(jnp.mean(centred * centred, axis=1, keepdims=True) + eps_norm)
         unit = centred * inverse
-        scaled = part[here, rows, :].astype(f32) * gain_ref[...]
+        scaled = part[here, rows, :].astype(f32) * gain
         inner = (
             scaled
             - jnp.mean(scaled, axis=1, keepdims=True)
@@ -601,7 +620,7 @@
     seq_len, columns = grads.shape
     block, width = tokens.shape
     piece_rows = a_keep.shape[2]
-    count = width // PIECES
+    count = columns // PIECES
     more = max(1, dp_bits - PIECE_BITS)
     copies = 16 + 2 * shards + 2 * (shards - 1) + 3 * dp_bits
     vm = pltpu.VMEM
@@ -612,21 +631,21 @@
         out_shape=[
             jax.ShapeDtypeStruct((block, width), f32),
             jax.ShapeDtypeStruct(vectors.shape, f32),
-            jax.ShapeDtypeStruct((PIECES, count, columns), bf16),
+            jax.ShapeDtypeStruct((PIECES, count, width), bf16),
             jax.ShapeDtypeStruct((PIECES, piece_rows, width), bf16),
         ],
         scratch_shapes=[
             vm((shards, block, width), bf16),
             vm((shards, block, width), bf16),
             vm((shards, block, width), bf16),
-            vm((width, columns), f32),
-            vm((PIECES, count, columns), bf16),
-            vm((4, count, columns), bf16),
-            vm((2, count, columns), bf16),
-            vm((4, count, columns), bf16),
-            vm((2, count, columns), bf16),
-            vm((count, columns), bf16),
-            vm((more, count, columns), bf16),
+            vm((columns, width), f32),
+            vm((PIECES, count, width), bf16),
+            vm((4, count, width), bf16),
+            vm((2, count, width), bf16),
+            vm((4, count, width), bf16),
+            vm((2, count, width), bf16),
+            vm((count, width), bf16),
+            vm((more, count, width), bf16),
             vm((dp_bits + 1,) + vectors.shape, f32),
             vm((dp_bits,) + vectors.shape, f32),
             vm((shards,) + vectors.shape, f32),
@@ -650,9 +669,47 @@
     )(grads, rows, weight, gain, shift, vectors, tokens, grad_hidden, a_keep, a_got, b_keep, b_got)
 
 
+def unpack_kernel(qkv_ref, weights_ref, totals_ref, fc1_out, fc2_out, proj_out, qkv_out, fc1_bias_out, *vector_outs):
+    fc_rows, proj_rows = fc1_out.shape[0], proj_out.shape[0]
+    fc1_out[...] = weights_ref[0, :fc_rows].astype(jnp.float32)
+    fc2_out[...] = weights_ref[0, fc_rows : 2 * fc_rows].astype(jnp.float32)
+    proj_out[...] = weights_ref[0, 2 * fc_rows : 2 * fc_rows + proj_rows].astype(jnp.float32)
+    qkv_out[...] = qkv_ref[0].astype(jnp.float32)
+
+    @pl.when(pl.program_id(0) == 0)
+    def _():
+        width = totals_ref.shape[1]
+        for at, out in enumerate(vector_outs):
+            out[...] = totals_ref[at : at + 1, :].reshape(width)
+        here = lax.axis_index("tensor")
+        fc1_bias_out[...] = totals_ref[pl.ds(8 + here, 1), :].reshape(width)
+
+
+def unpack(qkv, weights, totals, fc_rows, proj_rows):
+    f32 = jnp.float32
+    _, rows, width = weights.shape
+    qkv_rows = qkv.shape[1]
+    counts = (fc_rows, fc_rows, proj_rows, qkv_rows)
+    vector = pl.BlockSpec((width,), lambda i: (0,))
+    return pl.pallas_call(
+        unpack_kernel,
+        grid=(PIECES,),
+        in_specs=[
+            pl.BlockSpec((1, qkv_rows, width), lambda i: (i, 0, 0)),
+            pl.BlockSpec((1, rows, width), lambda i: (i, 0, 0)),
+            pl.BlockSpec(totals.shape, lambda i: (0, 0)),
+        ],
+        out_specs=[pl.BlockSpec((count, width), lambda i: (i, 0)) for count in counts] + [vector] * 9,
+        out_shape=[jax.ShapeDtypeStruct((PIECES * count, width), f32) for count in counts]
+        + [jax.ShapeDtypeStruct((width,), f32)] * 9,
+        name="unpack",
+    )(qkv, weights, totals)
+
+
 def start_kernel(
     shards,
     dp_bits,
+    visit_block,
     tokens_ref,
     ids_ref,
     gain_ref,
@@ -669,6 +726,7 @@
     v_out,
     weights_out,
     bias_out,
+    bounds_out,
     blocks,
     q_extra,
     k_extra,
@@ -713,6 +771,8 @@
     own[used : used + proj_rows, :] = proj_ref[rows, :]
     used += proj_rows
     own[used:, :] = jnp.zeros((own.shape[0] - used, width), bf16)
+    gain, shift = (ref[...].reshape(1, width) for ref in (gain_ref, shift_ref))
+    bias_out[here] = fc1_bias_ref[...].reshape(1, width)
     greet(dp_bits, shards)
     for load in loads:
         load.wait()
@@ -766,10 +826,9 @@
         hop_copy("t", last, False, True).start()
 
     bias_copies = []
-    bias_out[here] = fc1_bias_ref[...]
-    for shift in range(1, shards):
+    for way in range(1, shards):
         copy = copy_to(
-            fc1_bias_ref, bias_out.at[here], next(slots), tensor=lax.rem(here + shift, shards)
+            bias_out.at[here], bias_out.at[here], next(slots), tensor=lax.rem(here + way, shards)
         )
         copy.start()
         bias_copies.append(copy)
@@ -787,6 +846,15 @@
     ones_lane = (lane >= HEAD_DIM + 8) & (lane < HEAD_DIM + 11)
     q_extra[...] = jnp.where(segment_lane, (matched - 1.0) * large, 0.0).astype(bf16)
     k_extra[...] = jnp.where(ones_lane, 1.0, matched).astype(bf16)
+    ids = ids_ref[...]
+    groups = bounds_out.shape[1]
+    for group in range(groups):
+        first = group * (seq_len // groups)
+        last_row = first + seq_len // groups - 1
+        before = jnp.sum(jnp.where(ids < ids_ref[:, first : first + 1], 1.0, 0.0))
+        within = jnp.sum(jnp.where(ids <= ids_ref[:, last_row : last_row + 1], 1.0, 0.0))
+        bounds_out[0, group] = before.astype(jnp.int32) // visit_block
+        bounds_out[1, group] = (within.astype(jnp.int32) + visit_block - 1) // visit_block
     low_half = lax.broadcasted_iota(jnp.int32, (block, LANES), 1) < HEAD_DIM
     v_lane = lax.broadcasted_iota(jnp.int32, (block, LANES), 1)
     v_extra = jnp.where((v_lane >= HEAD_DIM) & (v_lane < HEAD_DIM + 3), 1.0, 0.0).astype(bf16)
@@ -795,11 +863,11 @@
         tokens = source.astype(f32)
         centred = tokens - jnp.mean(tokens, axis=1, keepdims=True)
         inverse = lax.rsqrt(jnp.mean(centred * centred, axis=1, keepdims=True) + eps_norm)
-        normed = (centred * inverse * gain_ref[...] + shift_ref[...]).astype(bf16)
+        normed = (centred * inverse * gain + shift).astype(bf16)
         rows = pl.ds(pl.multiple_of(owner * block, 16), block)
         normed_out[rows, :] = normed
         for which, out in ((0, q_out), (1, k_out), (2, v_out)):
-            product = jnp.dot(normed, qkv_ref[which], preferred_element_type=f32)
+            product = times_transposed(normed, qkv_ref[which])
             if which != 1:
                 product = product + qv_bias_ref[which // 2 : which // 2 + 1, :]
             if which == 0:
@@ -892,13 +960,13 @@
                         hop_copy(name, owner, False, False).wait_send()
 
 
-def start(shards, members, tokens, ids, gain, shift, qkv, qv_bias, fc1, fc2, proj, fc1_bias):
+def start(shards, members, visits, tokens, ids, gain, shift, qkv, qv_bias, fc1, fc2, proj, fc1_bias):
     dp_bits = members.bit_length() - 1
     assert members == 1 << dp_bits and dp_bits >= PIECE_BITS and shards >= 3
     f32, bf16 = jnp.float32, jnp.bfloat16
     block, width = tokens.shape
     seq_len = block * shards
-    heads = qkv.shape[2] // HEAD_DIM
+    heads = qkv.shape[1] // HEAD_DIM
     rows = -(-(fc1.shape[0] + fc2.shape[0] + proj.shape[0]) // PIECES // 16) * 16
     copies = 4 * shards + (shards - 1) + 6
     vm = pltpu.VMEM
@@ -906,16 +974,17 @@
     anywhere = pl.BlockSpec(memory_space=pl.ANY)
     head_rows = jax.ShapeDtypeStruct((heads, seq_len, LANES), bf16)
     return pl.pallas_call(
-        partial(start_kernel, shards, dp_bits),
+        partial(start_kernel, shards, dp_bits, visits[1]),
         in_specs=[on_chip] * 6 + [anywhere] * 2 + [on_chip] * 2,
-        out_specs=[on_chip] * 4 + [anywhere, on_chip],
+        out_specs=[on_chip] * 4 + [anywhere, on_chip, pl.BlockSpec(memory_space=pltpu.SMEM)],
         out_shape=[
             jax.ShapeDtypeStruct((seq_len, width), bf16),
             head_rows,
             head_rows,
             head_rows,
             jax.ShapeDtypeStruct((PIECES, shards, rows, width), bf16),
-            jax.ShapeDtypeStruct((shards,) + fc1_bias.shape, f32),
+            jax.ShapeDtypeStruct((shards, 1, width), f32),
+            jax.ShapeDtypeStruct((2, visits[0]), jnp.int32),
         ],
         scratch_shapes=[
             vm((shards, block, width), bf16),
@@ -944,7 +1013,12 @@
     mixed_ref,
     weights_ref,
     fc1_bias_ref,
-    params_ref,
+    proj_bias_ref,
+    scale_one_ref,
+    gain_ref,
+    shift_ref,
+    fc2_bias_ref,
+    scale_two_ref,
     tokens_ref,
     cotangent_ref,
     block_out,
@@ -983,7 +1057,8 @@
     proj_first = 2 * fc_rows
     slots = iter(range(send.shape[0]))
     proj_bias, scale_one, gain, shift, fc2_bias, scale_two = (
-        params_ref[at : at + 1, :] for at in range(6)
+        ref[...].reshape(1, width)
+        for ref in (proj_bias_ref, scale_one_ref, gain_ref, shift_ref, fc2_bias_ref, scale_two_ref)
     )
 
     def copy_to(src, dst, at, **peer):
@@ -1186,7 +1261,7 @@
         core_copy(owner).wait_send()
 
 
-def middle(shards, members, mixed, weights, fc1_bias, params, tokens, cotangent):
+def middle(shards, members, mixed, weights, fc1_bias, vectors, tokens, cotangent):
     dp_bits = members.bit_length() - 1
     f32, bf16 = jnp.float32, jnp.bfloat16
     block, width = tokens.shape
@@ -1198,7 +1273,7 @@
     copies = 2 * (shards - 1) + shards
     return pl.pallas_call(
         partial(middle_kernel, shards, dp_bits),
-        in_specs=[on_chip, pl.BlockSpec(memory_space=pl.ANY)] + [on_chip] * 4,
+        in_specs=[on_chip, pl.BlockSpec(memory_space=pl.ANY)] + [on_chip] * 9,
         out_specs=[on_chip] * 8,
         out_shape=[
             jax.ShapeDtypeStruct((block, width), bf16),
@@ -1236,7 +1311,7 @@
         cost_estimate=pl.CostEstimate(
             flops=12 * block * width * width * shards, transcendentals=0, bytes_accessed=40 * block * width
         ),
-    )(mixed, weights, fc1_bias, params, tokens, cotangent)
+    )(mixed, weights, fc1_bias, *vectors, tokens, cotangent)
 
 
 eps_norm = 1e-06
@@ -1272,24 +1347,26 @@
     ids = segment_ids[0]
     here = lax.axis_index("tensor")
 
-    full_one, queries, keys, values, gathered, fc1_bias_full = start(
+    visits = (4, seq_len // 6)
+    turned = qkv_weight.transpose(0, 2, 1)
+    full_one, queries, keys, values, gathered, fc1_bias_full, bounds = start(
         shards,
         members,
+        visits,
         tokens,
         segment_ids,
-        ln1_gain[None],
-        ln1_bias[None],
-        qkv_weight,
+        ln1_gain,
+        ln1_bias,
+        turned,
         qv_bias,
         fc1_weight,
         fc2_weight,
         proj_weight,
-        fc1_bias[None],
+        fc1_bias,
     )
-    bounds = visit_bounds(ids, 8, seq_len // 9)
-    mixed, queries_back = attend(bounds, queries, keys, values, seq_len // 9)
-
-    params = jnp.stack([proj_bias, scale_one, ln2_gain, ln2_bias, fc2_bias, scale_two])
+    mixed, queries_back = attend(bounds, queries, keys, values, visits[1])
+
+    params = (proj_bias, scale_one, ln2_gain, ln2_bias, fc2_bias, scale_two)
     block_out, grad_hidden, grad_mixed, vectors, a_keep, a_away, b_keep, b_away = middle(
         shards, members, mixed, gathered, fc1_bias_full, params, tokens, cotangent
     )
@@ -1299,17 +1376,15 @@
         return lax.ppermute(value, "dp", [(j, j ^ (1 << bit)) for j in range(members)])
 
     a_got, b_got = swap(a_away, 1), swap(b_away, 2)
-    grad_heads = attend_back(
-        bounds, queries_back, keys, values, mixed, grad_mixed, seq_len // 9
-    )
+    grad_heads = attend_back(bounds, queries_back, keys, values, mixed, grad_mixed, visits[1])
     grad_tokens, totals, qkv_pieces, weight_pieces = finish(
         shards,
         members,
         grad_heads,
         full_one,
-        qkv_weight.transpose(1, 0, 2).reshape(width, 3 * head_columns),
-        ln1_gain[None],
-        ln1_bias[None],
+        turned.reshape(3 * head_columns, width),
+        ln1_gain,
+        ln1_bias,
         vectors,
         tokens,
         grad_hidden,
@@ -1318,40 +1393,29 @@
         b_keep,
         b_got,
     )
-    grad_qkv_weight = (
-        qkv_pieces.reshape(width, 3, head_columns).transpose(1, 0, 2).astype(f32)
+    fc1_grad, fc2_grad, proj_grad, qkv_grad, fc1_bias_grad, *sums = unpack(
+        qkv_pieces, weight_pieces, totals, width // PIECES, head_columns // PIECES
     )
-    fc_rows, proj_count = width // PIECES, head_columns // PIECES
-    grad_fc1_weight = weight_pieces[:, :fc_rows].reshape(width, hidden_here).astype(f32)
-    grad_fc2_weight = (
-        weight_pieces[:, fc_rows : 2 * fc_rows].reshape(hidden_here, width).astype(f32)
-    )
-    grad_proj_weight = (
-        weight_pieces[:, 2 * fc_rows : 2 * fc_rows + proj_count]
-        .reshape(head_columns, width)
-        .astype(f32)
-    )
-    vectors = totals
-    grad_fc1_bias = lax.dynamic_index_in_dim(totals, 8 + here, 0, keepdims=False)
+    qkv_grad = qkv_grad.reshape(3, head_columns, width).transpose(0, 2, 1)
     qv_sums = lax.dynamic_index_in_dim(totals, 12 + here, 0, keepdims=False)
-    grad_qv_bias = jnp.stack([qv_sums[:head_columns], qv_sums[2 * head_columns : 3 * head_columns]])
+    qv_grad = jnp.stack([qv_sums[:head_columns], qv_sums[2 * head_columns : 3 * head_columns]])
     return (
         block_out,
         grad_tokens,
-        vectors[0],
-        vectors[1],
-        grad_qkv_weight,
-        grad_qv_bias,
-        grad_proj_weight,
-        vectors[2],
-        vectors[3],
-        vectors[4],
-        vectors[5],
-        grad_fc1_weight,
-        grad_fc1_bias,
-        grad_fc2_weight,
-        vectors[6],
-        vectors[7],
+        sums[0],
+        sums[1],
+        qkv_grad,
+        qv_grad,
+        proj_grad,
+        sums[2],
+        sums[3],
+        sums[4],
+        sums[5],
+        fc1_grad,
+        fc1_bias_grad,
+        fc2_grad,
+        sums[6],
+        sums[7],
     )
 
 

time: 426 us -> 376 us (0.88)
  Pallas kernels: 399 us -> 367 us
  local copies, waits for them, and re-layouts: 19.1 us -> 4.85 us
  other arithmetic: 6.35 us -> 0.59 us
    pallas_call x1, Pallas kernels: 43.7 us -> 22.8 us  [attend(): pl.pallas_call(partial(attend_kernel, key_block), grid_spec=pltpu.Prefetc...]
    pallas_call x1, Pallas kernels: 54.4 us -> 38.6 us  [attend_back(): pl.pallas_call(partial(attend_back_kernel, query_block), grid_spec=pltpu....]
    pallas_call x1 -> x2, Pallas kernels: 87.6 us -> 94.7 us  [the longest x1 87.6 us: start(): pl.pallas_call(partial(start_kernel, shards, dp_bits, visits[1]), in_spec...]
    slice x5 -> x0, local copies, waits for them, and re-layouts: 4.68 us -> none  [the longest x1 1.79 us: on_device(): weight_pieces[:, fc_rows:2 * fc_rows].reshape(hidden_here, width)]
  transfers between devices with their start and end apart: 2 -> 2, of which waited for: 0 -> 0; matrix products, arithmetic and copies ran while one was open for 0% -> 0% of each run, Pallas kernels for 13% -> 10%
where the time goes in v1:
time: 376 us; the launch traced here: 375 us
  Pallas kernels  367 us (98%)
  local copies, waits for them, and re-layouts  4.85 us (1%)
    pallas_call x1, Pallas kernels, finish(): pl.pallas_call(partial(finish_kernel, shards, dp_bits), in_specs=[pl.Bloc...  120 us
    pallas_call x1, Pallas kernels, middle(): pl.pallas_call(partial(middle_kernel, shards, dp_bits), in_specs=[on_chip...  91.1 us
    pallas_call x1, Pallas kernels, start(): pl.pallas_call(partial(start_kernel, shards, dp_bits, visits[1]), in_spec...  87.6 us
    pallas_call x1, Pallas kernels, attend_back(): pl.pallas_call(partial(attend_back_kernel, query_block), grid_spec=pltpu....  38.6 us
    pallas_call x1, Pallas kernels, attend(): pl.pallas_call(partial(attend_kernel, key_block), grid_spec=pltpu.Prefetc...  22.8 us
  transfers between devices with their start and end apart: 2, of which 0 were waited for; matrix products, arithmetic and copies ran while one was open for 0% of the time, Pallas kernels for 10%

profile of v1, /device:TPU:16, one launch (start us, length us, event | category | flops | bytes accessed | tf_op | source)
XLA Modules:
  0.0 375.1 jit_solution(13334394268967661006)
XLA Ops:
  0.6 87.6 %start.1 = (bf16[2304,768]{1,0:T(8,128)(2,1)}, bf16[3,2304,128]{2,1,0:T(8,128)(2,1)}, bf16[3,2304,128]{2,1,0:T(8,128)(2,1)}, bf16[3,2304,128]{2,1,0:T(8,128)(2,1...) custom-call(bf16[576,768]{1,0:T(8,128)(2,1)} %tokens_ref.5, s32[1,2304]{1,0:T(1,128)} %ids_ref.1, ...), custom_call_target="tpu_custom_call" | custom-call | flops 2038431744 | bytes 17694720 | tf_op jit(solution)/shard_map/start/pallas_call | solution.py:976
  88.2 22.8 %attend.1 = (bf16[2304,192]{1,0:T(8,128)(2,1)}, bf16[3,2304,128]{2,1,0:T(8,128)(2,1)}) custom-call(s32[2,4]{1,0:T(2,128)} %get-tuple-element.50.bounds_ref, bf16[3,2304,128]{2,1,0:T(8,128)(2,1)} %get-tuple-element.51.q_ref, bf16[3,2304,128]{2,1,0:T(8,128)(2,1)} %get-tuple-element.52.k_ref, bf16[3,2304,128]{2,1,0:T(8,128)(2,1)} %get-tuple-element.53.v_ref), custom_call_target="tpu_custom_call" | custom-call | flops 4076863488 | bytes 7077888 | tf_op jit(solution)/shard_map/attend/pallas_call | solution.py:96
  111.0 91.1 %middle.1 = (bf16[576,768]{1,0:T(8,128)(2,1)}, f32[576,768]{1,0:T(8,128)}, bf16[4,576,192]{2,1,0:T(8,128)(2,1)}, f32[16,768]{1,0:T(8,128)}, bf16[2,2,224,768]{3,...) custom-call(bf16[2304,192]{1,0:T(8,128)(2,1)} %get-tuple-element.54., ...), custom_call_target="tpu_custom_call" | custom-call | flops 16307453952 | bytes 17694720 | tf_op jit(solution)/shard_map/middle/pallas_call | solution.py:1274
  202.1 2.1 collective-permute-start
  204.2 0.1 collective-permute-start.1
  204.2 38.6 %attend_back.1.grads_ref = bf16[2304,576]{1,0:T(8,128)(2,1)} custom-call(s32[2,4]{1,0:T(2,128)} %get-tuple-element.50.bounds_ref, bf16[3,2304,128]{2,1,0:T(8,128)(2,1)} %get-tuple-element.58.q_ref, bf16[3,2304,128]{2,1,0:T(8,128)(2,1)} %get-tuple-element.52.k_ref, bf16[3,2304,128]{2,1,0:T(8,128)(2,1)} %get-tuple-element.53.v_ref, ...), custom_call_target="tpu_custom_call" | custom-call | flops 10192158720 | bytes 10616832 | tf_op jit(solution)/shard_map/attend_back/pallas_call | solution.py:243
  242.9 0.0 collective-permute-done.a_got
  242.9 0.0 copy-start.1
  242.9 0.0 collective-permute-done.1.b_got
  242.9 1.1 copy-done.1
  244.0 119.5 %finish.1 = (f32[576,768]{1,0:T(8,128)}, f32[16,768]{1,0:T(8,128)}, bf16[8,72,768]{2,1,0:T(8,128)(2,1)}, bf16[8,224,768]{2,1,0:T(8,128)(2,1)}) custom-call(bf16[2304,576]{1,0:T(8,128)(2,1)} %attend_back.1.grads_ref, bf16[2304,768]{1,0:T(8,128)(2,1)} %get-tuple-element.60.rows_ref, bf16[576,768]{1,0:T(8,128)(2,1)} %bitcast.8, f32[768]{0:T(1024)} %gain_ref.5, ...), custom_call_target="tpu_custom_call" | custom-call | flops 4076863488 | bytes 17694720 | tf_op jit(solution)/shard_map/finish/pallas_call | solution.py:627
  363.5 0.8 constant_dynamic-slice_fusion
  364.3 0.6 pad_maximum_fusion
  364.9 0.0 copy-start.2
  364.9 7.2 %unpack.1 = (f32[768,768]{1,0:T(8,128)}, f32[768,768]{1,0:T(8,128)}, f32[192,768]{1,0:T(8,128)}, f32[576,768]{1,0:T(8,128)}, f32[768]{0:T(1024)}, /*index=5*/f32...) custom-call(bf16[8,72,768]{2,1,0:T(8,128)(2,1)} %get-tuple-element.6, ...), custom_call_target="tpu_custom_call" | custom-call | tf_op jit(solution)/shard_map/unpack/pallas_call | solution.py:694
  372.0 0.0 copy-start
  372.1 0.0 copy-done.2
  372.1 0.9 copy.35
  373.0 0.9 copy-done
  373.8 1.2 copy.36
Async XLA Ops:
  202.1 40.8 %collective-permute-start = (bf16[2,2,224,768]{3,2,1,0:T(8,128)(2,1)}, bf16[2,2,224,768]{3,2,1,0:T(8,128)(2,1)S(1)}, u32[]{:S(2)}, u32[]{:S(2)}) collective-permute-start(bf16[2,2,224,768]{3,2,1,0:T(8,128)(2,1)} %get-tuple-element.64), channel_id=1, source_target_pairs={{0,8},{4,12},{8,0},{12,4},{16,24},{20,28},{24,16},{28,20},{1,9},{5... | collective-permute-start | bytes 4128776 | tf_op jit(solution)/shard_map/ppermute | solution.py:1376
  204.2 38.7 %collective-permute-start.1 = (bf16[2,2,224,768]{3,2,1,0:T(8,128)(2,1)}, bf16[2,2,224,768]{3,2,1,0:T(8,128)(2,1)}, u32[]{:S(2)}, u32[]{:S(2)}) collective-permute-start(bf16[2,2,224,768]{3,2,1,0:T(8,128)(2,1)} %get-tuple-element.66), channel_id=1, source_target_pairs={{0,16},{4,20},{8,24},{12,28},{16,0},{20,4},{24,8},{28,12},{1,17},{... | collective-permute-start | bytes 4128776 | tf_op jit(solution)/shard_map/ppermute | solution.py:1376
  242.9 1.1 copy-start.1
  364.9 7.2 %copy-start.2 = (bf16[576,768]{1,0:T(8,128)(2,1)S(1)}, bf16[576,768]{1,0:T(8,128)(2,1)}, u32[]{:S(2)}) copy-start(bf16[576,768]{1,0:T(8,128)(2,1)} %get-tuple-element.102) | copy-start | bytes 2654212
  372.0 1.8 copy-start

commit v2 on v1

--- a/solution.py
+++ b/solution.py
@@ -31,18 +31,24 @@
     return (high, middle, low)
 
 
-def join_heads(parts, low_half):
-    tiles = []
-    for at in range(0, len(parts), 2):
-        if at + 1 < len(parts):
-            tiles.append(jnp.where(low_half, parts[at], pltpu.roll(parts[at + 1], HEAD_DIM, 1)))
-        else:
-            tiles.append(parts[at])
-    return tiles
+def join_lanes(low, high):
+    lane = lax.broadcasted_iota(jnp.int32, low.shape, 1)
+    return jnp.where(lane < HEAD_DIM, low, pltpu.roll(high, HEAD_DIM, 1))
 
 
 def attend_kernel(
-    key_block, bounds_ref, q_ref, k_ref, v_ref, out_ref, q_back_ref, peak_ref, acc_ref, score_ref, weight_ref
+    key_block,
+    bounds_ref,
+    q_ref,
+    k_ref,
+    v_ref,
+    pair_ref,
+    single_ref,
+    q_back_ref,
+    peak_ref,
+    acc_ref,
+    score_ref,
+    weight_ref,
 ):
     step = pl.program_id(0)
     heads, count, _ = q_ref.shape
@@ -69,7 +75,6 @@
 
     lax.fori_loop(bounds_ref[0, step], bounds_ref[1, step], visit, 0)
     lane = lax.broadcasted_iota(jnp.int32, (count, LANES), 1)
-    low_half = lane < HEAD_DIM
     parts = []
     for head in range(heads):
         acc = acc_ref[head]
@@ -82,9 +87,9 @@
         kept = jnp.where(lane == HEAD_DIM + 9, middle.astype(jnp.float32), kept)
         kept = jnp.where(lane == HEAD_DIM + 10, low.astype(jnp.float32), kept)
         q_back_ref[head] = kept.astype(jnp.bfloat16)
-    for at, tile in enumerate(join_heads(parts, low_half)):
-        wide = min(LANES, heads * HEAD_DIM - at * LANES)
-        out_ref[:, at * LANES : at * LANES + wide] = tile[:, :wide].astype(jnp.bfloat16)
+    pair_ref[...] = join_lanes(parts[0], parts[1]).astype(jnp.bfloat16)
+    half = count // 2
+    single_ref[...] = join_lanes(parts[2][:half], parts[2][half:]).astype(jnp.bfloat16)
 
 
 def attend(bounds, queries, keys, values, key_block):
@@ -99,7 +104,11 @@
             num_scalar_prefetch=1,
             grid=(steps,),
             in_specs=[q_spec, full, full],
-            out_specs=[pl.BlockSpec((block, heads * HEAD_DIM), lambda i, b: (i, 0)), q_spec],
+            out_specs=[
+                pl.BlockSpec((block, LANES), lambda i, b: (i, 0)),
+                pl.BlockSpec((block // 2, LANES), lambda i, b: (i, 0)),
+                q_spec,
+            ],
             scratch_shapes=[
                 pltpu.VMEM((heads, block, LANES), jnp.float32),
                 pltpu.VMEM((heads, block, LANES), jnp.float32),
@@ -108,7 +117,8 @@
             ],
         ),
         out_shape=[
-            jax.ShapeDtypeStruct((seq_len, heads * HEAD_DIM), jnp.bfloat16),
+            jax.ShapeDtypeStruct((seq_len, LANES), jnp.bfloat16),
+            jax.ShapeDtypeStruct((seq_len // 2, LANES), jnp.bfloat16),
             jax.ShapeDtypeStruct((heads, seq_len, LANES), jnp.bfloat16),
         ],
         name="attend",
@@ -125,8 +135,10 @@
     q_ref,
     k_ref,
     v_ref,
-    mixed_ref,
-    grad_ref,
+    pair_ref,
+    single_ref,
+    pair_grad_ref,
+    single_grad_ref,
     out_ref,
     grad_heads_ref,
     dq_ref,
@@ -154,19 +166,22 @@
             summing = jnp.where(own & gathers, -1.0, 0.0).astype(bf16)
             moving = jnp.where(own & (source - HEAD_DIM * odd == target), 1.0, 0.0).astype(bf16)
             picks.append((summing, moving))
-        lane = lax.broadcasted_iota(jnp.int32, (query_block, LANES), 1)
+        half = count // 2
+        lane = lax.broadcasted_iota(jnp.int32, (half, LANES), 1)
 
         def prepare(at, carry):
-            rows = pl.ds(pl.multiple_of(at * query_block, query_block), query_block)
-            for first in range(0, heads * HEAD_DIM, LANES):
-                wide = min(LANES, heads * HEAD_DIM - first)
-                grad = grad_ref[rows, first : first + wide]
-                mixed = mixed_ref[rows, first : first + wide]
-                product = grad.astype(f32) * mixed.astype(f32)
-                high = product.astype(bf16)
-                low = (product - high.astype(f32)).astype(bf16)
-                for odd in range(-(-wide // HEAD_DIM)):
-                    summing, moving = (pick[:wide] for pick in picks[odd])
+            for part in range(2):
+                rows = pl.ds(pl.multiple_of((2 * at + part) * half, half), half)
+                single_rows = pl.ds(pl.multiple_of(at * half, half), half)
+                for head, odd, mixed, grad in (
+                    (0, 0, pair_ref[rows, :], pair_grad_ref[rows, :]),
+                    (1, 1, pair_ref[rows, :], pair_grad_ref[rows, :]),
+                    (2, part, single_ref[single_rows, :], single_grad_ref[single_rows, :]),
+                ):
+                    summing, moving = picks[odd]
+                    product = grad.astype(f32) * mixed.astype(f32)
+                    high = product.astype(bf16)
+                    low = (product - high.astype(f32)).astype(bf16)
                     shared = jnp.dot(high, summing, preferred_element_type=f32) + jnp.dot(
                         low, summing, preferred_element_type=f32
                     )
@@ -175,10 +190,10 @@
                     moved = jnp.where(lane == HEAD_DIM, first_part.astype(f32), moved)
                     moved = jnp.where(lane == HEAD_DIM + 1, second_part.astype(f32), moved)
                     moved = jnp.where(lane == HEAD_DIM + 2, third_part.astype(f32), moved)
-                    grad_heads_ref[first // HEAD_DIM + odd, rows, :] = moved.astype(bf16)
+                    grad_heads_ref[head, rows, :] = moved.astype(bf16)
             return carry
 
-        lax.fori_loop(0, blocks, prepare, 0)
+        lax.fori_loop(0, seq_len // count, prepare, 0)
 
     dk_ref[...] = jnp.zeros_like(dk_ref)
     dv_ref[...] = jnp.zeros_like(dv_ref)
@@ -233,19 +248,20 @@
         lax.fori_loop(0, blocks, close, 0)
 
 
-def attend_back(bounds, queries, keys, values, mixed, grads, query_block):
+def attend_back(bounds, queries, keys, values, pairs, singles, pair_grads, single_grads, query_block):
     heads, seq_len, _ = queries.shape
     steps = bounds.shape[1]
     block = seq_len // steps
     k_spec = pl.BlockSpec((heads, block, LANES), lambda i, b: (0, i, 0))
     full = pl.BlockSpec((heads, seq_len, LANES), lambda i, b: (0, 0, 0))
-    flat = pl.BlockSpec((seq_len, heads * HEAD_DIM), lambda i, b: (0, 0))
+    pair = pl.BlockSpec(pairs.shape, lambda i, b: (0, 0))
+    single = pl.BlockSpec(singles.shape, lambda i, b: (0, 0))
     return pl.pallas_call(
         partial(attend_back_kernel, query_block),
         grid_spec=pltpu.PrefetchScalarGridSpec(
             num_scalar_prefetch=1,
             grid=(steps,),
-            in_specs=[full, k_spec, k_spec, flat, flat],
+            in_specs=[full, k_spec, k_spec, pair, single, pair, single],
             out_specs=pl.BlockSpec((seq_len, 3 * heads * HEAD_DIM), lambda i, b: (0, 0)),
             scratch_shapes=[
                 pltpu.VMEM((heads, seq_len, LANES), jnp.bfloat16),
@@ -263,7 +279,7 @@
             flops=10 * heads * seq_len * seq_len * LANES // 2, transcendentals=heads * seq_len * seq_len // 2,
             bytes_accessed=12 * heads * seq_len * LANES,
         ),
-    )(bounds, queries, keys, values, mixed, grads)
+    )(bounds, queries, keys, values, pairs, singles, pair_grads, single_grads)
 
 
 MESH = pl.DeviceIdType.MESH
@@ -312,6 +328,9 @@
     vectors_out,
     qkv_out,
     weights_out,
+    rows_own,
+    tokens_own,
+    hidden_own,
     part,
     from_left,
     from_right,
@@ -335,8 +354,15 @@
     z_got,
     send,
     recv,
+    local,
 ):
     f32, bf16 = jnp.float32, jnp.bfloat16
+    loads = []
+    for at, (source, landing) in enumerate(
+        ((rows_ref, rows_own), (tokens_ref, tokens_own), (hidden_ref, hidden_own))
+    ):
+        loads.append(pltpu.make_async_copy(source, landing, local.at[at]))
+        loads[-1].start()
     member, here = lax.axis_index("dp"), lax.axis_index("tensor")
     core, x_bit, y_bit = bit_of(member, 0), bit_of(member, 1), bit_of(member, 2)
     own_piece = core * 4 + x_bit * 2 + y_bit
@@ -412,43 +438,49 @@
             grads_ref[owner * block : (owner + 1) * block, :], weight_ref[...], preferred_element_type=f32
         )
         part[owner] = product.astype(bf16)
-        if owner > 0:
+        if owner == last:
 
             @pl.when(here == 0)
             def _():
                 to_right(owner).start()
 
-        if owner < last:
+        if owner == 0:
 
             @pl.when(here == last)
             def _():
                 to_left(owner).start()
 
-    def hop(time):
-        for owner in range(shards):
-            at = time - (last - owner)
-            if 0 < at < owner:
+    def end_sends():
+        for owner in range(last - 1, 0, -1):
+
+            @pl.when(here == 0)
+            def _():
+                to_right(owner).start()
+
+        for owner in range(1, last):
+
+            @pl.when(here == last)
+            def _():
+                to_left(owner).start()
+
+    def hop(moved, nth):
+        for owner, at, rightward in ((last - nth, moved, True), (nth, last - moved, False)):
+            if (at < owner) if rightward else (at > owner):
 
                 @pl.when(here == at)
                 def _():
-                    to_right(owner).wait_recv()
-                    add_arrived(owner, from_left)
-                    to_right(owner).start()
-
-            at = last + owner - time
-            if owner < at < last:
-
-                @pl.when(here == at)
-                def _():
-                    to_left(owner).wait_recv()
-                    add_arrived(owner, from_right)
-                    to_left(owner).start()
-
+                    copy = to_right(owner) if rightward else to_left(owner)
+                    copy.wait_recv()
+                    add_arrived(owner, from_left if rightward else from_right)
+                    copy.start()
+
+    for load in loads:
+        load.wait()
     q_wide[...] = jnp.zeros_like(q_wide)
 
     def grow(at, carry):
         rows = pl.ds(pl.multiple_of(at * block, 16), block)
-        q_wide[...] += contract_rows(grads_ref[rows, :], rows_ref[rows, :])
+        q_wide[...] += contract_rows(grads_ref[rows, :], rows_own[rows, :])
         return carry
 
     lax.fori_loop(0, shards, grow, 0)
@@ -490,6 +522,7 @@
         copy.start()
         z_copies.append(copy)
     pending.extend(z_copies)
+    end_sends()
 
     q_core.wait_recv()
     for at in range(4):
@@ -498,8 +531,7 @@
     v_copy.wait_recv()
     v_now[1] = v_now[0] + v_got[0]
     v_copy = vector_stage(1)
-    if last > 1:
-        hop(1)
+    hop(1, 0)
     q_x.wait_recv()
     for at in range(2):
         q_quarter[at] = rounded_sum(q_half[x_bit * 2 + at], q_got_x[at])
@@ -532,8 +564,6 @@
     q_back = start_dp(
         qkv_out.at[pl.ds(core * 4 + x_bit * 2, 2)], qkv_out.at[pl.ds(core * 4 + x_bit * 2, 2)], 1
     )
-    for time in range(2, last):
-        hop(time)
     q_back.wait_recv()
     q_back = start_dp(qkv_out.at[pl.ds(core * 4, 4)], qkv_out.at[pl.ds(core * 4, 4)], 0)
 
@@ -558,6 +588,11 @@
         start_dp(own_half(False, core * 4 + 2 * at + y_bit), own_half(False, core * 4 + 2 * at + y_bit), 2)
         for at in range(2)
     ]
+    for moved in range(2, last):
+        hop(moved, 0)
+    for nth in range(1, last):
+        for moved in range(1, last):
+            hop(moved, nth)
     back_a.wait_recv()
     for copy in back_c:
         copy.wait_recv()
@@ -584,7 +619,7 @@
 
     def close(at, carry):
         rows = pl.ds(pl.multiple_of(at * (block // 4), 16), block // 4)
-        tokens = tokens_ref[rows, :].astype(f32)
+        tokens = tokens_own[rows, :].astype(f32)
         centred = tokens - jnp.mean(tokens, axis=1, keepdims=True)
         inverse = lax.rsqrt(jnp.mean(centred * centred, axis=1, keepdims=True) + eps_norm)
         unit = centred * inverse
@@ -594,7 +629,7 @@
             - jnp.mean(scaled, axis=1, keepdims=True)
             - unit * jnp.mean(scaled * unit, axis=1, keepdims=True)
         )
-        tokens_out[rows, :] = hidden_ref[rows, :] + inverse * inner
+        tokens_out[rows, :] = hidden_own[rows, :] + inverse * inner
         return carry
 
     lax.fori_loop(0, 4, close, 0)
@@ -626,7 +661,9 @@
     vm = pltpu.VMEM
     return pl.pallas_call(
         partial(finish_kernel, shards, dp_bits),
-        in_specs=[pl.BlockSpec(memory_space=vm)] * 12,
+        in_specs=[
+            pl.BlockSpec(memory_space=pl.ANY if at in (1, 6, 7) else vm) for at in range(12)
+        ],
         out_specs=[pl.BlockSpec(memory_space=vm)] * 4,
         out_shape=[
             jax.ShapeDtypeStruct((block, width), f32),
@@ -635,6 +672,9 @@
             jax.ShapeDtypeStruct((PIECES, piece_rows, width), bf16),
         ],
         scratch_shapes=[
+            vm((seq_len, width), bf16),
+            vm((block, width), bf16),
+            vm((block, width), f32),
             vm((shards, block, width), bf16),
             vm((shards, block, width), bf16),
             vm((shards, block, width), bf16),
@@ -658,6 +698,7 @@
             vm((shards - 1, piece_rows, width), bf16),
             pltpu.SemaphoreType.DMA((copies,)),
             pltpu.SemaphoreType.DMA((copies,)),
+            pltpu.SemaphoreType.DMA((3,)),
         ],
         compiler_params=pltpu.CompilerParams(
             collective_id=1, has_side_effects=True, vmem_limit_bytes=64 * 1024 * 1024 - 2048 * 1024
@@ -1010,7 +1051,8 @@
 def middle_kernel(
     shards,
     dp_bits,
-    mixed_ref,
+    pairs_ref,
+    singles_ref,
     weights_ref,
     fc1_bias_ref,
     proj_bias_ref,
@@ -1023,14 +1065,18 @@
     cotangent_ref,
     block_out,
     hidden_grad_out,
-    mixed_grad_out,
+    pair_grads_out,
+    single_grads_out,
     vectors_out,
     a_keep,
     a_away,
     b_keep,
     b_away,
     weights,
+    pairs,
+    singles,
     attended,
+    proj,
     branch,
     hidden,
     normed,
@@ -1041,7 +1087,8 @@
     grad_pre,
     grad_mlp,
     grad_branch,
-    grad_attended,
+    pair_grads,
+    single_grads,
     got,
     send,
     recv,
@@ -1051,7 +1098,7 @@
     member, here = lax.axis_index("dp"), lax.axis_index("tensor")
     core, x_bit, y_bit = bit_of(member, 0), bit_of(member, 1), bit_of(member, 2)
     block, width = tokens_ref.shape
-    columns = mixed_ref.shape[1]
+    columns = width // shards
     half = PIECES // 2
     fc_rows, proj_rows = width // PIECES, columns // PIECES
     proj_first = 2 * fc_rows
@@ -1073,16 +1120,18 @@
         loads.append(load)
     greet(dp_bits, shards)
 
-    def rows_of(owner):
-        return pl.ds(pl.multiple_of(owner * block, 16), block)
+    def rows_of(owner, count):
+        return pl.ds(pl.multiple_of(owner * count, 16), count)
 
     copies = []
-    for way in range(1, shards):
-        target = lax.rem(here + way, shards)
-        copy = copy_to(mixed_ref.at[rows_of(target)], attended.at[here], next(slots), tensor=target)
-        copy.start()
-        copies.append(copy)
-    attended[here] = mixed_ref[rows_of(here), :]
+    for source, landing in ((pairs_ref, pairs), (singles_ref, singles)):
+        count = landing.shape[1]
+        for way in range(1, shards):
+            target = lax.rem(here + way, shards)
+            copy = copy_to(source.at[rows_of(target, count)], landing.at[here], next(slots), tensor=target)
+            copy.start()
+            copies.append(copy)
+        landing[here] = source[rows_of(here, count), :]
     for load in loads:
         load.wait()
 
@@ -1109,11 +1158,28 @@
         inverse = lax.rsqrt(jnp.mean(centred * centred, axis=1, keepdims=True) + eps_norm)
         return centred * inverse, inverse
 
+    third = shards * LANES
+    for owner in range(shards):
+        own_proj = proj_of(owner)
+        proj[owner * LANES : (owner + 1) * LANES, :] = own_proj[:LANES]
+        proj[third + owner * HEAD_DIM : third + (owner + 1) * HEAD_DIM, :] = own_proj[LANES:]
     for copy in copies:
         copy.wait_recv()
-    product = jnp.dot(attended[0], proj_of(0), preferred_element_type=f32)
-    for owner in range(1, shards):
-        product += jnp.dot(attended[owner], proj_of(owner), preferred_element_type=f32)
+    middle_row = block // 2
+    for owner in range(shards):
+        attended[:, owner * LANES : (owner + 1) * LANES] = pairs[owner]
+    lane = lax.broadcasted_iota(jnp.int32, (middle_row, LANES), 1)
+    low_half = lane < HEAD_DIM
+
+    def swapped(value):
+        return pltpu.roll(value, HEAD_DIM, 1)
+
+    for at in range(shards // 2):
+        one, two = singles[2 * at].astype(f32), singles[2 * at + 1].astype(f32)
+        columns_here = slice(third + at * LANES, third + (at + 1) * LANES)
+        attended[:middle_row, columns_here] = jnp.where(low_half, one, swapped(two)).astype(bf16)
+        attended[middle_row:, columns_here] = jnp.where(low_half, swapped(one), two).astype(bf16)
+    product = jnp.dot(attended[...], proj[...], preferred_element_type=f32)
     branch[...] = product
 
     def enter(at, carry):
@@ -1129,7 +1195,7 @@
     each_chunk(enter, 0)
 
     def forward(owner, carry):
-        wide[...] = jnp.dot(normed[...], fc1_of(owner), preferred_element_type=f32)
+        wide[:block, :] = jnp.dot(normed[...], fc1_of(owner), preferred_element_type=f32)
         bias = fc1_bias_ref[owner]
 
         def activate(at, carry):
@@ -1163,7 +1229,7 @@
     scale_two_sum, fc2_bias_sum = each_chunk(turn, (empty, empty))
 
     def backward(owner, carry):
-        wide[...] = times_transposed(grad_mlp[...], fc2_of(owner))
+        wide[:block, :] = times_transposed(grad_mlp[...], fc2_of(owner))
 
         def slopes(at, sums):
             rows = chunk(at)
@@ -1206,15 +1272,22 @@
         vectors_out[at : at + 1, :] = value
     vectors_out[12:, :] = jnp.zeros((vectors_out.shape[0] - 12, width), f32)
 
+    wide[:block, :] = times_transposed(grad_branch[...], proj[...])
+    for owner in range(shards):
+        pair_grads[owner] = wide[:block, owner * LANES : (owner + 1) * LANES].astype(bf16)
+    for at in range(shards // 2):
+        columns_here = slice(third + at * LANES, third + (at + 1) * LANES)
+        upper, lower = wide[:middle_row, columns_here], wide[middle_row:block, columns_here]
+        single_grads[2 * at] = jnp.where(low_half, upper, swapped(lower)).astype(bf16)
+        single_grads[2 * at + 1] = jnp.where(low_half, swapped(upper), lower).astype(bf16)
     back = []
-    for way in (*range(1, shards), 0):
-        target = lax.rem(here + way, shards)
-        grad_attended[target] = times_transposed(grad_branch[...], proj_of(target)).astype(bf16)
-        if way:
-            copy = copy_to(grad_attended.at[target], mixed_grad_out.at[here], next(slots), tensor=target)
+    for source, out in ((pair_grads, pair_grads_out), (single_grads, single_grads_out)):
+        for way in range(1, shards):
+            target = lax.rem(here + way, shards)
+            copy = copy_to(source.at[target], out.at[here], next(slots), tensor=target)
             copy.start()
             back.append(copy)
-    mixed_grad_out[here] = grad_attended[here]
+        out[here] = source[here]
 
     first_slot = next(slots)
 
@@ -1228,11 +1301,21 @@
             device_id_type=MESH,
         )
 
+    wide[...] = contract_rows(attended[:, :], grad_branch[...])
+    for owner in range(shards):
+        for piece in range(PIECES):
+            first, end = piece * proj_rows, (piece + 1) * proj_rows
+            for low, high, start_row in ((0, LANES, owner * LANES), (LANES, columns, third + owner * HEAD_DIM)):
+                begin, stop = max(first, low), min(end, high)
+                if begin < stop:
+                    rows = slice(start_row + begin - low, start_row + stop - low)
+                    to = slice(proj_first + begin - first, proj_first + stop - first)
+                    weights[piece, owner, to, :] = wide[rows, :].astype(bf16)
+
     def weight_grads(owner, carry):
         for left, right, first, count in (
             (normed[...], grad_pre[owner], 0, fc_rows),
             (active[owner], grad_mlp[...], fc_rows, fc_rows),
-            (attended[owner], grad_branch[...], proj_first, proj_rows),
         ):
             product = contract_rows(left, right).astype(bf16)
             weights[:, owner, first : first + count, :] = product.reshape(PIECES, count, width)
@@ -1240,17 +1323,17 @@
         return carry
 
     lax.fori_loop(0, shards, weight_grads, 0)
-    pairs = shards // 2
+    split = shards // 2
     for owner in range(shards):
         core_copy(owner).wait_recv()
-        if owner < pairs:
+        if owner < split:
             for y in range(2):
                 for out, x in ((a_keep, x_bit), (a_away, 1 - x_bit)):
                     out[y, owner] = rounded_sum(weights[core * half + x * 2 + y, owner], got[x * 2 + y, owner])
         else:
             for x in range(2):
                 for out, y in ((b_keep, y_bit), (b_away, 1 - y_bit)):
-                    out[x, owner - pairs] = rounded_sum(
+                    out[x, owner - split] = rounded_sum(
                         weights[core * half + x * 2 + y, owner], got[x * 2 + y, owner]
                     )
     for copy in back:
@@ -1261,24 +1344,24 @@
         core_copy(owner).wait_send()
 
 
-def middle(shards, members, mixed, weights, fc1_bias, vectors, tokens, cotangent):
+def middle(shards, members, pairs, singles, weights, fc1_bias, vectors, tokens, cotangent):
     dp_bits = members.bit_length() - 1
     f32, bf16 = jnp.float32, jnp.bfloat16
     block, width = tokens.shape
-    columns = mixed.shape[1]
     rows = weights.shape[2]
     vm = pltpu.VMEM
     on_chip = pl.BlockSpec(memory_space=vm)
     quarter = jax.ShapeDtypeStruct((2, shards // 2, rows, width), bf16)
-    copies = 2 * (shards - 1) + shards
+    copies = 4 * (shards - 1) + shards
     return pl.pallas_call(
         partial(middle_kernel, shards, dp_bits),
-        in_specs=[on_chip, pl.BlockSpec(memory_space=pl.ANY)] + [on_chip] * 9,
-        out_specs=[on_chip] * 8,
+        in_specs=[on_chip, on_chip, pl.BlockSpec(memory_space=pl.ANY)] + [on_chip] * 9,
+        out_specs=[on_chip] * 9,
         out_shape=[
             jax.ShapeDtypeStruct((block, width), bf16),
             jax.ShapeDtypeStruct((block, width), f32),
-            jax.ShapeDtypeStruct((shards, block, columns), bf16),
+            jax.ShapeDtypeStruct((shards, block, LANES), bf16),
+            jax.ShapeDtypeStruct((shards, block // 2, LANES), bf16),
             jax.ShapeDtypeStruct((16, width), f32),
             quarter,
             quarter,
@@ -1287,18 +1370,22 @@
         ],
         scratch_shapes=[
             vm(weights.shape, bf16),
-            vm((shards, block, columns), bf16),
+            vm((shards, block, LANES), bf16),
+            vm((shards, block // 2, LANES), bf16),
+            vm((block, width), bf16),
+            vm((width, width), bf16),
             vm((block, width), f32),
             vm((block, width), f32),
             vm((block, width), bf16),
-            vm((block, width), f32),
+            vm((width, width), f32),
             vm((block, width), f32),
             vm((shards, block, width), bf16),
             vm((shards, block, width), f32),
             vm((shards, block, width), bf16),
             vm((block, width), bf16),
             vm((block, width), bf16),
-            vm((shards, block, columns), bf16),
+            vm((shards, block, LANES), bf16),
+            vm((shards, block // 2, LANES), bf16),
             vm((PIECES // 2, shards, rows, width), bf16),
             pltpu.SemaphoreType.DMA((copies,)),
             pltpu.SemaphoreType.DMA((copies,)),
@@ -1311,7 +1398,7 @@
         cost_estimate=pl.CostEstimate(
             flops=12 * block * width * width * shards, transcendentals=0, bytes_accessed=40 * block * width
         ),
-    )(mixed, weights, fc1_bias, *vectors, tokens, cotangent)
+    )(pairs, singles, weights, fc1_bias, *vectors, tokens, cotangent)
 
 
 eps_norm = 1e-06
@@ -1347,7 +1434,7 @@
     ids = segment_ids[0]
     here = lax.axis_index("tensor")
 
-    visits = (4, seq_len // 6)
+    visits = (shards, seq_len // 6)
     turned = qkv_weight.transpose(0, 2, 1)
     full_one, queries, keys, values, gathered, fc1_bias_full, bounds = start(
         shards,
@@ -1364,19 +1451,20 @@
         proj_weight,
         fc1_bias,
     )
-    mixed, queries_back = attend(bounds, queries, keys, values, visits[1])
+    pairs, singles, queries_back = attend(bounds, queries, keys, values, visits[1])
 
     params = (proj_bias, scale_one, ln2_gain, ln2_bias, fc2_bias, scale_two)
-    block_out, grad_hidden, grad_mixed, vectors, a_keep, a_away, b_keep, b_away = middle(
-        shards, members, mixed, gathered, fc1_bias_full, params, tokens, cotangent
+    block_out, grad_hidden, pair_grads, single_grads, vectors, a_keep, a_away, b_keep, b_away = middle(
+        shards, members, pairs, singles, gathered, fc1_bias_full, params, tokens, cotangent
     )
-    grad_mixed = grad_mixed.reshape(seq_len, head_columns)
+    pair_grads = pair_grads.reshape(seq_len, LANES)
+    single_grads = single_grads.reshape(seq_len // 2, LANES)
 
     def swap(value, bit):
         return lax.ppermute(value, "dp", [(j, j ^ (1 << bit)) for j in range(members)])
 
     a_got, b_got = swap(a_away, 1), swap(b_away, 2)
-    grad_heads = attend_back(bounds, queries_back, keys, values, mixed, grad_mixed, visits[1])
+    grad_heads = attend_back(bounds, queries_back, keys, values, pairs, singles, pair_grads, single_grads, visits[1])
     grad_tokens, totals, qkv_pieces, weight_pieces = finish(
         shards,
         members,

time: 376 us -> 350 us (0.931)
  Pallas kernels: 367 us -> 334 us
  starting transfers between devices: 2.15 us -> 8.99 us
    pallas_call x1, Pallas kernels: 120 us -> 99.6 us  [finish(): pl.pallas_call(partial(finish_kernel, shards, dp_bits), in_specs=[pl.Bloc...]
    pallas_call x1, Pallas kernels: 91.1 us -> 78.3 us  [middle(): pl.pallas_call(partial(middle_kernel, shards, dp_bits), in_specs=[on_chip...]
    ppermute x2, starting transfers between devices: 2.15 us -> 8.99 us  [swap(): lax.ppermute(value, 'dp', [(j, j ^ 1 << bit) for j in range(members)])]
  transfers between devices with their start and end apart: 2 -> 2, of which waited for: 0 -> 0; matrix products, arithmetic and copies ran while one was open for 0% -> 0% of each run, Pallas kernels for 10% -> 11%
where the time goes in v2:
time: 350 us; the launch traced here: 349 us
  Pallas kernels  334 us (95%)
  starting transfers between devices  8.99 us (3%)
  local copies, waits for them, and re-layouts  4.85 us (1%)
    pallas_call x1, Pallas kernels, finish(): pl.pallas_call(partial(finish_kernel, shards, dp_bits), in_specs=[pl.Bloc...  99.6 us
    pallas_call x1, Pallas kernels, start(): pl.pallas_call(partial(start_kernel, shards, dp_bits, visits[1]), in_spec...  87.6 us
    pallas_call x1, Pallas kernels, middle(): pl.pallas_call(partial(middle_kernel, shards, dp_bits), in_specs=[on_chip...  78.3 us
    pallas_call x1, Pallas kernels, attend_back(): pl.pallas_call(partial(attend_back_kernel, query_block), grid_spec=pltpu....  38.1 us
    pallas_call x1, Pallas kernels, attend(): pl.pallas_call(partial(attend_kernel, key_block), grid_spec=pltpu.Prefetc...  22.8 us
    ppermute x2, starting transfers between devices, swap(): lax.ppermute(value, 'dp', [(j, j ^ 1 << bit) for j in range(members)])  8.99 us
    pallas_call x1, Pallas kernels, unpack(): pl.pallas_call(unpack_kernel, grid=(PIECES,), in_specs=[pl.BlockSpec((1,...  7.16 us
  transfers between devices with their start and end apart: 2, of which 0 were waited for; matrix products, arithmetic and copies ran while one was open for 0% of the time, Pallas kernels for 11%

profile of v2, /device:TPU:16, one launch (start us, length us, event | category | flops | bytes accessed | tf_op | source)
XLA Modules:
  0.0 348.7 jit_solution(13436076632389247543)
XLA Ops:
  0.6 87.6 %start.1 = (bf16[2304,768]{1,0:T(8,128)(2,1)}, bf16[3,2304,128]{2,1,0:T(8,128)(2,1)}, bf16[3,2304,128]{2,1,0:T(8,128)(2,1)}, bf16[3,2304,128]{2,1,0:T(8,128)(2,1...) custom-call(bf16[576,768]{1,0:T(8,128)(2,1)} %tokens_ref.5, s32[1,2304]{1,0:T(1,128)} %ids_ref.1, ...), custom_call_target="tpu_custom_call" | custom-call | flops 2038431744 | bytes 17694720 | tf_op jit(solution)/shard_map/start/pallas_call | solution.py:1017
  88.2 22.8 %attend.1 = (bf16[2304,128]{1,0:T(8,128)(2,1)}, bf16[1152,128]{1,0:T(8,128)(2,1)}, bf16[3,2304,128]{2,1,0:T(8,128)(2,1)}) custom-call(s32[2,4]{1,0:T(2,128)} %get-tuple-element.52.bounds_ref, bf16[3,2304,128]{2,1,0:T(8,128)(2,1)} %get-tuple-element.53.q_ref, bf16[3,2304,128]{2,1,0:T(8,128)(2,1)} %get-tuple-element.54.k_ref, ...), custom_call_target="tpu_custom_call" | custom-call | flops 4076863488 | bytes 7077888 | tf_op jit(solution)/shard_map/attend/pallas_call | solution.py:101
  111.1 78.3 %middle.1 = (bf16[576,768]{1,0:T(8,128)(2,1)}, f32[576,768]{1,0:T(8,128)}, bf16[4,576,128]{2,1,0:T(8,128)(2,1)}, bf16[4,288,128]{2,1,0:T(8,128)(2,1)}, f32[16,76...) custom-call(bf16[2304,128]{1,0:T(8,128)(2,1)} %get-tuple-element.56., ...), custom_call_target="tpu_custom_call" | custom-call | flops 16307453952 | bytes 17694720 | tf_op jit(solution)/shard_map/middle/pallas_call | solution.py:1356
  189.4 7.8 %collective-permute-start = (bf16[2,2,224,768]{3,2,1,0:T(8,128)(2,1)}, bf16[2,2,224,768]{3,2,1,0:T(8,128)(2,1)S(1)}, u32[]{:S(2)}, u32[]{:S(2)}) collective-permute-start(bf16[2,2,224,768]{3,2,1,0:T(8,128)(2,1)} %get-tuple-element.68), channel_id=1, source_target_pairs={{0,8},{4,12},{8,0},{12,4},{16,24},{20,28},{24,16},{28,20},{1,9},{5... | collective-permute-start | bytes 4128776 | tf_op jit(solution)/shard_map/ppermute | solution.py:1464
  197.2 1.1 collective-permute-start.1
  198.4 38.1 %attend_back.1.grads_ref = bf16[2304,576]{1,0:T(8,128)(2,1)} custom-call(s32[2,4]{1,0:T(2,128)} %get-tuple-element.52.bounds_ref, bf16[3,2304,128]{2,1,0:T(8,128)(2,1)} %get-tuple-element.61.q_ref, bf16[3,2304,128]{2,1,0:T(8,128)(2,1)} %get-tuple-element.54.k_ref, bf16[3,2304,128]{2,1,0:T(8,128)(2,1)} %get-tuple-element.55.v_ref, ...), custom_call_target="tpu_custom_call" | custom-call | flops 10192158720 | bytes 10616832 | tf_op jit(solution)/shard_map/attend_back/pallas_call | solution.py:259
  236.4 0.0 collective-permute-done.a_got
  236.4 0.0 copy-start.1
  236.4 0.0 collective-permute-done.1.b_got
  236.5 1.1 copy-done.1
  237.5 99.6 %finish.1 = (f32[576,768]{1,0:T(8,128)}, f32[16,768]{1,0:T(8,128)}, bf16[8,72,768]{2,1,0:T(8,128)(2,1)}, bf16[8,224,768]{2,1,0:T(8,128)(2,1)}) custom-call(bf16[2304,576]{1,0:T(8,128)(2,1)} %attend_back.1.grads_ref, bf16[2304,768]{1,0:T(8,128)(2,1)} %get-tuple-element.64.rows_ref, bf16[576,768]{1,0:T(8,128)(2,1)} %bitcast.9, f32[768]{0:T(1024)} %gain_ref.5, ...), custom_call_target="tpu_custom_call" | custom-call | flops 4076863488 | bytes 17694720 | tf_op jit(solution)/shard_map/finish/pallas_call | solution.py:662
  337.1 0.8 constant_dynamic-slice_fusion
  337.9 0.6 pad_maximum_fusion
  338.5 0.0 copy-start.2
  338.5 7.2 %unpack.1 = (f32[768,768]{1,0:T(8,128)}, f32[768,768]{1,0:T(8,128)}, f32[192,768]{1,0:T(8,128)}, f32[576,768]{1,0:T(8,128)}, f32[768]{0:T(1024)}, /*index=5*/f32...) custom-call(bf16[8,72,768]{2,1,0:T(8,128)(2,1)} %get-tuple-element.7, ...), custom_call_target="tpu_custom_call" | custom-call | tf_op jit(solution)/shard_map/unpack/pallas_call | solution.py:735
  345.7 0.0 copy-start
  345.7 0.0 copy-done.2
  345.7 0.9 copy.35
  346.6 0.9 copy-done
  347.5 1.2 copy.36
Async XLA Ops:
  189.4 47.1 %collective-permute-start = (bf16[2,2,224,768]{3,2,1,0:T(8,128)(2,1)}, bf16[2,2,224,768]{3,2,1,0:T(8,128)(2,1)S(1)}, u32[]{:S(2)}, u32[]{:S(2)}) collective-permute-start(bf16[2,2,224,768]{3,2,1,0:T(8,128)(2,1)} %get-tuple-element.68), channel_id=1, source_target_pairs={{0,8},{4,12},{8,0},{12,4},{16,24},{20,28},{24,16},{28,20},{1,9},{5... | collective-permute-start | bytes 4128776 | tf_op jit(solution)/shard_map/ppermute | solution.py:1464
  197.2 39.2 %collective-permute-start.1 = (bf16[2,2,224,768]{3,2,1,0:T(8,128)(2,1)}, bf16[2,2,224,768]{3,2,1,0:T(8,128)(2,1)}, u32[]{:S(2)}, u32[]{:S(2)}) collective-permute-start(bf16[2,2,224,768]{3,2,1,0:T(8,128)(2,1)} %get-tuple-element.70), channel_id=1, source_target_pairs={{0,16},{4,20},{8,24},{12,28},{16,0},{20,4},{24,8},{28,12},{1,17},{... | collective-permute-start | bytes 4128776 | tf_op jit(solution)/shard_map/ppermute | solution.py:1464
  236.4 1.1 copy-start.1
  338.5 7.2 %copy-start.2 = (bf16[576,768]{1,0:T(8,128)(2,1)S(1)}, bf16[576,768]{1,0:T(8,128)(2,1)}, u32[]{:S(2)}) copy-start(bf16[576,768]{1,0:T(8,128)(2,1)} %get-tuple-element.106) | copy-start | bytes 2654212
  345.7 1.8 copy-start

commit v3 on v2

--- a/solution.py
+++ b/solution.py
@@ -10,6 +10,7 @@
 
 HEAD_DIM = 64
 LANES = 128
+MOST_TOKENS = 1152
 MASKED = -(2.0**100)
 
 
@@ -34,99 +35,6 @@
 def join_lanes(low, high):
     lane = lax.broadcasted_iota(jnp.int32, low.shape, 1)
     return jnp.where(lane < HEAD_DIM, low, pltpu.roll(high, HEAD_DIM, 1))
-
-
-def attend_kernel(
-    key_block,
-    bounds_ref,
-    q_ref,
-    k_ref,
-    v_ref,
-    pair_ref,
-    single_ref,
-    q_back_ref,
-    peak_ref,
-    acc_ref,
-    score_ref,
-    weight_ref,
-):
-    step = pl.program_id(0)
-    heads, count, _ = q_ref.shape
-    repeats = key_block // LANES
-    peak_ref[...] = jnp.full_like(peak_ref, -3e38)
-    acc_ref[...] = jnp.zeros_like(acc_ref)
-
-    def visit(at, carry):
-        keys = pl.ds(pl.multiple_of(at * key_block, key_block), key_block)
-        for head in range(heads):
-            score_ref[head] = times_transposed(q_ref[head], k_ref[head, keys, :])
-        for head in range(heads):
-            old_peak = peak_ref[head]
-            new_peak = jnp.maximum(old_peak, jnp.max(score_ref[head], axis=1, keepdims=True))
-            peak_ref[head] = new_peak
-            spread = jnp.concatenate([new_peak] * repeats, axis=1)
-            weight_ref[head] = jnp.exp(score_ref[head] - spread).astype(jnp.bfloat16)
-            acc_ref[head] = acc_ref[head] * jnp.exp(old_peak - new_peak)
-        for head in range(heads):
-            acc_ref[head] += jnp.dot(
-                weight_ref[head], v_ref[head, keys, :], preferred_element_type=jnp.float32
-            )
-        return carry
-
-    lax.fori_loop(bounds_ref[0, step], bounds_ref[1, step], visit, 0)
-    lane = lax.broadcasted_iota(jnp.int32, (count, LANES), 1)
-    parts = []
-    for head in range(heads):
-        acc = acc_ref[head]
-        total = acc[:, HEAD_DIM : HEAD_DIM + 1]
-        parts.append(acc / total)
-        log_total = -(peak_ref[head] + jnp.log(total))
-        high, middle, low = split_three(log_total)
-        kept = q_ref[head].astype(jnp.float32)
-        kept = jnp.where(lane == HEAD_DIM + 8, high.astype(jnp.float32), kept)
-        kept = jnp.where(lane == HEAD_DIM + 9, middle.astype(jnp.float32), kept)
-        kept = jnp.where(lane == HEAD_DIM + 10, low.astype(jnp.float32), kept)
-        q_back_ref[head] = kept.astype(jnp.bfloat16)
-    pair_ref[...] = join_lanes(parts[0], parts[1]).astype(jnp.bfloat16)
-    half = count // 2
-    single_ref[...] = join_lanes(parts[2][:half], parts[2][half:]).astype(jnp.bfloat16)
-
-
-def attend(bounds, queries, keys, values, key_block):
-    heads, seq_len, _ = queries.shape
-    steps = bounds.shape[1]
-    block = seq_len // steps
-    q_spec = pl.BlockSpec((heads, block, LANES), lambda i, b: (0, i, 0))
-    full = pl.BlockSpec((heads, seq_len, LANES), lambda i, b: (0, 0, 0))
-    return pl.pallas_call(
-        partial(attend_kernel, key_block),
-        grid_spec=pltpu.PrefetchScalarGridSpec(
-            num_scalar_prefetch=1,
-            grid=(steps,),
-            in_specs=[q_spec, full, full],
-            out_specs=[
-                pl.BlockSpec((block, LANES), lambda i, b: (i, 0)),
-                pl.BlockSpec((block // 2, LANES), lambda i, b: (i, 0)),
-                q_spec,
-            ],
-            scratch_shapes=[
-                pltpu.VMEM((heads, block, LANES), jnp.float32),
-                pltpu.VMEM((heads, block, LANES), jnp.float32),
-                pltpu.VMEM((heads, block, key_block), jnp.float32),
-                pltpu.VMEM((heads, block, key_block), jnp.bfloat16),
-            ],
-        ),
-        out_shape=[
-            jax.ShapeDtypeStruct((seq_len, LANES), jnp.bfloat16),
-            jax.ShapeDtypeStruct((seq_len // 2, LANES), jnp.bfloat16),
-            jax.ShapeDtypeStruct((heads, seq_len, LANES), jnp.bfloat16),
-        ],
-        name="attend",
-        cost_estimate=pl.CostEstimate(
-            flops=4 * heads * seq_len * seq_len * LANES // 2, transcendentals=heads * seq_len * seq_len // 2,
-            bytes_accessed=8 * heads * seq_len * LANES,
-        ),
-    )(bounds, queries, keys, values)
 
 
 def attend_back_kernel(
@@ -765,10 +673,22 @@
     q_out,
     k_out,
     v_out,
+    pairs_out,
+    singles_out,
+    pairs_here,
+    singles_here,
     weights_out,
     bias_out,
     bounds_out,
     blocks,
+    normed_all,
+    queries,
+    keys,
+    values,
+    peaks,
+    sums,
+    scores,
+    weights,
     q_extra,
     k_extra,
     own,
@@ -776,15 +696,17 @@
     send,
     recv,
     local,
+    stored,
 ):
     f32, bf16 = jnp.float32, jnp.bfloat16
     member, here = lax.axis_index("dp"), lax.axis_index("tensor")
     core, x_bit, y_bit = bit_of(member, 0), bit_of(member, 1), bit_of(member, 2)
     own_piece = core * 4 + x_bit * 2 + y_bit
     block, width = tokens_ref.shape
-    heads = q_out.shape[0]
+    heads = queries.shape[0]
     seq_len = ids_ref.shape[1]
     last = shards - 1
+    reach = -(-(MOST_TOKENS - 1) // block)
     slots = iter(range(send.shape[0]))
     pending = []
 
@@ -900,14 +822,27 @@
     v_lane = lax.broadcasted_iota(jnp.int32, (block, LANES), 1)
     v_extra = jnp.where((v_lane >= HEAD_DIM) & (v_lane < HEAD_DIM + 3), 1.0, 0.0).astype(bf16)
 
+    def rows_of(owner, count=block):
+        return pl.ds(pl.multiple_of(owner * count, 16), count)
+
+    def store(which, owner):
+        rows = rows_of(owner)
+        source, out = (
+            (normed_all.at[rows], normed_out.at[rows]),
+            (queries.at[:, rows], q_out.at[:, rows]),
+            (keys.at[:, rows], k_out.at[:, rows]),
+            (values.at[:, rows], v_out.at[:, rows]),
+        )[which]
+        return pltpu.make_async_copy(source, out, stored.at[which, owner])
+
     def project_block(source, owner):
         tokens = source.astype(f32)
         centred = tokens - jnp.mean(tokens, axis=1, keepdims=True)
         inverse = lax.rsqrt(jnp.mean(centred * centred, axis=1, keepdims=True) + eps_norm)
         normed = (centred * inverse * gain + shift).astype(bf16)
-        rows = pl.ds(pl.multiple_of(owner * block, 16), block)
-        normed_out[rows, :] = normed
-        for which, out in ((0, q_out), (1, k_out), (2, v_out)):
+        rows = rows_of(owner)
+        normed_all[rows, :] = normed
+        for which, out in ((0, queries), (1, keys), (2, values)):
             product = times_transposed(normed, qkv_ref[which])
             if which != 1:
                 product = product + qv_bias_ref[which // 2 : which // 2 + 1, :]
@@ -923,13 +858,111 @@
                 if head % 2:
                     tile = pltpu.roll(tile, HEAD_DIM, 1)
                 out[head, rows, :] = jnp.where(low_half, tile, extra.astype(f32)).astype(bf16)
+        store(0, owner).start()
+        store(2, owner).start()
+        store(3, owner).start()
+
+    peaks[...] = jnp.full_like(peaks, -3e38)
+    sums[...] = jnp.zeros_like(sums)
+
+    def away(index):
+        return jnp.maximum(index - here, here - index)
+
+    def visit(owner, other):
+        rows, across = rows_of(owner), rows_of(other)
+        for head in range(heads):
+            scores[head] = times_transposed(queries[head, rows, :], keys[head, across, :])
+        for head in range(heads):
+            old_peak = peaks[head, rows, :]
+            new_peak = jnp.maximum(old_peak, jnp.max(scores[head], axis=1, keepdims=True))
+            peaks[head, rows, :] = new_peak
+            spread = jnp.concatenate([new_peak] * -(-block // LANES), axis=1)[:, :block]
+            weights[head] = jnp.exp(scores[head] - spread).astype(bf16)
+            sums[head, rows, :] = sums[head, rows, :] * jnp.exp(old_peak - new_peak)
+        for head in range(heads):
+            sums[head, rows, :] += jnp.dot(
+                weights[head], values[head, across, :], preferred_element_type=f32
+            )
+
+    pair_slots = [next(slots) for _ in range(shards)]
+    single_slots = [next(slots) for _ in range(shards)]
+
+    def exchange(owner, source):
+        half_block = block // 2
+        return [
+            pltpu.make_async_remote_copy(
+                src_ref=out.at[rows_of(owner, count)],
+                dst_ref=landing.at[source],
+                send_sem=send.at[base + owner],
+                recv_sem=recv.at[base + source],
+                device_id={"tensor": owner},
+                device_id_type=MESH,
+            )
+            for out, landing, count, base in (
+                (pairs_out, pairs_here, block, pair_slots[0]),
+                (singles_out, singles_here, half_block, single_slots[0]),
+            )
+        ]
+
+    def complete(owner):
+        rows, half_block = rows_of(owner), block // 2
+        parts = []
+        for head in range(heads):
+            total = sums[head, rows, HEAD_DIM : HEAD_DIM + 1]
+            parts.append(sums[head, rows, :] / total)
+            high, middle_part, low = split_three(-(peaks[head, rows, :] + jnp.log(total)))
+            kept = queries[head, rows, :].astype(f32)
+            for at, value in enumerate((high, middle_part, low)):
+                kept = jnp.where(v_lane == HEAD_DIM + 8 + at, value.astype(f32), kept)
+            queries[head, rows, :] = kept.astype(bf16)
+        pair = join_lanes(parts[0], parts[1]).astype(bf16)
+        single = join_lanes(parts[2][:half_block], parts[2][half_block:]).astype(bf16)
+        pairs_out[rows, :] = pair
+        singles_out[rows_of(owner, half_block), :] = single
+        store(1, owner).start()
+
+        @pl.when(owner == here)
+        def _():
+            pairs_here[here] = pair
+            singles_here[here] = single
+
+        @pl.when(owner != here)
+        def _():
+            for copy in exchange(owner, here):
+                copy.start()
+
+    def attend_known(time):
+        def each(at, carry):
+            owner = lax.rem(here + shards // 2 + at, shards)
+
+            def other_block(other, carry):
+                near = jnp.maximum(owner - other, other - owner) <= reach
+                known = jnp.maximum(jnp.maximum(away(owner), away(other)), 1)
+
+                @pl.when(near & (known == time))
+                def _():
+                    visit(owner, other)
+
+                return carry
+
+            lax.fori_loop(0, shards, other_block, 0)
+            final = jnp.maximum(
+                away(jnp.maximum(owner - reach, 0)), away(jnp.minimum(owner + reach, last))
+            )
+
+            @pl.when(final == time)
+            def _():
+                complete(owner)
+
+            return carry
+
+        lax.fori_loop(0, shards, each, 0)
 
     project_block(tokens_ref[...], here)
     for time in range(1, shards):
         hop("w", time, "t")
 
     half = shards // 2
-    out_a = [weights_out.at[own_piece, 0:half]]
     stores = []
     for owner in range(shards):
         at = 2 + owner
@@ -943,8 +976,8 @@
             pltpu.make_async_copy(chain.at[owner], weights_out.at[own_piece, owner], local.at[at]).start()
 
         stores.append(pltpu.make_async_copy(own, weights_out.at[own_piece, owner], local.at[at]))
-    for store in stores:
-        store.wait()
+    for saved in stores:
+        saved.wait()
 
     def part(low, pieces):
         owners = pl.ds(0, half) if low else pl.ds(half, shards - half)
@@ -960,27 +993,40 @@
     stage = gather_stage(True, [own_piece], 2) + gather_stage(False, [own_piece], 1)
 
     def arrived(time):
-        for way in (-1, 1):
-            owner = here + way * time
+        def each(at, carry):
+            owner = here + (2 * at - 1) * time
 
             @pl.when((owner >= 0) & (owner <= last))
             def _():
                 project_block(blocks[owner], owner)
 
+            return carry
+
+        lax.fori_loop(0, 2, each, 0)
+
     for time in range(1, shards):
         hop("t", time)
+        arrived(time)
         if time == 1:
-            arrived(time)
             wait_all(stage)
             stage = gather_stage(True, [pl.ds(core * 4 + x_bit * 2, 2)], 1) + gather_stage(
                 False, [core * 4 + 2 * at + y_bit for at in range(2)], 2
             )
-        elif time == 2:
-            arrived(time)
+        attend_known(time)
+        if time == 2:
             wait_all(stage)
             stage = [start_dp(weights_out.at[pl.ds(core * 4, 4)], weights_out.at[pl.ds(core * 4, 4)], 0)]
-        else:
-            arrived(time)
+    for owner in range(shards):
+
+        @pl.when(here != owner)
+        def _():
+            for copy in exchange(here, owner):
+                copy.wait_recv()
+            for copy in exchange(owner, here):
+                copy.wait_send()
+
+        for which in range(4):
+            store(which, owner).wait()
     wait_all(stage)
     wait_all(bias_copies)
     for copy in pending:
@@ -1009,7 +1055,7 @@
     seq_len = block * shards
     heads = qkv.shape[1] // HEAD_DIM
     rows = -(-(fc1.shape[0] + fc2.shape[0] + proj.shape[0]) // PIECES // 16) * 16
-    copies = 4 * shards + (shards - 1) + 6
+    copies = 6 * shards + (shards - 1) + 6
     vm = pltpu.VMEM
     on_chip = pl.BlockSpec(memory_space=vm)
     anywhere = pl.BlockSpec(memory_space=pl.ANY)
@@ -1017,18 +1063,32 @@
     return pl.pallas_call(
         partial(start_kernel, shards, dp_bits, visits[1]),
         in_specs=[on_chip] * 6 + [anywhere] * 2 + [on_chip] * 2,
-        out_specs=[on_chip] * 4 + [anywhere, on_chip, pl.BlockSpec(memory_space=pltpu.SMEM)],
+        out_specs=[anywhere] * 4
+        + [on_chip] * 4
+        + [anywhere, on_chip, pl.BlockSpec(memory_space=pltpu.SMEM)],
         out_shape=[
             jax.ShapeDtypeStruct((seq_len, width), bf16),
             head_rows,
             head_rows,
             head_rows,
+            jax.ShapeDtypeStruct((seq_len, LANES), bf16),
+            jax.ShapeDtypeStruct((seq_len // 2, LANES), bf16),
+            jax.ShapeDtypeStruct((shards, block, LANES), bf16),
+            jax.ShapeDtypeStruct((shards, block // 2, LANES), bf16),
             jax.ShapeDtypeStruct((PIECES, shards, rows, width), bf16),
             jax.ShapeDtypeStruct((shards, 1, width), f32),
             jax.ShapeDtypeStruct((2, visits[0]), jnp.int32),
         ],
         scratch_shapes=[
             vm((shards, block, width), bf16),
+            vm((seq_len, width), bf16),
+            vm((heads, seq_len, LANES), bf16),
+            vm((heads, seq_len, LANES), bf16),
+            vm((heads, seq_len, LANES), bf16),
+            vm((heads, seq_len, LANES), f32),
+            vm((heads, seq_len, LANES), f32),
+            vm((heads, block, block), f32),
+            vm((heads, block, block), bf16),
             vm((seq_len, LANES), bf16),
             vm((seq_len, LANES), bf16),
             vm((rows, width), bf16),
@@ -1036,8 +1096,11 @@
             pltpu.SemaphoreType.DMA((copies,)),
             pltpu.SemaphoreType.DMA((copies,)),
             pltpu.SemaphoreType.DMA((2 + shards,)),
+            pltpu.SemaphoreType.DMA((4, shards)),
         ],
-        compiler_params=pltpu.CompilerParams(collective_id=0, has_side_effects=True),
+        compiler_params=pltpu.CompilerParams(
+            collective_id=0, has_side_effects=True, vmem_limit_bytes=62 * 1024 * 1024
+        ),
         name="start",
         cost_estimate=pl.CostEstimate(
             flops=6 * seq_len * width * heads * HEAD_DIM, transcendentals=0, bytes_accessed=40 * block * width
@@ -1051,8 +1114,8 @@
 def middle_kernel(
     shards,
     dp_bits,
-    pairs_ref,
-    singles_ref,
+    pairs,
+    singles,
     weights_ref,
     fc1_bias_ref,
     proj_bias_ref,
@@ -1073,8 +1136,6 @@
     b_keep,
     b_away,
     weights,
-    pairs,
-    singles,
     attended,
     proj,
     branch,
@@ -1120,18 +1181,6 @@
         loads.append(load)
     greet(dp_bits, shards)
 
-    def rows_of(owner, count):
-        return pl.ds(pl.multiple_of(owner * count, 16), count)
-
-    copies = []
-    for source, landing in ((pairs_ref, pairs), (singles_ref, singles)):
-        count = landing.shape[1]
-        for way in range(1, shards):
-            target = lax.rem(here + way, shards)
-            copy = copy_to(source.at[rows_of(target, count)], landing.at[here], next(slots), tensor=target)
-            copy.start()
-            copies.append(copy)
-        landing[here] = source[rows_of(here, count), :]
     for load in loads:
         load.wait()
 
@@ -1163,8 +1212,6 @@
         own_proj = proj_of(owner)
         proj[owner * LANES : (owner + 1) * LANES, :] = own_proj[:LANES]
         proj[third + owner * HEAD_DIM : third + (owner + 1) * HEAD_DIM, :] = own_proj[LANES:]
-    for copy in copies:
-        copy.wait_recv()
     middle_row = block // 2
     for owner in range(shards):
         attended[:, owner * LANES : (owner + 1) * LANES] = pairs[owner]
@@ -1338,7 +1385,7 @@
                     )
     for copy in back:
         copy.wait_recv()
-    for copy in copies + back:
+    for copy in back:
         copy.wait_send()
     for owner in range(shards):
         core_copy(owner).wait_send()
@@ -1352,7 +1399,7 @@
     vm = pltpu.VMEM
     on_chip = pl.BlockSpec(memory_space=vm)
     quarter = jax.ShapeDtypeStruct((2, shards // 2, rows, width), bf16)
-    copies = 4 * (shards - 1) + shards
+    copies = 2 * (shards - 1) + shards
     return pl.pallas_call(
         partial(middle_kernel, shards, dp_bits),
         in_specs=[on_chip, on_chip, pl.BlockSpec(memory_space=pl.ANY)] + [on_chip] * 9,
@@ -1370,8 +1417,6 @@
         ],
         scratch_shapes=[
             vm(weights.shape, bf16),
-            vm((shards, block, LANES), bf16),
-            vm((shards, block // 2, LANES), bf16),
             vm((block, width), bf16),
             vm((width, width), bf16),
             vm((block, width), f32),
@@ -1436,7 +1481,7 @@
 
     visits = (shards, seq_len // 6)
     turned = qkv_weight.transpose(0, 2, 1)
-    full_one, queries, keys, values, gathered, fc1_bias_full, bounds = start(
+    full_one, queries, keys, values, pairs, singles, pairs_here, singles_here, gathered, fc1_bias_full, bounds = start(
         shards,
         members,
         visits,
@@ -1451,11 +1496,9 @@
         proj_weight,
         fc1_bias,
     )
-    pairs, singles, queries_back = attend(bounds, queries, keys, values, visits[1])
-
     params = (proj_bias, scale_one, ln2_gain, ln2_bias, fc2_bias, scale_two)
     block_out, grad_hidden, pair_grads, single_grads, vectors, a_keep, a_away, b_keep, b_away = middle(
-        shards, members, pairs, singles, gathered, fc1_bias_full, params, tokens, cotangent
+        shards, members, pairs_here, singles_here, gathered, fc1_bias_full, params, tokens, cotangent
     )
     pair_grads = pair_grads.reshape(seq_len, LANES)
     single_grads = single_grads.reshape(seq_len // 2, LANES)
@@ -1464,7 +1507,7 @@
         return lax.ppermute(value, "dp", [(j, j ^ (1 << bit)) for j in range(members)])
 
     a_got, b_got = swap(a_away, 1), swap(b_away, 2)
-    grad_heads = attend_back(bounds, queries_back, keys, values, pairs, singles, pair_grads, single_grads, visits[1])
+    grad_heads = attend_back(bounds, queries, keys, values, pairs, singles, pair_grads, single_grads, visits[1])
     grad_tokens, totals, qkv_pieces, weight_pieces = finish(
         shards,
         members,

time: 350 us -> 333 us (0.951)
  Pallas kernels: 334 us -> 321 us
  starting transfers between devices: 8.99 us -> 3.07 us
    pallas_call x1 -> x0, Pallas kernels: 22.8 us -> none  [attend(): pl.pallas_call(partial(attend_kernel, key_block), grid_spec=pltpu.Prefetc...]
    pallas_call x1, Pallas kernels: 87.6 us -> 110 us  [start(): pl.pallas_call(partial(start_kernel, shards, dp_bits, visits[1]), in_spec...]
    pallas_call x1, Pallas kernels: 78.3 us -> 66.7 us  [middle(): pl.pallas_call(partial(middle_kernel, shards, dp_bits), in_specs=[on_chip...]
    ppermute x2, starting transfers between devices: 8.99 us -> 3.07 us  [swap(): lax.ppermute(value, 'dp', [(j, j ^ 1 << bit) for j in range(members)])]
  transfers between devices with their start and end apart: 2 -> 2, of which waited for: 0 -> 0; matrix products, arithmetic and copies ran while one was open for 0% -> 0% of each run, Pallas kernels for 11% -> 12%
where the time goes in v3:
time: 333 us; the launch traced here: 331 us
  Pallas kernels  321 us (96%)
  local copies, waits for them, and re-layouts  4.85 us (1%)
    pallas_call x1, Pallas kernels, start(): pl.pallas_call(partial(start_kernel, shards, dp_bits, visits[1]), in_spec...  110 us
    pallas_call x1, Pallas kernels, finish(): pl.pallas_call(partial(finish_kernel, shards, dp_bits), in_specs=[pl.Bloc...  97.6 us
    pallas_call x1, Pallas kernels, middle(): pl.pallas_call(partial(middle_kernel, shards, dp_bits), in_specs=[on_chip...  66.7 us
    pallas_call x1, Pallas kernels, attend_back(): pl.pallas_call(partial(attend_back_kernel, query_block), grid_spec=pltpu....  39.8 us
    pallas_call x1, Pallas kernels, unpack(): pl.pallas_call(unpack_kernel, grid=(PIECES,), in_specs=[pl.BlockSpec((1,...  7.16 us
  transfers between devices with their start and end apart: 2, of which 0 were waited for; matrix products, arithmetic and copies ran while one was open for 0% of the time, Pallas kernels for 12%

profile of v3, /device:TPU:16, one launch (start us, length us, event | category | flops | bytes accessed | tf_op | source)
XLA Modules:
  0.0 330.7 jit_solution(6471089788229714151)
XLA Ops:
  0.6 110.2 %start.1 = (bf16[2304,768]{1,0:T(8,128)(2,1)}, bf16[3,2304,128]{2,1,0:T(8,128)(2,1)}, bf16[3,2304,128]{2,1,0:T(8,128)(2,1)}, bf16[3,2304,128]{2,1,0:T(8,128)(2,1...) custom-call(bf16[576,768]{1,0:T(8,128)(2,1)} %tokens_ref.5, ...), custom_call_target="tpu_custom_call" | custom-call | flops 2038431744 | bytes 17694720 | tf_op jit(solution)/shard_map/start/pallas_call | solution.py:1063
  110.8 66.7 %middle.1 = (bf16[576,768]{1,0:T(8,128)(2,1)}, f32[576,768]{1,0:T(8,128)}, bf16[4,576,128]{2,1,0:T(8,128)(2,1)}, bf16[4,288,128]{2,1,0:T(8,128)(2,1)}, f32[16,76...) custom-call(bf16[4,576,128]{2,1,0:T(8,128)(2,1)} %get-tuple-element., ...), custom_call_target="tpu_custom_call" | custom-call | flops 16307453952 | bytes 17694720 | tf_op jit(solution)/shard_map/middle/pallas_call | solution.py:1403
  177.6 1.6 collective-permute-start
  179.1 1.5 collective-permute-start.1
  180.7 39.8 %attend_back.1.grads_ref = bf16[2304,576]{1,0:T(8,128)(2,1)} custom-call(s32[2,4]{1,0:T(2,128)} %get-tuple-element.58.bounds_ref, bf16[3,2304,128]{2,1,0:T(8,128)(2,1)} %get-tuple-element.59.q_ref, bf16[3,2304,128]{2,1,0:T(8,128)(2,1)} %get-tuple-element.60.k_ref, bf16[3,2304,128]{2,1,0:T(8,128)(2,1)} %get-tuple-element.61.v_ref, ...), custom_call_target="tpu_custom_call" | custom-call | flops 10192158720 | bytes 10616832 | tf_op jit(solution)/shard_map/attend_back/pallas_call | solution.py:167
  220.5 0.0 collective-permute-done.a_got
  220.5 0.0 copy-start.1
  220.5 0.0 collective-permute-done.1.b_got
  220.5 1.1 copy-done.1
  221.6 97.6 %finish.1 = (f32[576,768]{1,0:T(8,128)}, f32[16,768]{1,0:T(8,128)}, bf16[8,72,768]{2,1,0:T(8,128)(2,1)}, bf16[8,224,768]{2,1,0:T(8,128)(2,1)}) custom-call(bf16[2304,576]{1,0:T(8,128)(2,1)} %attend_back.1.grads_ref, bf16[2304,768]{1,0:T(8,128)(2,1)} %get-tuple-element.66.rows_ref, bf16[576,768]{1,0:T(8,128)(2,1)} %bitcast.9, f32[768]{0:T(1024)} %gain_ref.5, ...), custom_call_target="tpu_custom_call" | custom-call | flops 4076863488 | bytes 17694720 | tf_op jit(solution)/shard_map/finish/pallas_call | solution.py:570
  319.1 0.8 constant_dynamic-slice_fusion
  319.9 0.6 pad_maximum_fusion
  320.5 0.0 copy-start.2
  320.5 7.2 %unpack.1 = (f32[768,768]{1,0:T(8,128)}, f32[768,768]{1,0:T(8,128)}, f32[192,768]{1,0:T(8,128)}, f32[576,768]{1,0:T(8,128)}, f32[768]{0:T(1024)}, /*index=5*/f32...) custom-call(bf16[8,72,768]{2,1,0:T(8,128)(2,1)} %get-tuple-element.7, ...), custom_call_target="tpu_custom_call" | custom-call | tf_op jit(solution)/shard_map/unpack/pallas_call | solution.py:643
  327.7 0.0 copy-start
  327.7 0.0 copy-done.2
  327.7 0.9 copy.35
  328.6 0.9 copy-done
  329.5 1.2 copy.36
Async XLA Ops:
  177.6 42.9 %collective-permute-start = (bf16[2,2,224,768]{3,2,1,0:T(8,128)(2,1)}, bf16[2,2,224,768]{3,2,1,0:T(8,128)(2,1)S(1)}, u32[]{:S(2)}, u32[]{:S(2)}) collective-permute-start(bf16[2,2,224,768]{3,2,1,0:T(8,128)(2,1)} %get-tuple-element.70), channel_id=1, source_target_pairs={{0,8},{4,12},{8,0},{12,4},{16,24},{20,28},{24,16},{28,20},{1,9},{5... | collective-permute-start | bytes 4128776 | tf_op jit(solution)/shard_map/ppermute | solution.py:1507
  179.1 41.4 %collective-permute-start.1 = (bf16[2,2,224,768]{3,2,1,0:T(8,128)(2,1)}, bf16[2,2,224,768]{3,2,1,0:T(8,128)(2,1)}, u32[]{:S(2)}, u32[]{:S(2)}) collective-permute-start(bf16[2,2,224,768]{3,2,1,0:T(8,128)(2,1)} %get-tuple-element.72), channel_id=1, source_target_pairs={{0,16},{4,20},{8,24},{12,28},{16,0},{20,4},{24,8},{28,12},{1,17},{... | collective-permute-start | bytes 4128776 | tf_op jit(solution)/shard_map/ppermute | solution.py:1507
  220.5 1.1 copy-start.1
  320.5 7.2 %copy-start.2 = (bf16[576,768]{1,0:T(8,128)(2,1)S(1)}, bf16[576,768]{1,0:T(8,128)(2,1)}, u32[]{:S(2)}) copy-start(bf16[576,768]{1,0:T(8,128)(2,1)} %get-tuple-element.108) | copy-start | bytes 2654212
  327.7 1.8 copy-start

commit v4 on v3

--- a/solution.py
+++ b/solution.py
@@ -35,159 +35,6 @@
 def join_lanes(low, high):
     lane = lax.broadcasted_iota(jnp.int32, low.shape, 1)
     return jnp.where(lane < HEAD_DIM, low, pltpu.roll(high, HEAD_DIM, 1))
-
-
-def attend_back_kernel(
-    query_block,
-    bounds_ref,
-    q_ref,
-    k_ref,
-    v_ref,
-    pair_ref,
-    single_ref,
-    pair_grad_ref,
-    single_grad_ref,
-    out_ref,
-    grad_heads_ref,
-    dq_ref,
-    dk_ref,
-    dv_ref,
-    k0_ref,
-    prob_ref,
-    grad_score_ref,
-):
-    f32, bf16 = jnp.float32, jnp.bfloat16
-    step = pl.program_id(0)
-    heads, count, _ = k_ref.shape
-    seq_len = q_ref.shape[1]
-    blocks = seq_len // query_block
-
-    @pl.when(step == 0)
-    def _():
-        dq_ref[...] = jnp.zeros_like(dq_ref)
-        source = lax.broadcasted_iota(jnp.int32, (LANES, LANES), 0)
-        target = lax.broadcasted_iota(jnp.int32, (LANES, LANES), 1)
-        gathers = (target >= HEAD_DIM) & (target < HEAD_DIM + 3)
-        picks = []
-        for odd in range(2):
-            own = (source >= HEAD_DIM * odd) & (source < HEAD_DIM * (odd + 1))
-            summing = jnp.where(own & gathers, -1.0, 0.0).astype(bf16)
-            moving = jnp.where(own & (source - HEAD_DIM * odd == target), 1.0, 0.0).astype(bf16)
-            picks.append((summing, moving))
-        half = count // 2
-        lane = lax.broadcasted_iota(jnp.int32, (half, LANES), 1)
-
-        def prepare(at, carry):
-            for part in range(2):
-                rows = pl.ds(pl.multiple_of((2 * at + part) * half, half), half)
-                single_rows = pl.ds(pl.multiple_of(at * half, half), half)
-                for head, odd, mixed, grad in (
-                    (0, 0, pair_ref[rows, :], pair_grad_ref[rows, :]),
-                    (1, 1, pair_ref[rows, :], pair_grad_ref[rows, :]),
-                    (2, part, single_ref[single_rows, :], single_grad_ref[single_rows, :]),
-                ):
-                    summing, moving = picks[odd]
-                    product = grad.astype(f32) * mixed.astype(f32)
-                    high = product.astype(bf16)
-                    low = (product - high.astype(f32)).astype(bf16)
-                    shared = jnp.dot(high, summing, preferred_element_type=f32) + jnp.dot(
-                        low, summing, preferred_element_type=f32
-                    )
-                    first_part, second_part, third_part = split_three(shared)
-                    moved = jnp.dot(grad, moving, preferred_element_type=f32)
-                    moved = jnp.where(lane == HEAD_DIM, first_part.astype(f32), moved)
-                    moved = jnp.where(lane == HEAD_DIM + 1, second_part.astype(f32), moved)
-                    moved = jnp.where(lane == HEAD_DIM + 2, third_part.astype(f32), moved)
-                    grad_heads_ref[head, rows, :] = moved.astype(bf16)
-            return carry
-
-        lax.fori_loop(0, seq_len // count, prepare, 0)
-
-    dk_ref[...] = jnp.zeros_like(dk_ref)
-    dv_ref[...] = jnp.zeros_like(dv_ref)
-
-    def visit(at, carry):
-        rows = pl.ds(pl.multiple_of(at * query_block, query_block), query_block)
-        for head in range(heads):
-            probs = jnp.exp(times_transposed(k_ref[head], q_ref[head, rows, :]))
-            grad_probs = times_transposed(v_ref[head], grad_heads_ref[head, rows, :])
-            prob_ref[head] = probs.astype(bf16)
-            grad_score_ref[head] = (probs * grad_probs).astype(bf16)
-        for head in range(heads):
-            dv_ref[head] += jnp.dot(
-                prob_ref[head], grad_heads_ref[head, rows, :], preferred_element_type=f32
-            )
-            dk_ref[head] += jnp.dot(
-                grad_score_ref[head], q_ref[head, rows, :], preferred_element_type=f32
-            )
-            dq_ref[head, rows, :] += contract_rows(grad_score_ref[head], k_ref[head])
-        return carry
-
-    lax.fori_loop(bounds_ref[0, step], bounds_ref[1, step], visit, 0)
-    lane = lax.broadcasted_iota(jnp.int32, (count, LANES), 1)
-    low_half = lane < HEAD_DIM
-    here = pl.ds(pl.multiple_of(step * count, count), count)
-    k0_ref[here, :] = dk_ref[0].astype(bf16)
-    out_ref[here, 256:384] = jnp.where(
-        low_half, dk_ref[1], pltpu.roll(dk_ref[2], HEAD_DIM, 1)
-    ).astype(bf16)
-    out_ref[here, 384:512] = jnp.where(
-        low_half, dv_ref[0], pltpu.roll(dv_ref[1], HEAD_DIM, 1)
-    ).astype(bf16)
-    out_ref[here, 512:576] = dv_ref[2][:, :HEAD_DIM].astype(bf16)
-
-    @pl.when(step == pl.num_programs(0) - 1)
-    def _():
-        scale = HEAD_DIM**-0.5
-
-        def close(at, carry):
-            rows = pl.ds(pl.multiple_of(at * query_block, query_block), query_block)
-            low_half = lax.broadcasted_iota(jnp.int32, (query_block, LANES), 1) < HEAD_DIM
-            second = pltpu.roll(dq_ref[1, rows, :], HEAD_DIM, 1)
-            out_ref[rows, 0:128] = (
-                jnp.where(low_half, dq_ref[0, rows, :], second) * scale
-            ).astype(bf16)
-            first_keys = pltpu.roll(k0_ref[rows, :].astype(f32), HEAD_DIM, 1)
-            out_ref[rows, 128:256] = jnp.where(
-                low_half, dq_ref[2, rows, :] * scale, first_keys
-            ).astype(bf16)
-            return carry
-
-        lax.fori_loop(0, blocks, close, 0)
-
-
-def attend_back(bounds, queries, keys, values, pairs, singles, pair_grads, single_grads, query_block):
-    heads, seq_len, _ = queries.shape
-    steps = bounds.shape[1]
-    block = seq_len // steps
-    k_spec = pl.BlockSpec((heads, block, LANES), lambda i, b: (0, i, 0))
-    full = pl.BlockSpec((heads, seq_len, LANES), lambda i, b: (0, 0, 0))
-    pair = pl.BlockSpec(pairs.shape, lambda i, b: (0, 0))
-    single = pl.BlockSpec(singles.shape, lambda i, b: (0, 0))
-    return pl.pallas_call(
-        partial(attend_back_kernel, query_block),
-        grid_spec=pltpu.PrefetchScalarGridSpec(
-            num_scalar_prefetch=1,
-            grid=(steps,),
-            in_specs=[full, k_spec, k_spec, pair, single, pair, single],
-            out_specs=pl.BlockSpec((seq_len, 3 * heads * HEAD_DIM), lambda i, b: (0, 0)),
-            scratch_shapes=[
-                pltpu.VMEM((heads, seq_len, LANES), jnp.bfloat16),
-                pltpu.VMEM((heads, seq_len, LANES), jnp.float32),
-                pltpu.VMEM((heads, block, LANES), jnp.float32),
-                pltpu.VMEM((heads, block, LANES), jnp.float32),
-                pltpu.VMEM((seq_len, LANES), jnp.bfloat16),
-                pltpu.VMEM((heads, block, query_block), jnp.bfloat16),
-                pltpu.VMEM((heads, block, query_block), jnp.bfloat16),
-            ],
-        ),
-        out_shape=jax.ShapeDtypeStruct((seq_len, 3 * heads * HEAD_DIM), jnp.bfloat16),
-        name="attend_back",
-        cost_estimate=pl.CostEstimate(
-            flops=10 * heads * seq_len * seq_len * LANES // 2, transcendentals=heads * seq_len * seq_len // 2,
-            bytes_accessed=12 * heads * seq_len * LANES,
-        ),
-    )(bounds, queries, keys, values, pairs, singles, pair_grads, single_grads)
 
 
 MESH = pl.DeviceIdType.MESH
@@ -217,32 +64,45 @@
     pl.semaphore_wait(barrier, len(peers))
 
 
-def finish_kernel(
+def back_kernel(
     shards,
     dp_bits,
-    grads_ref,
-    rows_ref,
+    q_ref,
+    k_ref,
+    v_ref,
+    pair_ref,
+    single_ref,
+    pair_grad_ref,
+    single_grad_ref,
     weight_ref,
     gain_ref,
     shift_ref,
     vectors_ref,
+    rows_ref,
     tokens_ref,
     hidden_ref,
     a_keep,
-    a_got,
+    a_away,
     b_keep,
-    b_got,
+    b_away,
     tokens_out,
     vectors_out,
     qkv_out,
     weights_out,
+    grad_heads,
+    dq,
+    dk,
+    dv,
+    probs,
+    grad_scores,
+    packed,
     rows_own,
     tokens_own,
     hidden_own,
     part,
-    from_left,
-    from_right,
+    arrived,
     q_wide,
+    column_sums,
     q_all,
     q_half,
     q_quarter,
@@ -255,6 +115,8 @@
     v_shards,
     a_sum,
     b_sum,
+    a_got,
+    b_got,
     a_second,
     b_second,
     pieces,
@@ -265,20 +127,15 @@
     local,
 ):
     f32, bf16 = jnp.float32, jnp.bfloat16
-    loads = []
-    for at, (source, landing) in enumerate(
-        ((rows_ref, rows_own), (tokens_ref, tokens_own), (hidden_ref, hidden_own))
-    ):
-        loads.append(pltpu.make_async_copy(source, landing, local.at[at]))
-        loads[-1].start()
     member, here = lax.axis_index("dp"), lax.axis_index("tensor")
     core, x_bit, y_bit = bit_of(member, 0), bit_of(member, 1), bit_of(member, 2)
     own_piece = core * 4 + x_bit * 2 + y_bit
-    block = part.shape[1]
-    width = part.shape[2]
-    columns = grads_ref.shape[1]
+    block, width = part.shape[1], part.shape[2]
+    heads = q_ref.shape[0]
+    columns = weight_ref.shape[0]
     half_rows = weights_out.shape[1] // 2
     last = shards - 1
+    reach = -(-(MOST_TOKENS - 1) // block)
     gain, shift = (ref[...].reshape(1, width) for ref in (gain_ref, shift_ref))
     slots = iter(range(send.shape[0]))
     pending = []
@@ -295,108 +152,260 @@
             pending.append(copy)
         return copy
 
+    def load(at):
+        source, landing = ((a_keep, a_sum), (b_keep, b_sum), (tokens_ref, tokens_own), (hidden_ref, hidden_own))[at]
+        return pltpu.make_async_copy(source, landing, local.at[at])
+
+    def load_rows(owner):
+        rows = pl.ds(pl.multiple_of(owner * block, 16), block)
+        return pltpu.make_async_copy(rows_ref.at[rows], rows_own, local.at[4])
+
+    for at in range(4):
+        load(at).start()
+    load_rows(last).start()
     greet(dp_bits, shards)
-
-    def add_into(out, left, right):
-        def step(at, carry):
-            out[at] = rounded_sum(left[at], right[at])
-            return carry
-
-        lax.fori_loop(0, out.shape[0], step, 0)
-
-    def sum_pairs(out, left, right):
+    start_dp(a_away, a_got, 1)
+    start_dp(b_away, b_got, 2)
+    first_a, first_b = pending[-2:]
+    second_slots = [next(slots) for _ in range(2)]
+
+    def second(at):
+        if at:
+            return copy_to(b_sum.at[1 - x_bit], b_second, second_slots[1], dp=partner_of(member, 1))
+        return copy_to(a_sum.at[1 - y_bit], a_second, second_slots[0], dp=partner_of(member, 2))
+
+    z_slots = [next(slots) for _ in range(1, shards)]
+
+    def piece_copy(way):
+        target = lax.rem(here + way, shards)
+        return copy_to(pieces.at[target], z_got.at[way - 1], z_slots[way - 1], tensor=target)
+
+    more_slots = [next(slots) for _ in range(PIECE_BITS, dp_bits)]
+
+    def sum_pairs(out, right):
         def step(at, carry):
             one, two = at // out.shape[1], lax.rem(at, out.shape[1])
-            out[one, two] = rounded_sum(left[one, two], right[one, two])
+            out[one, two] = rounded_sum(out[one, two], right[one, two])
             return carry
 
         lax.fori_loop(0, out.shape[0] * out.shape[1], step, 0)
 
-    sum_pairs(a_sum, a_keep, a_got)
-    sum_pairs(b_sum, b_keep, b_got)
-    second_a = start_dp(a_sum.at[1 - y_bit], a_second, 2)
-    second_b = start_dp(b_sum.at[1 - x_bit], b_second, 1)
+    def second_exchange():
+        first_a.wait_recv()
+        first_b.wait_recv()
+        load(0).wait()
+        load(1).wait()
+        sum_pairs(a_sum, a_got)
+        sum_pairs(b_sum, b_got)
+        second(0).start()
+        second(1).start()
+
+    def shard_exchange():
+        second(0).wait_recv()
+        second(1).wait_recv()
+        split = shards // 2
+        for at in range(split):
+            pieces[at] = rounded_sum(a_sum[y_bit, at], a_second[at])
+            pieces[split + at] = rounded_sum(b_sum[x_bit, at], b_second[at])
+        for bit in range(PIECE_BITS, dp_bits):
+            at = bit - PIECE_BITS
+            extra = copy_to(pieces, pieces_more.at[at], more_slots[at], dp=partner_of(member, bit))
+            extra.start()
+            extra.wait_recv()
+            extra.wait_send()
+
+            def step(owner, carry):
+                pieces[owner] = rounded_sum(pieces[owner], pieces_more[at, owner])
+                return carry
+
+            lax.fori_loop(0, shards, step, 0)
+        for way in range(1, shards):
+            piece_copy(way).start()
 
     right_slots = [next(slots) for _ in range(shards)]
     left_slots = [next(slots) for _ in range(shards)]
 
     def to_right(owner):
-        return copy_to(part.at[owner], from_left.at[owner], right_slots[owner], tensor=lax.rem(here + 1, shards))
-
-    def to_left(owner):
+        return copy_to(part.at[owner], arrived.at[owner], right_slots[owner], tensor=lax.rem(here + 1, shards))
+
+    def to_left(owner, target=None):
+        to = lax.rem(here + last, shards) if target is None else target
+        landing = jnp.where(owner == to, shards, owner)
         return copy_to(
-            part.at[owner], from_right.at[owner], left_slots[owner], tensor=lax.rem(here + last, shards)
+            part.at[owner], arrived.at[landing], left_slots[owner], tensor=lax.rem(here + last, shards)
         )
 
-    def add_arrived(owner, arrived):
+    def add_arrived(owner, landing):
         def step(at, carry):
             rows = pl.ds(pl.multiple_of(at * (block // 4), 16), block // 4)
-            part[owner, rows, :] = rounded_sum(part[owner, rows, :], arrived[owner, rows, :])
+            part[owner, rows, :] = rounded_sum(part[owner, rows, :], arrived[landing, rows, :])
             return carry
 
         lax.fori_loop(0, 4, step, 0)
+
+    def hop(moved, nth, rightward):
+        owner, at = (last - nth, moved) if rightward else (nth, last - moved)
+        if (at < owner) if rightward else (at > owner):
+
+            @pl.when(here == at)
+            def _():
+                copy = to_right(owner) if rightward else to_left(owner)
+                copy.wait_recv()
+                add_arrived(owner, owner)
+                copy.start()
+
+    dq[...] = jnp.zeros_like(dq)
+    dk[...] = jnp.zeros_like(dk)
+    dv[...] = jnp.zeros_like(dv)
+    q_wide[...] = jnp.zeros_like(q_wide)
+    column_sums[...] = jnp.zeros_like(column_sums)
+    source = lax.broadcasted_iota(jnp.int32, (LANES, LANES), 0)
+    target = lax.broadcasted_iota(jnp.int32, (LANES, LANES), 1)
+    gathers = (target >= HEAD_DIM) & (target < HEAD_DIM + 3)
+    picks = []
+    for odd in range(2):
+        inside = (source >= HEAD_DIM * odd) & (source < HEAD_DIM * (odd + 1))
+        summing = jnp.where(inside & gathers, -1.0, 0.0).astype(bf16)
+        moving = jnp.where(inside & (source - HEAD_DIM * odd == target), 1.0, 0.0).astype(bf16)
+        picks.append((summing, moving))
+    half = block // 2
+    lane = lax.broadcasted_iota(jnp.int32, (half, LANES), 1)
+
+    def prepare(at, carry):
+        for side in range(2):
+            rows = pl.ds(pl.multiple_of((2 * at + side) * half, half), half)
+            single_rows = pl.ds(pl.multiple_of(at * half, half), half)
+            for head, odd, mixed, grad in (
+                (0, 0, pair_ref[rows, :], pair_grad_ref[rows, :]),
+                (1, 1, pair_ref[rows, :], pair_grad_ref[rows, :]),
+                (2, side, single_ref[single_rows, :], single_grad_ref[single_rows, :]),
+            ):
+                summing, moving = picks[odd]
+                product = grad.astype(f32) * mixed.astype(f32)
+                high = product.astype(bf16)
+                low = (product - high.astype(f32)).astype(bf16)
+                shared = jnp.dot(high, summing, preferred_element_type=f32) + jnp.dot(
+                    low, summing, preferred_element_type=f32
+                )
+                moved = jnp.dot(grad, moving, preferred_element_type=f32)
+                for place, value in enumerate(split_three(shared)):
+                    moved = jnp.where(lane == HEAD_DIM + place, value.astype(f32), moved)
+                grad_heads[head, rows, :] = moved.astype(bf16)
+        return carry
+
+    lax.fori_loop(0, shards, prepare, 0)
+
+    def rows_of(owner):
+        return pl.ds(pl.multiple_of(owner * block, 16), block)
+
+    def visit(owner, other):
+        key_rows, query_rows = rows_of(owner), rows_of(other)
+        for head in range(heads):
+            prob = jnp.exp(times_transposed(k_ref[head, key_rows, :], q_ref[head, query_rows, :]))
+            grad_prob = times_transposed(v_ref[head, key_rows, :], grad_heads[head, query_rows, :])
+            probs[head] = prob.astype(bf16)
+            grad_scores[head] = (prob * grad_prob).astype(bf16)
+        for head in range(heads):
+            dv[head, key_rows, :] += jnp.dot(
+                probs[head], grad_heads[head, query_rows, :], preferred_element_type=f32
+            )
+            dk[head, key_rows, :] += jnp.dot(
+                grad_scores[head], q_ref[head, query_rows, :], preferred_element_type=f32
+            )
+            dq[head, query_rows, :] += contract_rows(grad_scores[head], k_ref[head, key_rows, :])
+
+    def close_block(owner, following):
+        rows = rows_of(owner)
+        scale = HEAD_DIM**-0.5
+        for first, low, high in (
+            (0, dq[0, rows, :] * scale, dq[1, rows, :] * scale),
+            (1, dq[2, rows, :] * scale, dk[0, rows, :]),
+            (2, dk[1, rows, :], dk[2, rows, :]),
+            (3, dv[0, rows, :], dv[1, rows, :]),
+        ):
+            packed[:, first * LANES : (first + 1) * LANES] = join_lanes(low, high).astype(bf16)
+        packed[:, 4 * LANES : columns] = dv[2, rows, :HEAD_DIM].astype(bf16)
+        part[owner] = jnp.dot(packed[...], weight_ref[...], preferred_element_type=f32).astype(bf16)
+
+        @pl.when((owner == last) & (here == 0))
+        def _():
+            to_right(last).start()
+
+        @pl.when((owner == 0) & (here == last))
+        def _():
+            to_left(0).start()
+
+        load_rows(owner).wait()
+        q_wide[...] += contract_rows(packed[...], rows_own[...])
+        column_sums[...] += jnp.dot(jnp.ones((8, block), bf16), packed[...], preferred_element_type=f32)
+
+        @pl.when(following >= 0)
+        def _():
+            load_rows(following).start()
 
     order = []
     for near in range((shards + 1) // 2):
         for owner in (last - near, near):
             if owner not in order:
                 order.append(owner)
-    for owner in order:
-        product = jnp.dot(
-            grads_ref[owner * block : (owner + 1) * block, :], weight_ref[...], preferred_element_type=f32
-        )
-        part[owner] = product.astype(bf16)
-        if owner == last:
-
-            @pl.when(here == 0)
+    visits, closing = [], []
+    for at, owner in enumerate(order):
+        rest = order[at:]
+        both = [(owner, owner)]
+        for other in rest[1:]:
+            if abs(owner - other) <= reach:
+                both += [(owner, other), (other, owner)]
+        visits += both
+        closing.append(len(visits) - 1)
+    total_visits = len(visits)
+
+    def lookup(table, at):
+        value = 0
+        for place, entry in enumerate(table):
+            value = value + jnp.where(at == place, entry, 0)
+        return value
+
+    closed = [order[closing.index(at)] if at in closing else -1 for at in range(total_visits)]
+    later = [
+        order[closing.index(at) + 1] if at in closing and at != closing[-1] else -1 for at in range(total_visits)
+    ]
+    events = {
+        total_visits // 2: second_exchange,
+        closing[1] + 1: lambda: hop(1, 0, True),
+        closing[2]: shard_exchange,
+    }
+    assert len(events) == 3 and shards >= 4
+
+    def each_visit(at, carry):
+        visit(lookup([pair[0] for pair in visits], at), lookup([pair[1] for pair in visits], at))
+        for when, event in events.items():
+
+            @pl.when(at == when)
             def _():
-                to_right(owner).start()
-
-        if owner == 0:
-
-            @pl.when(here == last)
-            def _():
-                to_left(owner).start()
-
-    def end_sends():
-        for owner in range(last - 1, 0, -1):
-
-            @pl.when(here == 0)
-            def _():
-                to_right(owner).start()
-
-        for owner in range(1, last):
-
-            @pl.when(here == last)
-            def _():
-                to_left(owner).start()
-
-    def hop(moved, nth):
-        for owner, at, rightward in ((last - nth, moved, True), (nth, last - moved, False)):
-            if (at < owner) if rightward else (at > owner):
-
-                @pl.when(here == at)
-                def _():
-                    copy = to_right(owner) if rightward else to_left(owner)
-                    copy.wait_recv()
-                    add_arrived(owner, from_left if rightward else from_right)
-                    copy.start()
-
-    for load in loads:
-        load.wait()
-    q_wide[...] = jnp.zeros_like(q_wide)
-
-    def grow(at, carry):
-        rows = pl.ds(pl.multiple_of(at * block, 16), block)
-        q_wide[...] += contract_rows(grads_ref[rows, :], rows_own[rows, :])
+                event()
+
+        @pl.when(lookup([int(owner >= 0) for owner in closed], at) == 1)
+        def _():
+            close_block(lookup(closed, at), lookup(later, at))
+
         return carry
 
-    lax.fori_loop(0, shards, grow, 0)
-    sums = jnp.dot(jnp.ones((8, grads_ref.shape[0]), bf16), grads_ref[...], preferred_element_type=f32)
+    lax.fori_loop(0, total_visits, each_visit, 0)
+    for owner in range(last - 1, 0, -1):
+
+        @pl.when(here == 0)
+        def _():
+            to_right(owner).start()
+
+    for owner in range(1, last):
+
+        @pl.when(here == last)
+        def _():
+            to_left(owner).start()
+
+    sums = column_sums[...]
     weight = weight_ref[...].astype(f32)
-    shift_sum = jnp.dot(
-        sums, weight, preferred_element_type=f32, precision=lax.Precision.HIGHEST
-    )[0:1]
+    shift_sum = jnp.dot(sums, weight, preferred_element_type=f32, precision=lax.Precision.HIGHEST)[0:1]
     gain_sum = jnp.sum(weight * q_wide[...], axis=0, keepdims=True)
     v_now[0] = vectors_ref[...]
     v_now[0, 0:1, :] = (gain_sum - shift * shift_sum) / gain
@@ -411,27 +420,8 @@
 
     q_core = start_dp(q_all.at[pl.ds((1 - core) * 4, 4)], q_got_core, 0)
     v_copy = vector_stage(0)
-
-    second_a.wait_recv()
-    second_b.wait_recv()
-    pairs = shards // 2
-    for at in range(pairs):
-        pieces[at] = rounded_sum(a_sum[y_bit, at], a_second[at])
-        pieces[pairs + at] = rounded_sum(b_sum[x_bit, at], b_second[at])
-    for bit in range(PIECE_BITS, dp_bits):
-        extra = start_dp(pieces, pieces_more.at[bit - PIECE_BITS], bit, False)
-        extra.wait_recv()
-        extra.wait_send()
-        add_into(pieces, pieces, pieces_more.at[bit - PIECE_BITS])
-    z_copies = []
-    for way in range(1, shards):
-        target = lax.rem(here + way, shards)
-        copy = copy_to(pieces.at[target], z_got.at[way - 1], next(slots), tensor=target)
-        copy.start()
-        z_copies.append(copy)
-    pending.extend(z_copies)
-    end_sends()
-
+    hop(1, 0, False)
+    hop(2, 0, True)
     q_core.wait_recv()
     for at in range(4):
         q_half[at] = rounded_sum(q_all[core * 4 + at], q_got_core[at])
@@ -439,7 +429,6 @@
     v_copy.wait_recv()
     v_now[1] = v_now[0] + v_got[0]
     v_copy = vector_stage(1)
-    hop(1, 0)
     q_x.wait_recv()
     for at in range(2):
         q_quarter[at] = rounded_sum(q_half[x_bit * 2 + at], q_got_x[at])
@@ -475,8 +464,8 @@
     q_back.wait_recv()
     q_back = start_dp(qkv_out.at[pl.ds(core * 4, 4)], qkv_out.at[pl.ds(core * 4, 4)], 0)
 
-    for copy in z_copies:
-        copy.wait_recv()
+    for way in range(1, shards):
+        piece_copy(way).wait_recv()
     total = pieces[here].astype(f32)
     for way in range(1, shards):
         total = total + z_got[way - 1].astype(f32)
@@ -497,10 +486,13 @@
         for at in range(2)
     ]
     for moved in range(2, last):
-        hop(moved, 0)
+        hop(moved, 0, False)
+        if moved > 2:
+            hop(moved, 0, True)
     for nth in range(1, last):
         for moved in range(1, last):
-            hop(moved, nth)
+            hop(moved, nth, True)
+            hop(moved, nth, False)
     back_a.wait_recv()
     for copy in back_c:
         copy.wait_recv()
@@ -520,10 +512,13 @@
         def _():
             if owner > 0:
                 to_right(owner).wait_recv()
-                add_arrived(owner, from_left)
+                add_arrived(owner, owner)
             if owner < last:
-                to_left(owner).wait_recv()
-                add_arrived(owner, from_right)
+                to_left(owner, owner).wait_recv()
+                add_arrived(owner, shards)
+
+    load(2).wait()
+    load(3).wait()
 
     def close(at, carry):
         rows = pl.ds(pl.multiple_of(at * (block // 4), 16), block // 4)
@@ -545,6 +540,10 @@
     back_core.wait_recv()
     for copy in pending:
         copy.wait_send()
+    for at in range(2):
+        second(at).wait_send()
+    for way in range(1, shards):
+        piece_copy(way).wait_send()
     for owner in range(shards):
 
         @pl.when(here < owner)
@@ -556,22 +555,22 @@
             to_left(owner).wait_send()
 
 
-def finish(shards, members, grads, rows, weight, gain, shift, vectors, tokens, grad_hidden, a_keep, a_got, b_keep, b_got):
+def back(shards, members, heads_in, pair_in, weight, gain, shift, vectors, rows, tokens, grad_hidden, exchanged):
     dp_bits = members.bit_length() - 1
     assert members == 1 << dp_bits and dp_bits >= PIECE_BITS
     f32, bf16 = jnp.float32, jnp.bfloat16
-    seq_len, columns = grads.shape
-    block, width = tokens.shape
-    piece_rows = a_keep.shape[2]
+    heads, seq_len, _ = heads_in[0].shape
+    columns, width = weight.shape
+    block = tokens.shape[0]
+    quarter = exchanged[0].shape
+    piece_rows = quarter[2]
     count = columns // PIECES
     more = max(1, dp_bits - PIECE_BITS)
-    copies = 16 + 2 * shards + 2 * (shards - 1) + 3 * dp_bits
+    copies = 20 + 2 * shards + 2 * (shards - 1) + 4 * dp_bits
     vm = pltpu.VMEM
     return pl.pallas_call(
-        partial(finish_kernel, shards, dp_bits),
-        in_specs=[
-            pl.BlockSpec(memory_space=pl.ANY if at in (1, 6, 7) else vm) for at in range(12)
-        ],
+        partial(back_kernel, shards, dp_bits),
+        in_specs=[pl.BlockSpec(memory_space=vm)] * 11 + [pl.BlockSpec(memory_space=pl.ANY)] * 7,
         out_specs=[pl.BlockSpec(memory_space=vm)] * 4,
         out_shape=[
             jax.ShapeDtypeStruct((block, width), f32),
@@ -580,13 +579,20 @@
             jax.ShapeDtypeStruct((PIECES, piece_rows, width), bf16),
         ],
         scratch_shapes=[
-            vm((seq_len, width), bf16),
+            vm((heads, seq_len, LANES), bf16),
+            vm((heads, seq_len, LANES), f32),
+            vm((heads, seq_len, LANES), f32),
+            vm((heads, seq_len, LANES), f32),
+            vm((heads, block, block), bf16),
+            vm((heads, block, block), bf16),
+            vm((block, columns), bf16),
+            vm((block, width), bf16),
             vm((block, width), bf16),
             vm((block, width), f32),
             vm((shards, block, width), bf16),
-            vm((shards, block, width), bf16),
-            vm((shards, block, width), bf16),
+            vm((shards + 1, block, width), bf16),
             vm((columns, width), f32),
+            vm((8, columns), f32),
             vm((PIECES, count, width), bf16),
             vm((4, count, width), bf16),
             vm((2, count, width), bf16),
@@ -597,25 +603,27 @@
             vm((dp_bits + 1,) + vectors.shape, f32),
             vm((dp_bits,) + vectors.shape, f32),
             vm((shards,) + vectors.shape, f32),
-            vm(a_keep.shape, bf16),
-            vm(b_keep.shape, bf16),
-            vm(a_keep.shape[1:], bf16),
-            vm(b_keep.shape[1:], bf16),
+            vm(quarter, bf16),
+            vm(quarter, bf16),
+            vm(quarter, bf16),
+            vm(quarter, bf16),
+            vm(quarter[1:], bf16),
+            vm(quarter[1:], bf16),
             vm((shards, piece_rows, width), bf16),
             vm((more, shards, piece_rows, width), bf16),
             vm((shards - 1, piece_rows, width), bf16),
             pltpu.SemaphoreType.DMA((copies,)),
             pltpu.SemaphoreType.DMA((copies,)),
-            pltpu.SemaphoreType.DMA((3,)),
+            pltpu.SemaphoreType.DMA((5,)),
         ],
         compiler_params=pltpu.CompilerParams(
-            collective_id=1, has_side_effects=True, vmem_limit_bytes=64 * 1024 * 1024 - 2048 * 1024
+            collective_id=1, has_side_effects=True, vmem_limit_bytes=67043328
         ),
-        name="finish",
+        name="back",
         cost_estimate=pl.CostEstimate(
-            flops=4 * seq_len * columns * width, transcendentals=0, bytes_accessed=40 * block * width
+            flops=10 * heads * seq_len * seq_len * LANES, transcendentals=0, bytes_accessed=40 * block * width
         ),
-    )(grads, rows, weight, gain, shift, vectors, tokens, grad_hidden, a_keep, a_got, b_keep, b_got)
+    )(*heads_in, *pair_in, weight, gain, shift, vectors, rows, tokens, grad_hidden, *exchanged)
 
 
 def unpack_kernel(qkv_ref, weights_ref, totals_ref, fc1_out, fc2_out, proj_out, qkv_out, fc1_bias_out, *vector_outs):
@@ -658,7 +666,6 @@
 def start_kernel(
     shards,
     dp_bits,
-    visit_block,
     tokens_ref,
     ids_ref,
     gain_ref,
@@ -679,7 +686,6 @@
     singles_here,
     weights_out,
     bias_out,
-    bounds_out,
     blocks,
     normed_all,
     queries,
@@ -809,15 +815,6 @@
     ones_lane = (lane >= HEAD_DIM + 8) & (lane < HEAD_DIM + 11)
     q_extra[...] = jnp.where(segment_lane, (matched - 1.0) * large, 0.0).astype(bf16)
     k_extra[...] = jnp.where(ones_lane, 1.0, matched).astype(bf16)
-    ids = ids_ref[...]
-    groups = bounds_out.shape[1]
-    for group in range(groups):
-        first = group * (seq_len // groups)
-        last_row = first + seq_len // groups - 1
-        before = jnp.sum(jnp.where(ids < ids_ref[:, first : first + 1], 1.0, 0.0))
-        within = jnp.sum(jnp.where(ids <= ids_ref[:, last_row : last_row + 1], 1.0, 0.0))
-        bounds_out[0, group] = before.astype(jnp.int32) // visit_block
-        bounds_out[1, group] = (within.astype(jnp.int32) + visit_block - 1) // visit_block
     low_half = lax.broadcasted_iota(jnp.int32, (block, LANES), 1) < HEAD_DIM
     v_lane = lax.broadcasted_iota(jnp.int32, (block, LANES), 1)
     v_extra = jnp.where((v_lane >= HEAD_DIM) & (v_lane < HEAD_DIM + 3), 1.0, 0.0).astype(bf16)
@@ -1047,7 +1044,7 @@
                         hop_copy(name, owner, False, False).wait_send()
 
 
-def start(shards, members, visits, tokens, ids, gain, shift, qkv, qv_bias, fc1, fc2, proj, fc1_bias):
+def start(shards, members, tokens, ids, gain, shift, qkv, qv_bias, fc1, fc2, proj, fc1_bias):
     dp_bits = members.bit_length() - 1
     assert members == 1 << dp_bits and dp_bits >= PIECE_BITS and shards >= 3
     f32, bf16 = jnp.float32, jnp.bfloat16
@@ -1061,11 +1058,11 @@
     anywhere = pl.BlockSpec(memory_space=pl.ANY)
     head_rows = jax.ShapeDtypeStruct((heads, seq_len, LANES), bf16)
     return pl.pallas_call(
-        partial(start_kernel, shards, dp_bits, visits[1]),
+        partial(start_kernel, shards, dp_bits),
         in_specs=[on_chip] * 6 + [anywhere] * 2 + [on_chip] * 2,
         out_specs=[anywhere] * 4
         + [on_chip] * 4
-        + [anywhere, on_chip, pl.BlockSpec(memory_space=pltpu.SMEM)],
+        + [anywhere, on_chip],
         out_shape=[
             jax.ShapeDtypeStruct((seq_len, width), bf16),
             head_rows,
@@ -1077,7 +1074,6 @@
             jax.ShapeDtypeStruct((shards, block // 2, LANES), bf16),
             jax.ShapeDtypeStruct((PIECES, shards, rows, width), bf16),
             jax.ShapeDtypeStruct((shards, 1, width), f32),
-            jax.ShapeDtypeStruct((2, visits[0]), jnp.int32),
         ],
         scratch_shapes=[
             vm((shards, block, width), bf16),
@@ -1479,12 +1475,10 @@
     ids = segment_ids[0]
     here = lax.axis_index("tensor")
 
-    visits = (shards, seq_len // 6)
     turned = qkv_weight.transpose(0, 2, 1)
-    full_one, queries, keys, values, pairs, singles, pairs_here, singles_here, gathered, fc1_bias_full, bounds = start(
+    full_one, queries, keys, values, pairs, singles, pairs_here, singles_here, gathered, fc1_bias_full = start(
         shards,
         members,
-        visits,
         tokens,
         segment_ids,
         ln1_gain,
@@ -1503,26 +1497,19 @@
     pair_grads = pair_grads.reshape(seq_len, LANES)
     single_grads = single_grads.reshape(seq_len // 2, LANES)
 
-    def swap(value, bit):
-        return lax.ppermute(value, "dp", [(j, j ^ (1 << bit)) for j in range(members)])
-
-    a_got, b_got = swap(a_away, 1), swap(b_away, 2)
-    grad_heads = attend_back(bounds, queries, keys, values, pairs, singles, pair_grads, single_grads, visits[1])
-    grad_tokens, totals, qkv_pieces, weight_pieces = finish(
+    grad_tokens, totals, qkv_pieces, weight_pieces = back(
         shards,
         members,
-        grad_heads,
-        full_one,
+        (queries, keys, values),
+        (pairs, singles, pair_grads, single_grads),
         turned.reshape(3 * head_columns, width),
         ln1_gain,
         ln1_bias,
         vectors,
+        full_one,
         tokens,
         grad_hidden,
-        a_keep,
-        a_got,
-        b_keep,
-        b_got,
+        (a_keep, a_away, b_keep, b_away),
     )
     fc1_grad, fc2_grad, proj_grad, qkv_grad, fc1_bias_grad, *sums = unpack(
         qkv_pieces, weight_pieces, totals, width // PIECES, head_columns // PIECES

time: 333 us -> 324 us (0.973)
  Pallas kernels: 321 us -> 317 us
    pallas_call x3 -> x2, Pallas kernels: 248 us -> 243 us  [the longest x1 133 us: back(): pl.pallas_call(partial(back_kernel, shards, dp_bits), in_specs=[pl.BlockS...]
  transfers between devices with their start and end apart: 2 -> 0, of which waited for: 0 -> 0; matrix products, arithmetic and copies ran while one was open for 0% -> 0% of each run, Pallas kernels for 12% -> 0%
where the time goes in v4:
time: 324 us; the launch traced here: 322 us
  Pallas kernels  317 us (98%)
  local copies, waits for them, and re-layouts  3.78 us (1%)
    pallas_call x1, Pallas kernels, back(): pl.pallas_call(partial(back_kernel, shards, dp_bits), in_specs=[pl.BlockS...  133 us
    pallas_call x1, Pallas kernels, start(): pl.pallas_call(partial(start_kernel, shards, dp_bits), in_specs=[on_chip]...  110 us
    pallas_call x1, Pallas kernels, middle(): pl.pallas_call(partial(middle_kernel, shards, dp_bits), in_specs=[on_chip...  66.7 us
    pallas_call x1, Pallas kernels, unpack(): pl.pallas_call(unpack_kernel, grid=(PIECES,), in_specs=[pl.BlockSpec((1,...  7.16 us

profile of v4, /device:TPU:16, one launch (start us, length us, event | category | flops | bytes accessed | tf_op | source)
XLA Modules:
  0.0 321.8 jit_solution(14647673561513690428)
XLA Ops:
  0.6 110.1 %start.1 = (bf16[2304,768]{1,0:T(8,128)(2,1)}, bf16[3,2304,128]{2,1,0:T(8,128)(2,1)}, bf16[3,2304,128]{2,1,0:T(8,128)(2,1)}, bf16[3,2304,128]{2,1,0:T(8,128)(2,1...) custom-call(bf16[576,768]{1,0:T(8,128)(2,1)} %tokens_ref.5, ...), custom_call_target="tpu_custom_call" | custom-call | flops 2038431744 | bytes 17694720 | tf_op jit(solution)/shard_map/start/pallas_call | solution.py:1060
  110.8 66.7 %middle.1 = (bf16[576,768]{1,0:T(8,128)(2,1)}, f32[576,768]{1,0:T(8,128)}, bf16[4,576,128]{2,1,0:T(8,128)(2,1)}, bf16[4,288,128]{2,1,0:T(8,128)(2,1)}, f32[16,76...) custom-call(bf16[4,576,128]{2,1,0:T(8,128)(2,1)} %get-tuple-element., ...), custom_call_target="tpu_custom_call" | custom-call | flops 16307453952 | bytes 17694720 | tf_op jit(solution)/shard_map/middle/pallas_call | solution.py:1399
  177.5 132.8 %back.1 = (f32[576,768]{1,0:T(8,128)}, f32[16,768]{1,0:T(8,128)}, bf16[8,72,768]{2,1,0:T(8,128)(2,1)}, bf16[8,224,768]{2,1,0:T(8,128)(2,1)}) custom-call(bf16[3,2304,128]{2,1,0:T(8,128)(2,1)} %get-tuple-element.57.q_ref, bf16[3,2304,128]{2,1,0:T(8,128)(2,1)} %get-tuple-element.58.k_ref, bf16[3,2304,128]{2,1,0:T(8,128)(2,1)} %get-tuple-element.59.v_ref, ...), custom_call_target="tpu_custom_call" | custom-call | flops 20384317440 | bytes 17694720 | tf_op jit(solution)/shard_map/back/pallas_call | solution.py:571
  310.3 0.8 constant_dynamic-slice_fusion
  311.1 0.6 pad_maximum_fusion
  311.6 0.0 copy-start.1
  311.7 7.2 %unpack.1 = (f32[768,768]{1,0:T(8,128)}, f32[768,768]{1,0:T(8,128)}, f32[192,768]{1,0:T(8,128)}, f32[576,768]{1,0:T(8,128)}, f32[768]{0:T(1024)}, /*index=5*/f32...) custom-call(bf16[8,72,768]{2,1,0:T(8,128)(2,1)} %get-tuple-element.7, ...), custom_call_target="tpu_custom_call" | custom-call | tf_op jit(solution)/shard_map/unpack/pallas_call | solution.py:651
  318.8 0.0 copy-start
  318.8 0.0 copy-done.1
  318.8 0.9 copy.35
  319.8 0.9 copy-done
  320.6 1.2 copy.36
Async XLA Ops:
  311.6 7.2 %copy-start.1 = (bf16[576,768]{1,0:T(8,128)(2,1)S(1)}, bf16[576,768]{1,0:T(8,128)(2,1)}, u32[]{:S(2)}) copy-start(bf16[576,768]{1,0:T(8,128)(2,1)} %get-tuple-element.106) | copy-start | bytes 2654212
  318.8 1.8 copy-start

commit v5 on v4

--- a/solution.py
+++ b/solution.py
@@ -85,6 +85,7 @@
     a_away,
     b_keep,
     b_away,
+    early,
     tokens_out,
     vectors_out,
     qkv_out,
@@ -120,8 +121,11 @@
     a_second,
     b_second,
     pieces,
+    early_own,
     pieces_more,
+    early_more,
     z_got,
+    early_got,
     send,
     recv,
     local,
@@ -153,14 +157,20 @@
         return copy
 
     def load(at):
-        source, landing = ((a_keep, a_sum), (b_keep, b_sum), (tokens_ref, tokens_own), (hidden_ref, hidden_own))[at]
+        source, landing = (
+            (a_keep, a_sum),
+            (b_keep, b_sum),
+            (tokens_ref, tokens_own),
+            (hidden_ref, hidden_own),
+            (early, early_own),
+        )[at]
         return pltpu.make_async_copy(source, landing, local.at[at])
 
     def load_rows(owner):
         rows = pl.ds(pl.multiple_of(owner * block, 16), block)
-        return pltpu.make_async_copy(rows_ref.at[rows], rows_own, local.at[4])
-
-    for at in range(4):
+        return pltpu.make_async_copy(rows_ref.at[rows], rows_own, local.at[5])
+
+    for at in range(5):
         load(at).start()
     load_rows(last).start()
     greet(dp_bits, shards)
@@ -174,13 +184,34 @@
             return copy_to(b_sum.at[1 - x_bit], b_second, second_slots[1], dp=partner_of(member, 1))
         return copy_to(a_sum.at[1 - y_bit], a_second, second_slots[0], dp=partner_of(member, 2))
 
-    z_slots = [next(slots) for _ in range(1, shards)]
-
-    def piece_copy(way):
+    z_slots = [[next(slots) for _ in range(1, shards)] for _ in range(2)]
+
+    def piece_copy(way, first=False):
         target = lax.rem(here + way, shards)
-        return copy_to(pieces.at[target], z_got.at[way - 1], z_slots[way - 1], tensor=target)
-
-    more_slots = [next(slots) for _ in range(PIECE_BITS, dp_bits)]
+        source, landing = (early_own, early_got) if first else (pieces, z_got)
+        return copy_to(source.at[target], landing.at[way - 1], z_slots[first][way - 1], tensor=target)
+
+    more_slots = [[next(slots) for _ in range(PIECE_BITS, dp_bits)] for _ in range(2)]
+
+    def send_pieces(first):
+        source, landing = (early_own, early_more) if first else (pieces, pieces_more)
+        for bit in range(PIECE_BITS, dp_bits):
+            at = bit - PIECE_BITS
+            extra = copy_to(source, landing.at[at], more_slots[first][at], dp=partner_of(member, bit))
+            extra.start()
+            extra.wait_recv()
+            extra.wait_send()
+
+            def step(owner, carry):
+                source[owner] = rounded_sum(source[owner], landing[at, owner])
+                return carry
+
+            lax.fori_loop(0, shards, step, 0)
+        for way in range(1, shards):
+            piece_copy(way, first).start()
+
+    load(4).wait()
+    send_pieces(True)
 
     def sum_pairs(out, right):
         def step(at, carry):
@@ -207,20 +238,7 @@
         for at in range(split):
             pieces[at] = rounded_sum(a_sum[y_bit, at], a_second[at])
             pieces[split + at] = rounded_sum(b_sum[x_bit, at], b_second[at])
-        for bit in range(PIECE_BITS, dp_bits):
-            at = bit - PIECE_BITS
-            extra = copy_to(pieces, pieces_more.at[at], more_slots[at], dp=partner_of(member, bit))
-            extra.start()
-            extra.wait_recv()
-            extra.wait_send()
-
-            def step(owner, carry):
-                pieces[owner] = rounded_sum(pieces[owner], pieces_more[at, owner])
-                return carry
-
-            lax.fori_loop(0, shards, step, 0)
-        for way in range(1, shards):
-            piece_copy(way).start()
+        send_pieces(False)
 
     right_slots = [next(slots) for _ in range(shards)]
     left_slots = [next(slots) for _ in range(shards)]
@@ -370,9 +388,9 @@
         order[closing.index(at) + 1] if at in closing and at != closing[-1] else -1 for at in range(total_visits)
     ]
     events = {
-        total_visits // 2: second_exchange,
+        closing[0] - 1: second_exchange,
+        closing[0] + 2: shard_exchange,
         closing[1] + 1: lambda: hop(1, 0, True),
-        closing[2]: shard_exchange,
     }
     assert len(events) == 3 and shards >= 4
 
@@ -464,12 +482,17 @@
     q_back.wait_recv()
     q_back = start_dp(qkv_out.at[pl.ds(core * 4, 4)], qkv_out.at[pl.ds(core * 4, 4)], 0)
 
-    for way in range(1, shards):
-        piece_copy(way).wait_recv()
-    total = pieces[here].astype(f32)
-    for way in range(1, shards):
-        total = total + z_got[way - 1].astype(f32)
-    weights_out[own_piece] = total.astype(bf16)
+    split_row = early_own.shape[1]
+    for first, source, landing, rows in (
+        (True, early_own, early_got, slice(0, split_row)),
+        (False, pieces, z_got, slice(split_row, 2 * half_rows)),
+    ):
+        for way in range(1, shards):
+            piece_copy(way, first).wait_recv()
+        total = source[here].astype(f32)
+        for way in range(1, shards):
+            total = total + landing[way - 1].astype(f32)
+        weights_out[own_piece, rows, :] = total.astype(bf16)
 
     def own_half(low, *index):
         rows = pl.ds(0 if low else half_rows, half_rows)
@@ -543,6 +566,7 @@
     for at in range(2):
         second(at).wait_send()
     for way in range(1, shards):
+        piece_copy(way, True).wait_send()
         piece_copy(way).wait_send()
     for owner in range(shards):
 
@@ -563,20 +587,21 @@
     columns, width = weight.shape
     block = tokens.shape[0]
     quarter = exchanged[0].shape
-    piece_rows = quarter[2]
+    early_rows = exchanged[4].shape[1]
+    late_rows = quarter[2]
     count = columns // PIECES
     more = max(1, dp_bits - PIECE_BITS)
-    copies = 20 + 2 * shards + 2 * (shards - 1) + 4 * dp_bits
+    copies = 20 + 2 * shards + 3 * (shards - 1) + 5 * dp_bits
     vm = pltpu.VMEM
     return pl.pallas_call(
         partial(back_kernel, shards, dp_bits),
-        in_specs=[pl.BlockSpec(memory_space=vm)] * 11 + [pl.BlockSpec(memory_space=pl.ANY)] * 7,
+        in_specs=[pl.BlockSpec(memory_space=vm)] * 11 + [pl.BlockSpec(memory_space=pl.ANY)] * 8,
         out_specs=[pl.BlockSpec(memory_space=vm)] * 4,
         out_shape=[
             jax.ShapeDtypeStruct((block, width), f32),
             jax.ShapeDtypeStruct(vectors.shape, f32),
             jax.ShapeDtypeStruct((PIECES, count, width), bf16),
-            jax.ShapeDtypeStruct((PIECES, piece_rows, width), bf16),
+            jax.ShapeDtypeStruct((PIECES, early_rows + late_rows, width), bf16),
         ],
         scratch_shapes=[
             vm((heads, seq_len, LANES), bf16),
@@ -609,12 +634,15 @@
             vm(quarter, bf16),
             vm(quarter[1:], bf16),
             vm(quarter[1:], bf16),
-            vm((shards, piece_rows, width), bf16),
-            vm((more, shards, piece_rows, width), bf16),
-            vm((shards - 1, piece_rows, width), bf16),
+            vm((shards, late_rows, width), bf16),
+            vm((shards, early_rows, width), bf16),
+            vm((more, shards, late_rows, width), bf16),
+            vm((more, shards, early_rows, width), bf16),
+            vm((shards - 1, late_rows, width), bf16),
+            vm((shards - 1, early_rows, width), bf16),
             pltpu.SemaphoreType.DMA((copies,)),
             pltpu.SemaphoreType.DMA((copies,)),
-            pltpu.SemaphoreType.DMA((5,)),
+            pltpu.SemaphoreType.DMA((6,)),
         ],
         compiler_params=pltpu.CompilerParams(
             collective_id=1, has_side_effects=True, vmem_limit_bytes=67043328
@@ -628,8 +656,8 @@
 
 def unpack_kernel(qkv_ref, weights_ref, totals_ref, fc1_out, fc2_out, proj_out, qkv_out, fc1_bias_out, *vector_outs):
     fc_rows, proj_rows = fc1_out.shape[0], proj_out.shape[0]
-    fc1_out[...] = weights_ref[0, :fc_rows].astype(jnp.float32)
-    fc2_out[...] = weights_ref[0, fc_rows : 2 * fc_rows].astype(jnp.float32)
+    fc2_out[...] = weights_ref[0, :fc_rows].astype(jnp.float32)
+    fc1_out[...] = weights_ref[0, fc_rows : 2 * fc_rows].astype(jnp.float32)
     proj_out[...] = weights_ref[0, 2 * fc_rows : 2 * fc_rows + proj_rows].astype(jnp.float32)
     qkv_out[...] = qkv_ref[0].astype(jnp.float32)
 
@@ -730,7 +758,7 @@
     fc1_rows, fc2_rows, proj_rows = (ref.shape[0] // PIECES for ref in (fc1_ref, fc2_ref, proj_ref))
     loads = []
     for at, (ref, first, count) in enumerate(
-        ((fc1_ref, 0, fc1_rows), (fc2_ref, fc1_rows, fc2_rows))
+        ((fc2_ref, 0, fc2_rows), (fc1_ref, fc2_rows, fc1_rows))
     ):
         rows = pl.ds(pl.multiple_of(own_piece * count, 16), count)
         loads.append(pltpu.make_async_copy(ref.at[rows], own.at[first : first + count], local.at[at]))
@@ -1131,6 +1159,7 @@
     a_away,
     b_keep,
     b_away,
+    early_out,
     weights,
     attended,
     proj,
@@ -1146,7 +1175,12 @@
     grad_branch,
     pair_grads,
     single_grads,
+    got_early,
     got,
+    a_got,
+    b_got,
+    a_second,
+    b_second,
     send,
     recv,
     local,
@@ -1181,10 +1215,10 @@
         load.wait()
 
     def fc1_of(owner):
+        return weights[:, owner, fc_rows:proj_first, :].reshape(width, width)
+
+    def fc2_of(owner):
         return weights[:, owner, :fc_rows, :].reshape(width, width)
-
-    def fc2_of(owner):
-        return weights[:, owner, fc_rows:proj_first, :].reshape(width, width)
 
     def proj_of(owner):
         return weights[:, owner, proj_first : proj_first + proj_rows, :].reshape(columns, width)
@@ -1271,6 +1305,80 @@
 
     scale_two_sum, fc2_bias_sum = each_chunk(turn, (empty, empty))
 
+    split = shards // 2
+
+    def slot_row():
+        return [next(slots) for _ in range(shards)]
+
+    early_slots, late_slots = slot_row(), slot_row()
+
+    def core_copy(owner, early):
+        rows = pl.ds(0, fc_rows) if early else pl.ds(fc_rows, weights.shape[2] - fc_rows)
+        base = (early_slots if early else late_slots)[0]
+        return pltpu.make_async_remote_copy(
+            src_ref=weights.at[pl.ds((1 - core) * half, half), owner, rows],
+            dst_ref=(got_early if early else got).at[:, owner],
+            send_sem=send.at[base + owner],
+            recv_sem=recv.at[base + owner],
+            device_id={"dp": partner_of(member, 0)},
+            device_id_type=MESH,
+        )
+
+    piece_rows = pl.ds(0, fc_rows)
+    own = core * half
+    side_slots = [next(slots) for _ in range(5)]
+
+    def side_copies(stage):
+        first_half, second_half = pl.ds(0, split), pl.ds(split, shards - split)
+        if stage == 0:
+            moves = [(weights.at[pl.ds(own + (1 - x_bit) * 2, 2), first_half, piece_rows], a_got, 1)]
+            moves += [
+                (weights.at[own + 2 * x + 1 - y_bit, second_half, piece_rows], b_got.at[x], 2) for x in range(2)
+            ]
+        else:
+            moves = [
+                (weights.at[own + 2 * x_bit + 1 - y_bit, first_half, piece_rows], a_second, 2),
+                (weights.at[own + 2 * (1 - x_bit) + y_bit, second_half, piece_rows], b_second, 1),
+            ]
+        return [
+            copy_to(source, landing, side_slots[3 * stage + at], dp=partner_of(member, bit))
+            for at, (source, landing, bit) in enumerate(moves)
+        ]
+
+    def grow_piece(piece, owner, other):
+        weights[piece, owner, piece_rows, :] = rounded_sum(weights[piece, owner, piece_rows, :], other)
+
+    def early_pairs():
+        for owner in range(shards):
+            core_copy(owner, True).wait_recv()
+
+        def step(at, carry):
+            piece, owner = at // shards, lax.rem(at, shards)
+            grow_piece(own + piece, owner, got_early[piece, owner])
+            return carry
+
+        lax.fori_loop(0, half * shards, step, 0)
+        for copy in side_copies(0):
+            copy.start()
+
+    def early_sides():
+        for copy in side_copies(0):
+            copy.wait_recv()
+        for owner in range(split):
+            for at in range(2):
+                grow_piece(own + 2 * x_bit + at, owner, a_got[at, owner])
+                grow_piece(own + 2 * at + y_bit, split + owner, b_got[at, owner])
+        for copy in side_copies(1):
+            copy.start()
+
+    def early_end():
+        for copy in side_copies(1):
+            copy.wait_recv()
+        mine = own + 2 * x_bit + y_bit
+        for owner in range(split):
+            early_out[owner] = rounded_sum(weights[mine, owner, piece_rows, :], a_second[owner])
+            early_out[split + owner] = rounded_sum(weights[mine, split + owner, piece_rows, :], b_second[owner])
+
     def backward(owner, carry):
         wide[:block, :] = times_transposed(grad_mlp[...], fc2_of(owner))
 
@@ -1283,9 +1391,13 @@
         vectors_out[pl.ds(8 + owner, 1), :] = each_chunk(slopes, empty)
         product = times_transposed(grad_pre[owner], fc1_of(owner))
         total[...] = jnp.where(owner == 0, product, total[...] + product)
+        product = contract_rows(active[owner], grad_mlp[...]).astype(bf16)
+        weights[:, owner, :fc_rows, :] = product.reshape(PIECES, fc_rows, width)
+        core_copy(owner, True).start()
         return carry
 
     lax.fori_loop(0, shards, backward, 0)
+    early_pairs()
 
     def leave(at, sums):
         rows = chunk(at)
@@ -1332,18 +1444,6 @@
             back.append(copy)
         out[here] = source[here]
 
-    first_slot = next(slots)
-
-    def core_copy(owner):
-        return pltpu.make_async_remote_copy(
-            src_ref=weights.at[pl.ds((1 - core) * half, half), owner],
-            dst_ref=got.at[:, owner],
-            send_sem=send.at[first_slot + owner],
-            recv_sem=recv.at[first_slot + owner],
-            device_id={"dp": partner_of(member, 0)},
-            device_id_type=MESH,
-        )
-
     wide[...] = contract_rows(attended[:, :], grad_branch[...])
     for owner in range(shards):
         for piece in range(PIECES):
@@ -1356,35 +1456,38 @@
                     weights[piece, owner, to, :] = wide[rows, :].astype(bf16)
 
     def weight_grads(owner, carry):
-        for left, right, first, count in (
-            (normed[...], grad_pre[owner], 0, fc_rows),
-            (active[owner], grad_mlp[...], fc_rows, fc_rows),
-        ):
-            product = contract_rows(left, right).astype(bf16)
-            weights[:, owner, first : first + count, :] = product.reshape(PIECES, count, width)
-        core_copy(owner).start()
+        product = contract_rows(normed[...], grad_pre[owner]).astype(bf16)
+        weights[:, owner, fc_rows:proj_first, :] = product.reshape(PIECES, fc_rows, width)
+        core_copy(owner, False).start()
         return carry
 
     lax.fori_loop(0, shards, weight_grads, 0)
-    split = shards // 2
+    early_sides()
     for owner in range(shards):
-        core_copy(owner).wait_recv()
-        if owner < split:
+        core_copy(owner, False).wait_recv()
+        for x in range(2):
             for y in range(2):
-                for out, x in ((a_keep, x_bit), (a_away, 1 - x_bit)):
-                    out[y, owner] = rounded_sum(weights[core * half + x * 2 + y, owner], got[x * 2 + y, owner])
-        else:
-            for x in range(2):
-                for out, y in ((b_keep, y_bit), (b_away, 1 - y_bit)):
-                    out[x, owner - split] = rounded_sum(
-                        weights[core * half + x * 2 + y, owner], got[x * 2 + y, owner]
-                    )
+                piece = x * 2 + y
+                if owner < split:
+                    moves = [(out, y, owner, at == x) for out, at in ((a_keep, x_bit), (a_away, 1 - x_bit))]
+                else:
+                    moves = [(out, x, owner - split, at == y) for out, at in ((b_keep, y_bit), (b_away, 1 - y_bit))]
+                for out, first, second, wanted in moves:
+
+                    @pl.when(wanted)
+                    def _():
+                        out[first, second] = rounded_sum(
+                            weights[own + piece, owner, fc_rows:, :], got[piece, owner]
+                        )
+
+    early_end()
     for copy in back:
         copy.wait_recv()
-    for copy in back:
+    for copy in back + side_copies(0) + side_copies(1):
         copy.wait_send()
     for owner in range(shards):
-        core_copy(owner).wait_send()
+        core_copy(owner, True).wait_send()
+        core_copy(owner, False).wait_send()
 
 
 def middle(shards, members, pairs, singles, weights, fc1_bias, vectors, tokens, cotangent):
@@ -1394,12 +1497,13 @@
     rows = weights.shape[2]
     vm = pltpu.VMEM
     on_chip = pl.BlockSpec(memory_space=vm)
-    quarter = jax.ShapeDtypeStruct((2, shards // 2, rows, width), bf16)
-    copies = 2 * (shards - 1) + shards
+    fc_rows = width // PIECES
+    quarter = jax.ShapeDtypeStruct((2, shards // 2, rows - fc_rows, width), bf16)
+    copies = 2 * (shards - 1) + 2 * shards + 5
     return pl.pallas_call(
         partial(middle_kernel, shards, dp_bits),
         in_specs=[on_chip, on_chip, pl.BlockSpec(memory_space=pl.ANY)] + [on_chip] * 9,
-        out_specs=[on_chip] * 9,
+        out_specs=[on_chip] * 10,
         out_shape=[
             jax.ShapeDtypeStruct((block, width), bf16),
             jax.ShapeDtypeStruct((block, width), f32),
@@ -1410,6 +1514,7 @@
             quarter,
             quarter,
             quarter,
+            jax.ShapeDtypeStruct((shards, fc_rows, width), bf16),
         ],
         scratch_shapes=[
             vm(weights.shape, bf16),
@@ -1427,7 +1532,12 @@
             vm((block, width), bf16),
             vm((shards, block, LANES), bf16),
             vm((shards, block // 2, LANES), bf16),
-            vm((PIECES // 2, shards, rows, width), bf16),
+            vm((PIECES // 2, shards, fc_rows, width), bf16),
+            vm((PIECES // 2, shards, rows - fc_rows, width), bf16),
+            vm((2, shards // 2, fc_rows, width), bf16),
+            vm((2, shards // 2, fc_rows, width), bf16),
+            vm((shards // 2, fc_rows, width), bf16),
+            vm((shards // 2, fc_rows, width), bf16),
             pltpu.SemaphoreType.DMA((copies,)),
             pltpu.SemaphoreType.DMA((copies,)),
             pltpu.SemaphoreType.DMA((shards,)),
@@ -1491,7 +1601,7 @@
         fc1_bias,
     )
     params = (proj_bias, scale_one, ln2_gain, ln2_bias, fc2_bias, scale_two)
-    block_out, grad_hidden, pair_grads, single_grads, vectors, a_keep, a_away, b_keep, b_away = middle(
+    block_out, grad_hidden, pair_grads, single_grads, vectors, *exchanged = middle(
         shards, members, pairs_here, singles_here, gathered, fc1_bias_full, params, tokens, cotangent
     )
     pair_grads = pair_grads.reshape(seq_len, LANES)
@@ -1509,7 +1619,7 @@
         full_one,
         tokens,
         grad_hidden,
-        (a_keep, a_away, b_keep, b_away),
+        exchanged,
     )
     fc1_grad, fc2_grad, proj_grad, qkv_grad, fc1_bias_grad, *sums = unpack(
         qkv_pieces, weight_pieces, totals, width // PIECES, head_columns // PIECES

time: 324 us -> 331 us (1.022)
  Pallas kernels: 317 us -> 321 us
    pallas_call x1, Pallas kernels: 66.7 us -> 73.2 us  [middle(): pl.pallas_call(partial(middle_kernel, shards, dp_bits), in_specs=[on_chip...]
where the time goes in v5:
time: 331 us; the launch traced here: 326 us
  Pallas kernels  321 us (97%)
  local copies, waits for them, and re-layouts  3.78 us (1%)
    pallas_call x1, Pallas kernels, back(): pl.pallas_call(partial(back_kernel, shards, dp_bits), in_specs=[pl.BlockS...  131 us
    pallas_call x1, Pallas kernels, start(): pl.pallas_call(partial(start_kernel, shards, dp_bits), in_specs=[on_chip]...  110 us
    pallas_call x1, Pallas kernels, middle(): pl.pallas_call(partial(middle_kernel, shards, dp_bits), in_specs=[on_chip...  73.2 us
    pallas_call x1, Pallas kernels, unpack(): pl.pallas_call(unpack_kernel, grid=(PIECES,), in_specs=[pl.BlockSpec((1,...  7.16 us

profile of v5, /device:TPU:16, one launch (start us, length us, event | category | flops | bytes accessed | tf_op | source)
XLA Modules:
  0.0 326.1 jit_solution(14676919945812300400)
XLA Ops:
  0.6 110.1 %start.1 = (bf16[2304,768]{1,0:T(8,128)(2,1)}, bf16[3,2304,128]{2,1,0:T(8,128)(2,1)}, bf16[3,2304,128]{2,1,0:T(8,128)(2,1)}, bf16[3,2304,128]{2,1,0:T(8,128)(2,1...) custom-call(bf16[576,768]{1,0:T(8,128)(2,1)} %tokens_ref.5, ...), custom_call_target="tpu_custom_call" | custom-call | flops 2038431744 | bytes 17694720 | tf_op jit(solution)/shard_map/start/pallas_call | solution.py:1088
  110.7 73.2 %middle.1 = (bf16[576,768]{1,0:T(8,128)(2,1)}, f32[576,768]{1,0:T(8,128)}, bf16[4,576,128]{2,1,0:T(8,128)(2,1)}, bf16[4,288,128]{2,1,0:T(8,128)(2,1)}, f32[16,76...) custom-call(bf16[4,576,128]{2,1,0:T(8,128)(2,1)} %get-tuple-element., ...), custom_call_target="tpu_custom_call" | custom-call | flops 16307453952 | bytes 17694720 | tf_op jit(solution)/shard_map/middle/pallas_call | solution.py:1503
  183.9 130.6 %back.1 = (f32[576,768]{1,0:T(8,128)}, f32[16,768]{1,0:T(8,128)}, bf16[8,72,768]{2,1,0:T(8,128)(2,1)}, bf16[8,224,768]{2,1,0:T(8,128)(2,1)}) custom-call(bf16[3,2304,128]{2,1,0:T(8,128)(2,1)} %get-tuple-element.58.q_ref, bf16[3,2304,128]{2,1,0:T(8,128)(2,1)} %get-tuple-element.59.k_ref, bf16[3,2304,128]{2,1,0:T(8,128)(2,1)} %get-tuple-element.60.v_ref, ...), custom_call_target="tpu_custom_call" | custom-call | flops 20384317440 | bytes 17694720 | tf_op jit(solution)/shard_map/back/pallas_call | solution.py:596
  314.5 0.8 constant_dynamic-slice_fusion
  315.3 0.6 pad_maximum_fusion
  315.9 0.0 copy-start.1
  315.9 7.2 %unpack.1 = (f32[768,768]{1,0:T(8,128)}, f32[768,768]{1,0:T(8,128)}, f32[192,768]{1,0:T(8,128)}, f32[576,768]{1,0:T(8,128)}, f32[768]{0:T(1024)}, /*index=5*/f32...) custom-call(bf16[8,72,768]{2,1,0:T(8,128)(2,1)} %get-tuple-element.7, ...), custom_call_target="tpu_custom_call" | custom-call | tf_op jit(solution)/shard_map/unpack/pallas_call | solution.py:679
  323.0 0.0 copy-start
  323.1 0.0 copy-done.1
  323.1 0.9 copy.35
  324.0 0.9 copy-done
  324.8 1.2 copy.36
Async XLA Ops:
  315.9 7.2 %copy-start.1 = (bf16[576,768]{1,0:T(8,128)(2,1)S(1)}, bf16[576,768]{1,0:T(8,128)(2,1)}, u32[]{:S(2)}) copy-start(bf16[576,768]{1,0:T(8,128)(2,1)} %get-tuple-element.108) | copy-start | bytes 2654212
  323.0 1.8 copy-start

commit v6 on v5

--- a/solution.py
+++ b/solution.py
@@ -85,7 +85,10 @@
     a_away,
     b_keep,
     b_away,
-    early,
+    a_early,
+    a_early_away,
+    b_early,
+    b_early_away,
     tokens_out,
     vectors_out,
     qkv_out,
@@ -126,6 +129,7 @@
     early_more,
     z_got,
     early_got,
+    early_side,
     send,
     recv,
     local,
@@ -162,18 +166,22 @@
             (b_keep, b_sum),
             (tokens_ref, tokens_own),
             (hidden_ref, hidden_own),
-            (early, early_own),
+            (a_early, early_own.at[pl.ds(0, shards // 2)]),
+            (b_early, early_own.at[pl.ds(shards // 2, shards // 2)]),
         )[at]
         return pltpu.make_async_copy(source, landing, local.at[at])
 
     def load_rows(owner):
         rows = pl.ds(pl.multiple_of(owner * block, 16), block)
-        return pltpu.make_async_copy(rows_ref.at[rows], rows_own, local.at[5])
-
-    for at in range(5):
+        return pltpu.make_async_copy(rows_ref.at[rows], rows_own, local.at[6])
+
+    for at in range(6):
         load(at).start()
     load_rows(last).start()
     greet(dp_bits, shards)
+    start_dp(a_early_away, early_side.at[pl.ds(0, shards // 2)], 2)
+    start_dp(b_early_away, early_side.at[pl.ds(shards // 2, shards // 2)], 1)
+    early_sides = pending[-2:]
     start_dp(a_away, a_got, 1)
     start_dp(b_away, b_got, 2)
     first_a, first_b = pending[-2:]
@@ -210,8 +218,14 @@
         for way in range(1, shards):
             piece_copy(way, first).start()
 
-    load(4).wait()
-    send_pieces(True)
+    def early_exchange():
+        for at, copy in enumerate(early_sides):
+            load(4 + at).wait()
+            copy.wait_recv()
+        for owner in range(shards):
+            early_own[owner] = rounded_sum(early_own[owner], early_side[owner])
+        send_pieces(True)
+
 
     def sum_pairs(out, right):
         def step(at, carry):
@@ -239,6 +253,49 @@
             pieces[at] = rounded_sum(a_sum[y_bit, at], a_second[at])
             pieces[split + at] = rounded_sum(b_sum[x_bit, at], b_second[at])
         send_pieces(False)
+
+    split_row = early_own.shape[1]
+    gather_slots = [[next(slots) for _ in range(count)] for count in (2, 3, 1)]
+
+    def gather_copies(stage):
+        first_rows, other_rows = pl.ds(0, half_rows), pl.ds(half_rows, half_rows)
+        if stage == 0:
+            moves = [(own_piece, first_rows, 2), (own_piece, other_rows, 1)]
+        elif stage == 1:
+            moves = [(pl.ds(core * 4 + x_bit * 2, 2), first_rows, 1)]
+            moves += [(core * 4 + 2 * at + y_bit, other_rows, 2) for at in range(2)]
+        else:
+            moves = [(pl.ds(core * 4, 4), pl.ds(0, 2 * half_rows), 0)]
+        return [
+            copy_to(
+                weights_out.at[piece, rows],
+                weights_out.at[piece, rows],
+                gather_slots[stage][at],
+                dp=partner_of(member, bit),
+            )
+            for at, (piece, rows, bit) in enumerate(moves)
+        ]
+
+    def gather_start(stage):
+        for copy in gather_copies(stage):
+            copy.start()
+
+    def gather_wait(stage):
+        for copy in gather_copies(stage):
+            copy.wait_recv()
+
+    def sum_shards():
+        for first, source, landing, rows in (
+            (True, early_own, early_got, slice(0, split_row)),
+            (False, pieces, z_got, slice(split_row, 2 * half_rows)),
+        ):
+            for way in range(1, shards):
+                piece_copy(way, first).wait_recv()
+            total = source[here].astype(f32)
+            for way in range(1, shards):
+                total = total + landing[way - 1].astype(f32)
+            weights_out[own_piece, rows, :] = total.astype(bf16)
+        gather_start(0)
 
     right_slots = [next(slots) for _ in range(shards)]
     left_slots = [next(slots) for _ in range(shards)]
@@ -388,11 +445,13 @@
         order[closing.index(at) + 1] if at in closing and at != closing[-1] else -1 for at in range(total_visits)
     ]
     events = {
-        closing[0] - 1: second_exchange,
-        closing[0] + 2: shard_exchange,
-        closing[1] + 1: lambda: hop(1, 0, True),
+        1: early_exchange,
+        closing[0] + 1: second_exchange,
+        closing[0] + 4: shard_exchange,
+        closing[1] + 2: lambda: hop(1, 0, True),
+        closing[-1]: sum_shards,
     }
-    assert len(events) == 3 and shards >= 4
+    assert len(events) == 5 and shards >= 4
 
     def each_visit(at, carry):
         visit(lookup([pair[0] for pair in visits], at), lookup([pair[1] for pair in visits], at))
@@ -409,17 +468,20 @@
         return carry
 
     lax.fori_loop(0, total_visits, each_visit, 0)
-    for owner in range(last - 1, 0, -1):
-
-        @pl.when(here == 0)
-        def _():
-            to_right(owner).start()
-
-    for owner in range(1, last):
-
-        @pl.when(here == last)
-        def _():
-            to_left(owner).start()
+    def end_sends(nths):
+        for nth in nths:
+
+            @pl.when(here == 0)
+            def _():
+                to_right(last - nth).start()
+
+            @pl.when(here == last)
+            def _():
+                to_left(nth).start()
+
+    end_sends(range(1, last - 1))
+    gather_wait(0)
+    gather_start(1)
 
     sums = column_sums[...]
     weight = weight_ref[...].astype(f32)
@@ -438,8 +500,6 @@
 
     q_core = start_dp(q_all.at[pl.ds((1 - core) * 4, 4)], q_got_core, 0)
     v_copy = vector_stage(0)
-    hop(1, 0, False)
-    hop(2, 0, True)
     q_core.wait_recv()
     for at in range(4):
         q_half[at] = rounded_sum(q_all[core * 4 + at], q_got_core[at])
@@ -447,6 +507,11 @@
     v_copy.wait_recv()
     v_now[1] = v_now[0] + v_got[0]
     v_copy = vector_stage(1)
+    hop(1, 0, False)
+    for moved in range(2, last):
+        hop(moved, 0, True)
+    gather_wait(1)
+    gather_start(2)
     q_x.wait_recv()
     for at in range(2):
         q_quarter[at] = rounded_sum(q_half[x_bit * 2 + at], q_got_x[at])
@@ -466,6 +531,7 @@
         qkv_out[own_piece] = rounded_sum(qkv_out[own_piece], q_got_more[bit - PIECE_BITS])
         v_copy.wait_recv()
         v_now[bit + 1] = v_now[bit] + v_got[bit]
+    q_back = start_dp(qkv_out.at[own_piece], qkv_out.at[own_piece], 2)
     v_shards[here] = v_now[dp_bits]
     for way in range(1, shards):
         copy = copy_to(
@@ -474,54 +540,21 @@
         copy.start()
         pending.append(copy)
     v_waits = pending[-last:]
-    q_back = start_dp(qkv_out.at[own_piece], qkv_out.at[own_piece], 2)
+    end_sends([last - 1])
     q_back.wait_recv()
-    q_back = start_dp(
-        qkv_out.at[pl.ds(core * 4 + x_bit * 2, 2)], qkv_out.at[pl.ds(core * 4 + x_bit * 2, 2)], 1
-    )
-    q_back.wait_recv()
-    q_back = start_dp(qkv_out.at[pl.ds(core * 4, 4)], qkv_out.at[pl.ds(core * 4, 4)], 0)
-
-    split_row = early_own.shape[1]
-    for first, source, landing, rows in (
-        (True, early_own, early_got, slice(0, split_row)),
-        (False, pieces, z_got, slice(split_row, 2 * half_rows)),
-    ):
-        for way in range(1, shards):
-            piece_copy(way, first).wait_recv()
-        total = source[here].astype(f32)
-        for way in range(1, shards):
-            total = total + landing[way - 1].astype(f32)
-        weights_out[own_piece, rows, :] = total.astype(bf16)
-
-    def own_half(low, *index):
-        rows = pl.ds(0 if low else half_rows, half_rows)
-        return weights_out.at[index[0], rows]
-
-    back_a = start_dp(own_half(True, own_piece), own_half(True, own_piece), 2)
-    back_b = start_dp(own_half(False, own_piece), own_half(False, own_piece), 1)
-    back_a.wait_recv()
     span = pl.ds(core * 4 + x_bit * 2, 2)
-    back_a = start_dp(own_half(True, span), own_half(True, span), 1)
-    back_b.wait_recv()
-    back_c = [
-        start_dp(own_half(False, core * 4 + 2 * at + y_bit), own_half(False, core * 4 + 2 * at + y_bit), 2)
-        for at in range(2)
-    ]
-    for moved in range(2, last):
-        hop(moved, 0, False)
-        if moved > 2:
-            hop(moved, 0, True)
+    q_back = start_dp(qkv_out.at[span], qkv_out.at[span], 1)
     for nth in range(1, last):
         for moved in range(1, last):
             hop(moved, nth, True)
             hop(moved, nth, False)
-    back_a.wait_recv()
-    for copy in back_c:
-        copy.wait_recv()
+        if nth == 1:
+            for moved in range(2, last):
+                hop(moved, 0, False)
+    q_back.wait_recv()
     span = pl.ds(core * 4, 4)
-    back_core = start_dp(weights_out.at[span], weights_out.at[span], 0)
-
+    q_back = start_dp(qkv_out.at[span], qkv_out.at[span], 0)
+    gather_wait(2)
     for copy in v_waits:
         copy.wait_recv()
     vectors_sum = v_shards[0]
@@ -560,11 +593,13 @@
 
     lax.fori_loop(0, 4, close, 0)
     q_back.wait_recv()
-    back_core.wait_recv()
     for copy in pending:
         copy.wait_send()
     for at in range(2):
         second(at).wait_send()
+    for stage in range(3):
+        for copy in gather_copies(stage):
+            copy.wait_send()
     for way in range(1, shards):
         piece_copy(way, True).wait_send()
         piece_copy(way).wait_send()
@@ -591,11 +626,11 @@
     late_rows = quarter[2]
     count = columns // PIECES
     more = max(1, dp_bits - PIECE_BITS)
-    copies = 20 + 2 * shards + 3 * (shards - 1) + 5 * dp_bits
+    copies = 26 + 2 * shards + 3 * (shards - 1) + 5 * dp_bits
     vm = pltpu.VMEM
     return pl.pallas_call(
         partial(back_kernel, shards, dp_bits),
-        in_specs=[pl.BlockSpec(memory_space=vm)] * 11 + [pl.BlockSpec(memory_space=pl.ANY)] * 8,
+        in_specs=[pl.BlockSpec(memory_space=vm)] * 11 + [pl.BlockSpec(memory_space=pl.ANY)] * 11,
         out_specs=[pl.BlockSpec(memory_space=vm)] * 4,
         out_shape=[
             jax.ShapeDtypeStruct((block, width), f32),
@@ -640,9 +675,10 @@
             vm((more, shards, early_rows, width), bf16),
             vm((shards - 1, late_rows, width), bf16),
             vm((shards - 1, early_rows, width), bf16),
+            vm((shards, early_rows, width), bf16),
             pltpu.SemaphoreType.DMA((copies,)),
             pltpu.SemaphoreType.DMA((copies,)),
-            pltpu.SemaphoreType.DMA((6,)),
+            pltpu.SemaphoreType.DMA((7,)),
         ],
         compiler_params=pltpu.CompilerParams(
             collective_id=1, has_side_effects=True, vmem_limit_bytes=67043328
@@ -1159,7 +1195,10 @@
     a_away,
     b_keep,
     b_away,
-    early_out,
+    a_early,
+    a_early_away,
+    b_early,
+    b_early_away,
     weights,
     attended,
     proj,
@@ -1179,8 +1218,6 @@
     got,
     a_got,
     b_got,
-    a_second,
-    b_second,
     send,
     recv,
     local,
@@ -1326,22 +1363,16 @@
 
     piece_rows = pl.ds(0, fc_rows)
     own = core * half
-    side_slots = [next(slots) for _ in range(5)]
-
-    def side_copies(stage):
+    side_slots = [next(slots) for _ in range(3)]
+
+    def side_copies():
         first_half, second_half = pl.ds(0, split), pl.ds(split, shards - split)
-        if stage == 0:
-            moves = [(weights.at[pl.ds(own + (1 - x_bit) * 2, 2), first_half, piece_rows], a_got, 1)]
-            moves += [
-                (weights.at[own + 2 * x + 1 - y_bit, second_half, piece_rows], b_got.at[x], 2) for x in range(2)
-            ]
-        else:
-            moves = [
-                (weights.at[own + 2 * x_bit + 1 - y_bit, first_half, piece_rows], a_second, 2),
-                (weights.at[own + 2 * (1 - x_bit) + y_bit, second_half, piece_rows], b_second, 1),
-            ]
+        moves = [(weights.at[pl.ds(own + (1 - x_bit) * 2, 2), first_half, piece_rows], a_got, 1)]
+        moves += [
+            (weights.at[own + 2 * x + 1 - y_bit, second_half, piece_rows], b_got.at[x], 2) for x in range(2)
+        ]
         return [
-            copy_to(source, landing, side_slots[3 * stage + at], dp=partner_of(member, bit))
+            copy_to(source, landing, side_slots[at], dp=partner_of(member, bit))
             for at, (source, landing, bit) in enumerate(moves)
         ]
 
@@ -1358,26 +1389,21 @@
             return carry
 
         lax.fori_loop(0, half * shards, step, 0)
-        for copy in side_copies(0):
+        for copy in side_copies():
             copy.start()
 
     def early_sides():
-        for copy in side_copies(0):
+        for copy in side_copies():
             copy.wait_recv()
         for owner in range(split):
-            for at in range(2):
-                grow_piece(own + 2 * x_bit + at, owner, a_got[at, owner])
-                grow_piece(own + 2 * at + y_bit, split + owner, b_got[at, owner])
-        for copy in side_copies(1):
-            copy.start()
-
-    def early_end():
-        for copy in side_copies(1):
-            copy.wait_recv()
-        mine = own + 2 * x_bit + y_bit
-        for owner in range(split):
-            early_out[owner] = rounded_sum(weights[mine, owner, piece_rows, :], a_second[owner])
-            early_out[split + owner] = rounded_sum(weights[mine, split + owner, piece_rows, :], b_second[owner])
+            for keep, away, side, got_side, y_side in (
+                (a_early, a_early_away, x_bit, a_got, True),
+                (b_early, b_early_away, y_bit, b_got, False),
+            ):
+                for out, at in ((keep, y_bit if y_side else x_bit), (away, 1 - (y_bit if y_side else x_bit))):
+                    piece = own + (2 * side + at if y_side else 2 * at + side)
+                    shard = owner if y_side else split + owner
+                    out[owner] = rounded_sum(weights[piece, shard, piece_rows, :], got_side[at, owner])
 
     def backward(owner, carry):
         wide[:block, :] = times_transposed(grad_mlp[...], fc2_of(owner))
@@ -1391,13 +1417,9 @@
         vectors_out[pl.ds(8 + owner, 1), :] = each_chunk(slopes, empty)
         product = times_transposed(grad_pre[owner], fc1_of(owner))
         total[...] = jnp.where(owner == 0, product, total[...] + product)
-        product = contract_rows(active[owner], grad_mlp[...]).astype(bf16)
-        weights[:, owner, :fc_rows, :] = product.reshape(PIECES, fc_rows, width)
-        core_copy(owner, True).start()
         return carry
 
     lax.fori_loop(0, shards, backward, 0)
-    early_pairs()
 
     def leave(at, sums):
         rows = chunk(at)
@@ -1444,6 +1466,13 @@
             back.append(copy)
         out[here] = source[here]
 
+    def early_grads(owner, carry):
+        product = contract_rows(active[owner], grad_mlp[...]).astype(bf16)
+        weights[:, owner, :fc_rows, :] = product.reshape(PIECES, fc_rows, width)
+        core_copy(owner, True).start()
+        return carry
+
+    lax.fori_loop(0, shards, early_grads, 0)
     wide[...] = contract_rows(attended[:, :], grad_branch[...])
     for owner in range(shards):
         for piece in range(PIECES):
@@ -1455,6 +1484,8 @@
                     to = slice(proj_first + begin - first, proj_first + stop - first)
                     weights[piece, owner, to, :] = wide[rows, :].astype(bf16)
 
+    early_pairs()
+
     def weight_grads(owner, carry):
         product = contract_rows(normed[...], grad_pre[owner]).astype(bf16)
         weights[:, owner, fc_rows:proj_first, :] = product.reshape(PIECES, fc_rows, width)
@@ -1462,7 +1493,6 @@
         return carry
 
     lax.fori_loop(0, shards, weight_grads, 0)
-    early_sides()
     for owner in range(shards):
         core_copy(owner, False).wait_recv()
         for x in range(2):
@@ -1480,10 +1510,10 @@
                             weights[own + piece, owner, fc_rows:, :], got[piece, owner]
                         )
 
-    early_end()
+    early_sides()
     for copy in back:
         copy.wait_recv()
-    for copy in back + side_copies(0) + side_copies(1):
+    for copy in back + side_copies():
         copy.wait_send()
     for owner in range(shards):
         core_copy(owner, True).wait_send()
@@ -1499,11 +1529,12 @@
     on_chip = pl.BlockSpec(memory_space=vm)
     fc_rows = width // PIECES
     quarter = jax.ShapeDtypeStruct((2, shards // 2, rows - fc_rows, width), bf16)
-    copies = 2 * (shards - 1) + 2 * shards + 5
+    early_half = jax.ShapeDtypeStruct((shards // 2, fc_rows, width), bf16)
+    copies = 2 * (shards - 1) + 2 * shards + 3
     return pl.pallas_call(
         partial(middle_kernel, shards, dp_bits),
         in_specs=[on_chip, on_chip, pl.BlockSpec(memory_space=pl.ANY)] + [on_chip] * 9,
-        out_specs=[on_chip] * 10,
+        out_specs=[on_chip] * 13,
         out_shape=[
             jax.ShapeDtypeStruct((block, width), bf16),
             jax.ShapeDtypeStruct((block, width), f32),
@@ -1514,7 +1545,10 @@
             quarter,
             quarter,
             quarter,
-            jax.ShapeDtypeStruct((shards, fc_rows, width), bf16),
+            early_half,
+            early_half,
+            early_half,
+            early_half,
         ],
         scratch_shapes=[
             vm(weights.shape, bf16),
@@ -1536,8 +1570,6 @@
             vm((PIECES // 2, shards, rows - fc_rows, width), bf16),
             vm((2, shards // 2, fc_rows, width), bf16),
             vm((2, shards // 2, fc_rows, width), bf16),
-            vm((shards // 2, fc_rows, width), bf16),
-            vm((shards // 2, fc_rows, width), bf16),
             pltpu.SemaphoreType.DMA((copies,)),
             pltpu.SemaphoreType.DMA((copies,)),
             pltpu.SemaphoreType.DMA((shards,)),

time: 331 us -> 317 us (0.958)
  Pallas kernels: 321 us -> 309 us
    pallas_call x1, Pallas kernels: 131 us -> 123 us  [back(): pl.pallas_call(partial(back_kernel, shards, dp_bits), in_specs=[pl.BlockS...]
    pallas_call x1, Pallas kernels: 73.2 us -> 69.1 us  [middle(): pl.pallas_call(partial(middle_kernel, shards, dp_bits), in_specs=[on_chip...]
where the time goes in v6:
time: 317 us; the launch traced here: 314 us
  Pallas kernels  309 us (97%)
  local copies, waits for them, and re-layouts  3.78 us (1%)
    pallas_call x1, Pallas kernels, back(): pl.pallas_call(partial(back_kernel, shards, dp_bits), in_specs=[pl.BlockS...  123 us
    pallas_call x1, Pallas kernels, start(): pl.pallas_call(partial(start_kernel, shards, dp_bits), in_specs=[on_chip]...  110 us
    pallas_call x1, Pallas kernels, middle(): pl.pallas_call(partial(middle_kernel, shards, dp_bits), in_specs=[on_chip...  69.1 us
    pallas_call x1, Pallas kernels, unpack(): pl.pallas_call(unpack_kernel, grid=(PIECES,), in_specs=[pl.BlockSpec((1,...  7.16 us

profile of v6, /device:TPU:16, one launch (start us, length us, event | category | flops | bytes accessed | tf_op | source)
XLA Modules:
  0.0 313.9 jit_solution(13991370316393368937)
XLA Ops:
  0.6 110.1 %start.1 = (bf16[2304,768]{1,0:T(8,128)(2,1)}, bf16[3,2304,128]{2,1,0:T(8,128)(2,1)}, bf16[3,2304,128]{2,1,0:T(8,128)(2,1)}, bf16[3,2304,128]{2,1,0:T(8,128)(2,1...) custom-call(bf16[576,768]{1,0:T(8,128)(2,1)} %tokens_ref.5, ...), custom_call_target="tpu_custom_call" | custom-call | flops 2038431744 | bytes 17694720 | tf_op jit(solution)/shard_map/start/pallas_call | solution.py:1124
  110.8 69.1 %middle.1 = (bf16[576,768]{1,0:T(8,128)(2,1)}, f32[576,768]{1,0:T(8,128)}, bf16[4,576,128]{2,1,0:T(8,128)(2,1)}, bf16[4,288,128]{2,1,0:T(8,128)(2,1)}, f32[16,76...) custom-call(bf16[4,576,128]{2,1,0:T(8,128)(2,1)} %get-tuple-element., ...), custom_call_target="tpu_custom_call" | custom-call | flops 16307453952 | bytes 17694720 | tf_op jit(solution)/shard_map/middle/pallas_call | solution.py:1534
  179.8 122.5 %back.1 = (f32[576,768]{1,0:T(8,128)}, f32[16,768]{1,0:T(8,128)}, bf16[8,72,768]{2,1,0:T(8,128)(2,1)}, bf16[8,224,768]{2,1,0:T(8,128)(2,1)}) custom-call(bf16[3,2304,128]{2,1,0:T(8,128)(2,1)} %get-tuple-element.61.q_ref, bf16[3,2304,128]{2,1,0:T(8,128)(2,1)} %get-tuple-element.62.k_ref, bf16[3,2304,128]{2,1,0:T(8,128)(2,1)} %get-tuple-element.63.v_ref, ...), custom_call_target="tpu_custom_call" | custom-call | flops 20384317440 | bytes 17694720 | tf_op jit(solution)/shard_map/back/pallas_call | solution.py:631
  302.4 0.8 constant_dynamic-slice_fusion
  303.2 0.6 pad_maximum_fusion
  303.8 0.0 copy-start.1
  303.8 7.2 %unpack.1 = (f32[768,768]{1,0:T(8,128)}, f32[768,768]{1,0:T(8,128)}, f32[192,768]{1,0:T(8,128)}, f32[576,768]{1,0:T(8,128)}, f32[768]{0:T(1024)}, /*index=5*/f32...) custom-call(bf16[8,72,768]{2,1,0:T(8,128)(2,1)} %get-tuple-element.8, ...), custom_call_target="tpu_custom_call" | custom-call | tf_op jit(solution)/shard_map/unpack/pallas_call | solution.py:715
  310.9 0.0 copy-start
  310.9 0.0 copy-done.1
  310.9 0.9 copy.35
  311.9 0.9 copy-done
  312.7 1.2 copy.36
Async XLA Ops:
  303.8 7.2 %copy-start.1 = (bf16[576,768]{1,0:T(8,128)(2,1)S(1)}, bf16[576,768]{1,0:T(8,128)(2,1)}, u32[]{:S(2)}) copy-start(bf16[576,768]{1,0:T(8,128)(2,1)} %get-tuple-element.114) | copy-start | bytes 2654212
  310.9 1.8 copy-start

commit v7 on v6

--- a/solution.py
+++ b/solution.py
@@ -54,13 +54,15 @@
     return index + (1 - 2 * bit_of(index, bit)) * (1 << bit)
 
 
-def greet(dp_bits, shards):
+def greet(dp_bits, shards, ahead=None):
     barrier = pltpu.get_barrier_semaphore()
     member, here = lax.axis_index("dp"), lax.axis_index("tensor")
     peers = [{"dp": partner_of(member, bit)} for bit in range(dp_bits)]
     peers += [{"tensor": lax.rem(here + way, shards)} for way in range(1, shards)]
     for peer in peers:
         pl.semaphore_signal(barrier, inc=1, device_id=peer, device_id_type=MESH)
+    if ahead is not None:
+        ahead()
     pl.semaphore_wait(barrier, len(peers))
 
 
@@ -177,8 +179,55 @@
 
     for at in range(6):
         load(at).start()
-    load_rows(last).start()
-    greet(dp_bits, shards)
+    flipped = here >= shards // 2
+
+    def mirrored(owner):
+        return jnp.where(flipped, last - owner, owner)
+
+    load_rows(mirrored(last)).start()
+    def set_up():
+        dq[...] = jnp.zeros_like(dq)
+        dk[...] = jnp.zeros_like(dk)
+        dv[...] = jnp.zeros_like(dv)
+        q_wide[...] = jnp.zeros_like(q_wide)
+        column_sums[...] = jnp.zeros_like(column_sums)
+        source = lax.broadcasted_iota(jnp.int32, (LANES, LANES), 0)
+        target = lax.broadcasted_iota(jnp.int32, (LANES, LANES), 1)
+        gathers = (target >= HEAD_DIM) & (target < HEAD_DIM + 3)
+        picks = []
+        for odd in range(2):
+            inside = (source >= HEAD_DIM * odd) & (source < HEAD_DIM * (odd + 1))
+            summing = jnp.where(inside & gathers, -1.0, 0.0).astype(bf16)
+            moving = jnp.where(inside & (source - HEAD_DIM * odd == target), 1.0, 0.0).astype(bf16)
+            picks.append((summing, moving))
+        half = block // 2
+        lane = lax.broadcasted_iota(jnp.int32, (half, LANES), 1)
+
+        def prepare(at, carry):
+            for side in range(2):
+                rows = pl.ds(pl.multiple_of((2 * at + side) * half, half), half)
+                single_rows = pl.ds(pl.multiple_of(at * half, half), half)
+                for head, odd, mixed, grad in (
+                    (0, 0, pair_ref[rows, :], pair_grad_ref[rows, :]),
+                    (1, 1, pair_ref[rows, :], pair_grad_ref[rows, :]),
+                    (2, side, single_ref[single_rows, :], single_grad_ref[single_rows, :]),
+                ):
+                    summing, moving = picks[odd]
+                    product = grad.astype(f32) * mixed.astype(f32)
+                    high = product.astype(bf16)
+                    low = (product - high.astype(f32)).astype(bf16)
+                    shared = jnp.dot(high, summing, preferred_element_type=f32) + jnp.dot(
+                        low, summing, preferred_element_type=f32
+                    )
+                    moved = jnp.dot(grad, moving, preferred_element_type=f32)
+                    for place, value in enumerate(split_three(shared)):
+                        moved = jnp.where(lane == HEAD_DIM + place, value.astype(f32), moved)
+                    grad_heads[head, rows, :] = moved.astype(bf16)
+            return carry
+
+        lax.fori_loop(0, shards, prepare, 0)
+
+    greet(dp_bits, shards, set_up)
     start_dp(a_early_away, early_side.at[pl.ds(0, shards // 2)], 2)
     start_dp(b_early_away, early_side.at[pl.ds(shards // 2, shards // 2)], 1)
     early_sides = pending[-2:]
@@ -301,13 +350,13 @@
     left_slots = [next(slots) for _ in range(shards)]
 
     def to_right(owner):
-        return copy_to(part.at[owner], arrived.at[owner], right_slots[owner], tensor=lax.rem(here + 1, shards))
+        return copy_to(part.at[owner], arrived.at[owner], right_slots[0] + owner, tensor=lax.rem(here + 1, shards))
 
     def to_left(owner, target=None):
         to = lax.rem(here + last, shards) if target is None else target
         landing = jnp.where(owner == to, shards, owner)
         return copy_to(
-            part.at[owner], arrived.at[landing], left_slots[owner], tensor=lax.rem(here + last, shards)
+            part.at[owner], arrived.at[landing], left_slots[0] + owner, tensor=lax.rem(here + last, shards)
         )
 
     def add_arrived(owner, landing):
@@ -328,47 +377,6 @@
                 copy.wait_recv()
                 add_arrived(owner, owner)
                 copy.start()
-
-    dq[...] = jnp.zeros_like(dq)
-    dk[...] = jnp.zeros_like(dk)
-    dv[...] = jnp.zeros_like(dv)
-    q_wide[...] = jnp.zeros_like(q_wide)
-    column_sums[...] = jnp.zeros_like(column_sums)
-    source = lax.broadcasted_iota(jnp.int32, (LANES, LANES), 0)
-    target = lax.broadcasted_iota(jnp.int32, (LANES, LANES), 1)
-    gathers = (target >= HEAD_DIM) & (target < HEAD_DIM + 3)
-    picks = []
-    for odd in range(2):
-        inside = (source >= HEAD_DIM * odd) & (source < HEAD_DIM * (odd + 1))
-        summing = jnp.where(inside & gathers, -1.0, 0.0).astype(bf16)
-        moving = jnp.where(inside & (source - HEAD_DIM * odd == target), 1.0, 0.0).astype(bf16)
-        picks.append((summing, moving))
-    half = block // 2
-    lane = lax.broadcasted_iota(jnp.int32, (half, LANES), 1)
-
-    def prepare(at, carry):
-        for side in range(2):
-            rows = pl.ds(pl.multiple_of((2 * at + side) * half, half), half)
-            single_rows = pl.ds(pl.multiple_of(at * half, half), half)
-            for head, odd, mixed, grad in (
-                (0, 0, pair_ref[rows, :], pair_grad_ref[rows, :]),
-                (1, 1, pair_ref[rows, :], pair_grad_ref[rows, :]),
-                (2, side, single_ref[single_rows, :], single_grad_ref[single_rows, :]),
-            ):
-                summing, moving = picks[odd]
-                product = grad.astype(f32) * mixed.astype(f32)
-                high = product.astype(bf16)
-                low = (product - high.astype(f32)).astype(bf16)
-                shared = jnp.dot(high, summing, preferred_element_type=f32) + jnp.dot(
-                    low, summing, preferred_element_type=f32
-                )
-                moved = jnp.dot(grad, moving, preferred_element_type=f32)
-                for place, value in enumerate(split_three(shared)):
-                    moved = jnp.where(lane == HEAD_DIM + place, value.astype(f32), moved)
-                grad_heads[head, rows, :] = moved.astype(bf16)
-        return carry
-
-    lax.fori_loop(0, shards, prepare, 0)
 
     def rows_of(owner):
         return pl.ds(pl.multiple_of(owner * block, 16), block)
@@ -402,13 +410,13 @@
         packed[:, 4 * LANES : columns] = dv[2, rows, :HEAD_DIM].astype(bf16)
         part[owner] = jnp.dot(packed[...], weight_ref[...], preferred_element_type=f32).astype(bf16)
 
-        @pl.when((owner == last) & (here == 0))
+        @pl.when((owner > 1) & (here == 0))
         def _():
-            to_right(last).start()
-
-        @pl.when((owner == 0) & (here == last))
+            to_right(owner).start()
+
+        @pl.when((owner < last - 1) & (here == last))
         def _():
-            to_left(0).start()
+            to_left(owner).start()
 
         load_rows(owner).wait()
         q_wide[...] += contract_rows(packed[...], rows_own[...])
@@ -444,17 +452,21 @@
     later = [
         order[closing.index(at) + 1] if at in closing and at != closing[-1] else -1 for at in range(total_visits)
     ]
+    def first_hops():
+        hop(1, 0, True)
+        hop(1, 0, False)
+
     events = {
         1: early_exchange,
         closing[0] + 1: second_exchange,
         closing[0] + 4: shard_exchange,
-        closing[1] + 2: lambda: hop(1, 0, True),
+        closing[1] + 1: first_hops,
         closing[-1]: sum_shards,
     }
     assert len(events) == 5 and shards >= 4
 
     def each_visit(at, carry):
-        visit(lookup([pair[0] for pair in visits], at), lookup([pair[1] for pair in visits], at))
+        visit(*(mirrored(lookup([pair[side] for pair in visits], at)) for side in range(2)))
         for when, event in events.items():
 
             @pl.when(at == when)
@@ -463,7 +475,8 @@
 
         @pl.when(lookup([int(owner >= 0) for owner in closed], at) == 1)
         def _():
-            close_block(lookup(closed, at), lookup(later, at))
+            following = lookup(later, at)
+            close_block(mirrored(lookup(closed, at)), jnp.where(following < 0, -1, mirrored(following)))
 
         return carry
 
@@ -479,7 +492,6 @@
             def _():
                 to_left(nth).start()
 
-    end_sends(range(1, last - 1))
     gather_wait(0)
     gather_start(1)
 
@@ -507,9 +519,9 @@
     v_copy.wait_recv()
     v_now[1] = v_now[0] + v_got[0]
     v_copy = vector_stage(1)
-    hop(1, 0, False)
     for moved in range(2, last):
         hop(moved, 0, True)
+        hop(moved, 0, False)
     gather_wait(1)
     gather_start(2)
     q_x.wait_recv()
@@ -548,9 +560,6 @@
         for moved in range(1, last):
             hop(moved, nth, True)
             hop(moved, nth, False)
-        if nth == 1:
-            for moved in range(2, last):
-                hop(moved, 0, False)
     q_back.wait_recv()
     span = pl.ds(core * 4, 4)
     q_back = start_dp(qkv_out.at[span], qkv_out.at[span], 0)
@@ -690,12 +699,29 @@
     )(*heads_in, *pair_in, weight, gain, shift, vectors, rows, tokens, grad_hidden, *exchanged)
 
 
-def unpack_kernel(qkv_ref, weights_ref, totals_ref, fc1_out, fc2_out, proj_out, qkv_out, fc1_bias_out, *vector_outs):
+def unpack_kernel(
+    qkv_ref,
+    weights_ref,
+    totals_ref,
+    tokens_ref,
+    rows_ref,
+    fc1_out,
+    fc2_out,
+    proj_out,
+    qkv_out,
+    tokens_out,
+    rows_out,
+    qv_out,
+    fc1_bias_out,
+    *vector_outs
+):
     fc_rows, proj_rows = fc1_out.shape[0], proj_out.shape[0]
     fc2_out[...] = weights_ref[0, :fc_rows].astype(jnp.float32)
     fc1_out[...] = weights_ref[0, fc_rows : 2 * fc_rows].astype(jnp.float32)
     proj_out[...] = weights_ref[0, 2 * fc_rows : 2 * fc_rows + proj_rows].astype(jnp.float32)
     qkv_out[...] = qkv_ref[0].astype(jnp.float32)
+    tokens_out[...] = tokens_ref[...]
+    rows_out[...] = rows_ref[...]
 
     @pl.when(pl.program_id(0) == 0)
     def _():
@@ -704,14 +730,21 @@
             out[...] = totals_ref[at : at + 1, :].reshape(width)
         here = lax.axis_index("tensor")
         fc1_bias_out[...] = totals_ref[pl.ds(8 + here, 1), :].reshape(width)
-
-
-def unpack(qkv, weights, totals, fc_rows, proj_rows):
+        columns = qv_out.shape[1]
+        row = totals_ref[pl.ds(12 + here, 1), :]
+        qv_out[0:1, :] = row[:, :columns]
+        qv_out[1:2, :] = row[:, 2 * columns : 3 * columns]
+
+
+def unpack(qkv, weights, totals, tokens, rows_in, fc_rows, proj_rows):
     f32 = jnp.float32
     _, rows, width = weights.shape
     qkv_rows = qkv.shape[1]
-    counts = (fc_rows, fc_rows, proj_rows, qkv_rows)
+    token_rows = tokens.shape[0] // PIECES
+    columns = proj_rows * PIECES
+    counts = (fc_rows, fc_rows, proj_rows, qkv_rows, token_rows)
     vector = pl.BlockSpec((width,), lambda i: (0,))
+    token_spec = pl.BlockSpec((token_rows, width), lambda i: (i, 0))
     return pl.pallas_call(
         unpack_kernel,
         grid=(PIECES,),
@@ -719,12 +752,17 @@
             pl.BlockSpec((1, qkv_rows, width), lambda i: (i, 0, 0)),
             pl.BlockSpec((1, rows, width), lambda i: (i, 0, 0)),
             pl.BlockSpec(totals.shape, lambda i: (0, 0)),
+            token_spec,
+            token_spec,
         ],
-        out_specs=[pl.BlockSpec((count, width), lambda i: (i, 0)) for count in counts] + [vector] * 9,
+        out_specs=[pl.BlockSpec((count, width), lambda i: (i, 0)) for count in counts]
+        + [token_spec, pl.BlockSpec((2, columns), lambda i: (0, 0))]
+        + [vector] * 9,
         out_shape=[jax.ShapeDtypeStruct((PIECES * count, width), f32) for count in counts]
+        + [jax.ShapeDtypeStruct(rows_in.shape, rows_in.dtype), jax.ShapeDtypeStruct((2, columns), f32)]
         + [jax.ShapeDtypeStruct((width,), f32)] * 9,
         name="unpack",
-    )(qkv, weights, totals)
+    )(qkv, weights, totals, tokens, rows_in)
 
 
 def start_kernel(
@@ -1242,14 +1280,15 @@
         )
 
     loads = []
-    for owner in range(shards):
-        load = pltpu.make_async_copy(weights_ref.at[:, owner], weights.at[:, owner], local.at[owner])
-        load.start()
-        loads.append(load)
+    for at, (first, end) in enumerate(
+        ((proj_first, weights.shape[2]), (fc_rows, proj_first), (0, fc_rows))
+    ):
+        rows = pl.ds(first, end - first)
+        loads.append(pltpu.make_async_copy(weights_ref.at[:, :, rows], weights.at[:, :, rows], local.at[at]))
+        loads[-1].start()
     greet(dp_bits, shards)
 
-    for load in loads:
-        load.wait()
+    loads[0].wait()
 
     def fc1_of(owner):
         return weights[:, owner, fc_rows:proj_first, :].reshape(width, width)
@@ -1326,6 +1365,8 @@
         total[...] = jnp.where(owner == 0, product, total[...] + product)
         return carry
 
+    for load in loads[1:]:
+        load.wait()
     lax.fori_loop(0, shards, forward, 0)
     empty = jnp.zeros((1, width), f32)
 
@@ -1653,12 +1694,10 @@
         grad_hidden,
         exchanged,
     )
-    fc1_grad, fc2_grad, proj_grad, qkv_grad, fc1_bias_grad, *sums = unpack(
-        qkv_pieces, weight_pieces, totals, width // PIECES, head_columns // PIECES
+    fc1_grad, fc2_grad, proj_grad, qkv_grad, grad_tokens, block_out, qv_grad, fc1_bias_grad, *sums = unpack(
+        qkv_pieces, weight_pieces, totals, grad_tokens, block_out, width // PIECES, head_columns // PIECES
     )
     qkv_grad = qkv_grad.reshape(3, head_columns, width).transpose(0, 2, 1)
-    qv_sums = lax.dynamic_index_in_dim(totals, 12 + here, 0, keepdims=False)
-    qv_grad = jnp.stack([qv_sums[:head_columns], qv_sums[2 * head_columns : 3 * head_columns]])
     return (
         block_out,
         grad_tokens,

time: 317 us -> 304 us (0.959)
  Pallas kernels: 309 us -> 303 us
  local copies, waits for them, and re-layouts: 3.78 us -> 0 us
    pallas_call x1, Pallas kernels: 123 us -> 115 us  [back(): pl.pallas_call(partial(back_kernel, shards, dp_bits), in_specs=[pl.BlockS...]
where the time goes in v7:
time: 304 us; the launch traced here: 303 us
  Pallas kernels  303 us (100%)
    pallas_call x1, Pallas kernels, back(): pl.pallas_call(partial(back_kernel, shards, dp_bits), in_specs=[pl.BlockS...  115 us
    pallas_call x1, Pallas kernels, start(): pl.pallas_call(partial(start_kernel, shards, dp_bits), in_specs=[on_chip]...  110 us
    pallas_call x1, Pallas kernels, middle(): pl.pallas_call(partial(middle_kernel, shards, dp_bits), in_specs=[on_chip...  69 us
    pallas_call x1, Pallas kernels, unpack(): pl.pallas_call(unpack_kernel, grid=(PIECES,), in_specs=[pl.BlockSpec((1,...  8.45 us

profile of v7, /device:TPU:16, one launch (start us, length us, event | category | flops | bytes accessed | tf_op | source)
XLA Modules:
  0.0 303.4 jit_solution(18123294916972900106)
XLA Ops:
  0.6 110.1 %start.1 = (bf16[2304,768]{1,0:T(8,128)(2,1)}, bf16[3,2304,128]{2,1,0:T(8,128)(2,1)}, bf16[3,2304,128]{2,1,0:T(8,128)(2,1)}, bf16[3,2304,128]{2,1,0:T(8,128)(2,1...) custom-call(bf16[576,768]{1,0:T(8,128)(2,1)} %tokens_ref.5, ...), custom_call_target="tpu_custom_call" | custom-call | flops 2038431744 | bytes 17694720 | tf_op jit(solution)/shard_map/start/pallas_call | solution.py:1162
  110.7 69.0 %middle.1 = (bf16[576,768]{1,0:T(8,128)(2,1)}, f32[576,768]{1,0:T(8,128)}, bf16[4,576,128]{2,1,0:T(8,128)(2,1)}, bf16[4,288,128]{2,1,0:T(8,128)(2,1)}, f32[16,76...) custom-call(bf16[4,576,128]{2,1,0:T(8,128)(2,1)} %get-tuple-element., ...), custom_call_target="tpu_custom_call" | custom-call | flops 16307453952 | bytes 17694720 | tf_op jit(solution)/shard_map/middle/pallas_call | solution.py:1575
  179.8 114.9 %back.1 = (f32[576,768]{1,0:T(8,128)}, f32[16,768]{1,0:T(8,128)}, bf16[8,72,768]{2,1,0:T(8,128)(2,1)}, bf16[8,224,768]{2,1,0:T(8,128)(2,1)}) custom-call(bf16[3,2304,128]{2,1,0:T(8,128)(2,1)} %get-tuple-element.59.q_ref, bf16[3,2304,128]{2,1,0:T(8,128)(2,1)} %get-tuple-element.60.k_ref, bf16[3,2304,128]{2,1,0:T(8,128)(2,1)} %get-tuple-element.61.v_ref, ...), custom_call_target="tpu_custom_call" | custom-call | flops 20384317440 | bytes 17694720 | tf_op jit(solution)/shard_map/back/pallas_call | solution.py:640
  294.7 8.4 %unpack.1 = (f32[768,768]{1,0:T(8,128)}, f32[768,768]{1,0:T(8,128)}, f32[192,768]{1,0:T(8,128)}, f32[576,768]{1,0:T(8,128)}, f32[576,768]{1,0:T(8,128)}, /*index...) custom-call(bf16[8,72,768]{2,1,0:T(8,128)(2,1)} %get-tuple-element.8, ...), custom_call_target="tpu_custom_call" | custom-call | tf_op jit(solution)/shard_map/unpack/pallas_call | solution.py:748

commit v8 on v7

--- a/solution.py
+++ b/solution.py
@@ -40,6 +40,7 @@
 MESH = pl.DeviceIdType.MESH
 PIECES = 8
 PIECE_BITS = 3
+UNPACK_STEPS = 2
 
 
 def rounded_sum(left, right):
@@ -69,9 +70,9 @@
 def back_kernel(
     shards,
     dp_bits,
-    q_ref,
-    k_ref,
-    v_ref,
+    q_in,
+    k_in,
+    v_in,
     pair_ref,
     single_ref,
     pair_grad_ref,
@@ -93,6 +94,11 @@
     b_early_away,
     tokens_out,
     vectors_out,
+    qkv_result,
+    weights_result,
+    q_ref,
+    k_ref,
+    v_ref,
     qkv_out,
     weights_out,
     grad_heads,
@@ -170,14 +176,19 @@
             (hidden_ref, hidden_own),
             (a_early, early_own.at[pl.ds(0, shards // 2)]),
             (b_early, early_own.at[pl.ds(shards // 2, shards // 2)]),
+            (q_in, q_ref),
+            (k_in, k_ref),
+            (v_in, v_ref),
+            (qkv_out, qkv_result),
+            (weights_out, weights_result),
         )[at]
         return pltpu.make_async_copy(source, landing, local.at[at])
 
     def load_rows(owner):
         rows = pl.ds(pl.multiple_of(owner * block, 16), block)
-        return pltpu.make_async_copy(rows_ref.at[rows], rows_own, local.at[6])
-
-    for at in range(6):
+        return pltpu.make_async_copy(rows_ref.at[rows], rows_own, local.at[11])
+
+    for at in (6, 7, 8, 0, 1, 2, 3, 4, 5):
         load(at).start()
     flipped = here >= shards // 2
 
@@ -377,6 +388,9 @@
                 copy.wait_recv()
                 add_arrived(owner, owner)
                 copy.start()
+
+    for at in (6, 7, 8):
+        load(at).wait()
 
     def rows_of(owner):
         return pl.ds(pl.multiple_of(owner * block, 16), block)
@@ -564,6 +578,7 @@
     span = pl.ds(core * 4, 4)
     q_back = start_dp(qkv_out.at[span], qkv_out.at[span], 0)
     gather_wait(2)
+    load(10).start()
     for copy in v_waits:
         copy.wait_recv()
     vectors_sum = v_shards[0]
@@ -600,8 +615,11 @@
         tokens_out[rows, :] = hidden_own[rows, :] + inverse * inner
         return carry
 
+    q_back.wait_recv()
+    load(9).start()
     lax.fori_loop(0, 4, close, 0)
-    q_back.wait_recv()
+    load(9).wait()
+    load(10).wait()
     for copy in pending:
         copy.wait_send()
     for at in range(2):
@@ -639,8 +657,10 @@
     vm = pltpu.VMEM
     return pl.pallas_call(
         partial(back_kernel, shards, dp_bits),
-        in_specs=[pl.BlockSpec(memory_space=vm)] * 11 + [pl.BlockSpec(memory_space=pl.ANY)] * 11,
-        out_specs=[pl.BlockSpec(memory_space=vm)] * 4,
+        in_specs=[pl.BlockSpec(memory_space=pl.ANY)] * 3
+        + [pl.BlockSpec(memory_space=vm)] * 8
+        + [pl.BlockSpec(memory_space=pl.ANY)] * 11,
+        out_specs=[pl.BlockSpec(memory_space=vm)] * 2 + [pl.BlockSpec(memory_space=pl.ANY)] * 2,
         out_shape=[
             jax.ShapeDtypeStruct((block, width), f32),
             jax.ShapeDtypeStruct(vectors.shape, f32),
@@ -648,6 +668,11 @@
             jax.ShapeDtypeStruct((PIECES, early_rows + late_rows, width), bf16),
         ],
         scratch_shapes=[
+            vm((heads, seq_len, LANES), bf16),
+            vm((heads, seq_len, LANES), bf16),
+            vm((heads, seq_len, LANES), bf16),
+            vm((PIECES, count, width), bf16),
+            vm((PIECES, early_rows + late_rows, width), bf16),
             vm((heads, seq_len, LANES), bf16),
             vm((heads, seq_len, LANES), f32),
             vm((heads, seq_len, LANES), f32),
@@ -687,7 +712,7 @@
             vm((shards, early_rows, width), bf16),
             pltpu.SemaphoreType.DMA((copies,)),
             pltpu.SemaphoreType.DMA((copies,)),
-            pltpu.SemaphoreType.DMA((7,)),
+            pltpu.SemaphoreType.DMA((12,)),
         ],
         compiler_params=pltpu.CompilerParams(
             collective_id=1, has_side_effects=True, vmem_limit_bytes=67043328
@@ -715,11 +740,16 @@
     fc1_bias_out,
     *vector_outs
 ):
-    fc_rows, proj_rows = fc1_out.shape[0], proj_out.shape[0]
-    fc2_out[...] = weights_ref[0, :fc_rows].astype(jnp.float32)
-    fc1_out[...] = weights_ref[0, fc_rows : 2 * fc_rows].astype(jnp.float32)
-    proj_out[...] = weights_ref[0, 2 * fc_rows : 2 * fc_rows + proj_rows].astype(jnp.float32)
-    qkv_out[...] = qkv_ref[0].astype(jnp.float32)
+    group = weights_ref.shape[0]
+    fc_rows, proj_rows, qkv_rows = (ref.shape[0] // group for ref in (fc1_out, proj_out, qkv_out))
+    for at in range(group):
+        for out, source, first, count in (
+            (fc2_out, weights_ref, 0, fc_rows),
+            (fc1_out, weights_ref, fc_rows, fc_rows),
+            (proj_out, weights_ref, 2 * fc_rows, proj_rows),
+            (qkv_out, qkv_ref, 0, qkv_rows),
+        ):
+            out[at * count : (at + 1) * count, :] = source[at, first : first + count].astype(jnp.float32)
     tokens_out[...] = tokens_ref[...]
     rows_out[...] = rows_ref[...]
 
@@ -740,17 +770,19 @@
     f32 = jnp.float32
     _, rows, width = weights.shape
     qkv_rows = qkv.shape[1]
-    token_rows = tokens.shape[0] // PIECES
+    steps = UNPACK_STEPS
+    group = PIECES // steps
+    token_rows = tokens.shape[0] // steps
     columns = proj_rows * PIECES
-    counts = (fc_rows, fc_rows, proj_rows, qkv_rows, token_rows)
+    counts = (*(group * count for count in (fc_rows, fc_rows, proj_rows, qkv_rows)), token_rows)
     vector = pl.BlockSpec((width,), lambda i: (0,))
     token_spec = pl.BlockSpec((token_rows, width), lambda i: (i, 0))
     return pl.pallas_call(
         unpack_kernel,
-        grid=(PIECES,),
+        grid=(steps,),
         in_specs=[
-            pl.BlockSpec((1, qkv_rows, width), lambda i: (i, 0, 0)),
-            pl.BlockSpec((1, rows, width), lambda i: (i, 0, 0)),
+            pl.BlockSpec((group, qkv_rows, width), lambda i: (i, 0, 0)),
+            pl.BlockSpec((group, rows, width), lambda i: (i, 0, 0)),
             pl.BlockSpec(totals.shape, lambda i: (0, 0)),
             token_spec,
             token_spec,
@@ -758,7 +790,7 @@
         out_specs=[pl.BlockSpec((count, width), lambda i: (i, 0)) for count in counts]
         + [token_spec, pl.BlockSpec((2, columns), lambda i: (0, 0))]
         + [vector] * 9,
-        out_shape=[jax.ShapeDtypeStruct((PIECES * count, width), f32) for count in counts]
+        out_shape=[jax.ShapeDtypeStruct((steps * count, width), f32) for count in counts]
         + [jax.ShapeDtypeStruct(rows_in.shape, rows_in.dtype), jax.ShapeDtypeStruct((2, columns), f32)]
         + [jax.ShapeDtypeStruct((width,), f32)] * 9,
         name="unpack",
@@ -1224,19 +1256,39 @@
     scale_two_ref,
     tokens_ref,
     cotangent_ref,
-    block_out,
-    hidden_grad_out,
+    block_result,
+    hidden_grad_result,
     pair_grads_out,
     single_grads_out,
     vectors_out,
-    a_keep,
-    a_away,
-    b_keep,
-    b_away,
-    a_early,
-    a_early_away,
-    b_early,
-    b_early_away,
+    *rest,
+):
+    results, rest = rest[:8], rest[8:]
+    parts, rest = rest[:8], rest[8:]
+    middle_body(
+        shards,
+        dp_bits,
+        (pairs, singles, weights_ref, fc1_bias_ref),
+        (proj_bias_ref, scale_one_ref, gain_ref, shift_ref, fc2_bias_ref, scale_two_ref),
+        (tokens_ref, cotangent_ref),
+        (block_result, hidden_grad_result, *results),
+        (pair_grads_out, single_grads_out, vectors_out),
+        parts,
+        *rest,
+    )
+
+
+def middle_body(
+    shards,
+    dp_bits,
+    sources,
+    parameter_refs,
+    row_refs,
+    results,
+    outs,
+    parts,
+    block_out,
+    hidden_grad_out,
     weights,
     attended,
     proj,
@@ -1259,7 +1311,16 @@
     send,
     recv,
     local,
+    stored,
 ):
+    pairs, singles, weights_ref, fc1_bias_ref = sources
+    tokens_ref, cotangent_ref = row_refs
+    pair_grads_out, single_grads_out, vectors_out = outs
+    a_keep, a_away, b_keep, b_away, a_early, a_early_away, b_early, b_early_away = parts
+
+    def store(at):
+        return pltpu.make_async_copy((block_out, hidden_grad_out, *parts)[at], results[at], stored.at[at])
+
     f32, bf16 = jnp.float32, jnp.bfloat16
     member, here = lax.axis_index("dp"), lax.axis_index("tensor")
     core, x_bit, y_bit = bit_of(member, 0), bit_of(member, 1), bit_of(member, 2)
@@ -1271,7 +1332,7 @@
     slots = iter(range(send.shape[0]))
     proj_bias, scale_one, gain, shift, fc2_bias, scale_two = (
         ref[...].reshape(1, width)
-        for ref in (proj_bias_ref, scale_one_ref, gain_ref, shift_ref, fc2_bias_ref, scale_two_ref)
+        for ref in parameter_refs
     )
 
     def copy_to(src, dst, at, **peer):
@@ -1382,6 +1443,7 @@
         )
 
     scale_two_sum, fc2_bias_sum = each_chunk(turn, (empty, empty))
+    store(0).start()
 
     split = shards // 2
 
@@ -1484,6 +1546,7 @@
         )
 
     gain_sum, shift_sum, scale_one_sum, proj_bias_sum = each_chunk(leave, (empty,) * 4)
+    store(1).start()
     for at, value in enumerate(
         (empty, empty, proj_bias_sum, scale_one_sum, gain_sum, shift_sum, fc2_bias_sum, scale_two_sum)
     ):
@@ -1551,9 +1614,15 @@
                             weights[own + piece, owner, fc_rows:, :], got[piece, owner]
                         )
 
+    for at in range(2, 6):
+        store(at).start()
     early_sides()
+    for at in range(6, 10):
+        store(at).start()
     for copy in back:
         copy.wait_recv()
+    for at in range(10):
+        store(at).wait()
     for copy in back + side_copies():
         copy.wait_send()
     for owner in range(shards):
@@ -1575,7 +1644,9 @@
     return pl.pallas_call(
         partial(middle_kernel, shards, dp_bits),
         in_specs=[on_chip, on_chip, pl.BlockSpec(memory_space=pl.ANY)] + [on_chip] * 9,
-        out_specs=[on_chip] * 13,
+        out_specs=[pl.BlockSpec(memory_space=pl.ANY)] * 2
+        + [on_chip] * 3
+        + [pl.BlockSpec(memory_space=pl.ANY)] * 8,
         out_shape=[
             jax.ShapeDtypeStruct((block, width), bf16),
             jax.ShapeDtypeStruct((block, width), f32),
@@ -1591,7 +1662,11 @@
             early_half,
             early_half,
         ],
-        scratch_shapes=[
+        scratch_shapes=[vm(quarter.shape, bf16)] * 4
+        + [vm(early_half.shape, bf16)] * 4
+        + [
+            vm((block, width), bf16),
+            vm((block, width), f32),
             vm(weights.shape, bf16),
             vm((block, width), bf16),
             vm((width, width), bf16),
@@ -1614,6 +1689,7 @@
             pltpu.SemaphoreType.DMA((copies,)),
             pltpu.SemaphoreType.DMA((copies,)),
             pltpu.SemaphoreType.DMA((shards,)),
+            pltpu.SemaphoreType.DMA((10,)),
         ],
         compiler_params=pltpu.CompilerParams(
             collective_id=2, has_side_effects=True, vmem_limit_bytes=62 * 1024 * 1024

time: 304 us -> 298 us (0.980)
  Pallas kernels: 303 us -> 296 us
where the time goes in v8:
time: 298 us; the launch traced here: 297 us
  Pallas kernels  296 us (99%)
    pallas_call x1, Pallas kernels, back(): pl.pallas_call(partial(back_kernel, shards, dp_bits), in_specs=[pl.BlockS...  112 us
    pallas_call x1, Pallas kernels, start(): pl.pallas_call(partial(start_kernel, shards, dp_bits), in_specs=[on_chip]...  110 us
    pallas_call x1, Pallas kernels, middle(): pl.pallas_call(partial(middle_kernel, shards, dp_bits), in_specs=[on_chip...  67.8 us
    pallas_call x1, Pallas kernels, unpack(): pl.pallas_call(unpack_kernel, grid=(steps,), in_specs=[pl.BlockSpec((grou...  6.24 us

profile of v8, /device:TPU:16, one launch (start us, length us, event | category | flops | bytes accessed | tf_op | source)
XLA Modules:
  0.0 297.3 jit_solution(15431091672255882365)
XLA Ops:
  0.6 110.1 %start.1 = (bf16[2304,768]{1,0:T(8,128)(2,1)}, bf16[3,2304,128]{2,1,0:T(8,128)(2,1)}, bf16[3,2304,128]{2,1,0:T(8,128)(2,1)}, bf16[3,2304,128]{2,1,0:T(8,128)(2,1...) custom-call(bf16[576,768]{1,0:T(8,128)(2,1)} %tokens_ref.5, ...), custom_call_target="tpu_custom_call" | custom-call | flops 2038431744 | bytes 17694720 | tf_op jit(solution)/shard_map/start/pallas_call | solution.py:1194
  110.7 67.8 %middle.1 = (bf16[576,768]{1,0:T(8,128)(2,1)}, f32[576,768]{1,0:T(8,128)}, bf16[4,576,128]{2,1,0:T(8,128)(2,1)}, bf16[4,288,128]{2,1,0:T(8,128)(2,1)}, f32[16,76...) custom-call(bf16[4,576,128]{2,1,0:T(8,128)(2,1)} %get-tuple-element., ...), custom_call_target="tpu_custom_call" | custom-call | flops 16307453952 | bytes 17694720 | tf_op jit(solution)/shard_map/middle/pallas_call | solution.py:1644
  178.5 112.4 %back.1 = (f32[576,768]{1,0:T(8,128)}, f32[16,768]{1,0:T(8,128)}, bf16[8,72,768]{2,1,0:T(8,128)(2,1)}, bf16[8,224,768]{2,1,0:T(8,128)(2,1)}) custom-call(bf16[3,2304,128]{2,1,0:T(8,128)(2,1)} %get-tuple-element.59.q_in, bf16[3,2304,128]{2,1,0:T(8,128)(2,1)} %get-tuple-element.60.k_in, bf16[3,2304,128]{2,1,0:T(8,128)(2,1)} %get-tuple-element.61.v_in, ...), custom_call_target="tpu_custom_call" | custom-call | flops 20384317440 | bytes 17694720 | tf_op jit(solution)/shard_map/back/pallas_call | solution.py:658
  290.9 6.2 %unpack.1 = (f32[768,768]{1,0:T(8,128)}, f32[768,768]{1,0:T(8,128)}, f32[192,768]{1,0:T(8,128)}, f32[576,768]{1,0:T(8,128)}, f32[576,768]{1,0:T(8,128)}, /*index...) custom-call(bf16[8,72,768]{2,1,0:T(8,128)(2,1)} %get-tuple-element.8, ...), custom_call_target="tpu_custom_call" | custom-call | tf_op jit(solution)/shard_map/unpack/pallas_call | solution.py:780

commit v9 on v8

--- a/solution.py
+++ b/solution.py
@@ -1238,7 +1238,7 @@
     )(tokens, ids, gain, shift, qkv, qv_bias, fc1, fc2, proj, fc1_bias)
 
 
-CHUNK = 32
+CHUNK = 192
 
 
 def middle_kernel(
@@ -1361,7 +1361,7 @@
         return weights[:, owner, proj_first : proj_first + proj_rows, :].reshape(columns, width)
 
     def chunk(at):
-        return pl.ds(pl.multiple_of(at * CHUNK, CHUNK), CHUNK)
+        return pl.ds(pl.multiple_of(at * CHUNK, 16), CHUNK)
 
     def each_chunk(body, init):
         return lax.fori_loop(0, block // CHUNK, body, init)

time: 298 us -> 291 us (0.977)
  Pallas kernels: 296 us -> 290 us
    pallas_call x1, Pallas kernels: 67.8 us -> 59.9 us  [middle(): pl.pallas_call(partial(middle_kernel, shards, dp_bits), in_specs=[on_chip...]
where the time goes in v9:
time: 291 us; the launch traced here: 290 us
  Pallas kernels  290 us (100%)
    pallas_call x1, Pallas kernels, back(): pl.pallas_call(partial(back_kernel, shards, dp_bits), in_specs=[pl.BlockS...  113 us
    pallas_call x1, Pallas kernels, start(): pl.pallas_call(partial(start_kernel, shards, dp_bits), in_specs=[on_chip]...  110 us
    pallas_call x1, Pallas kernels, middle(): pl.pallas_call(partial(middle_kernel, shards, dp_bits), in_specs=[on_chip...  59.9 us
    pallas_call x1, Pallas kernels, unpack(): pl.pallas_call(unpack_kernel, grid=(steps,), in_specs=[pl.BlockSpec((grou...  6.24 us

profile of v9, /device:TPU:16, one launch (start us, length us, event | category | flops | bytes accessed | tf_op | source)
XLA Modules:
  0.0 290.4 jit_solution(8144991761934881569)
XLA Ops:
  0.6 110.1 %start.1 = (bf16[2304,768]{1,0:T(8,128)(2,1)}, bf16[3,2304,128]{2,1,0:T(8,128)(2,1)}, bf16[3,2304,128]{2,1,0:T(8,128)(2,1)}, bf16[3,2304,128]{2,1,0:T(8,128)(2,1...) custom-call(bf16[576,768]{1,0:T(8,128)(2,1)} %tokens_ref.5, ...), custom_call_target="tpu_custom_call" | custom-call | flops 2038431744 | bytes 17694720 | tf_op jit(solution)/shard_map/start/pallas_call | solution.py:1194
  110.7 59.9 %middle.1 = (bf16[576,768]{1,0:T(8,128)(2,1)}, f32[576,768]{1,0:T(8,128)}, bf16[4,576,128]{2,1,0:T(8,128)(2,1)}, bf16[4,288,128]{2,1,0:T(8,128)(2,1)}, f32[16,76...) custom-call(bf16[4,576,128]{2,1,0:T(8,128)(2,1)} %get-tuple-element., ...), custom_call_target="tpu_custom_call" | custom-call | flops 16307453952 | bytes 17694720 | tf_op jit(solution)/shard_map/middle/pallas_call | solution.py:1644
  170.7 113.3 %back.1 = (f32[576,768]{1,0:T(8,128)}, f32[16,768]{1,0:T(8,128)}, bf16[8,72,768]{2,1,0:T(8,128)(2,1)}, bf16[8,224,768]{2,1,0:T(8,128)(2,1)}) custom-call(bf16[3,2304,128]{2,1,0:T(8,128)(2,1)} %get-tuple-element.59.q_in, bf16[3,2304,128]{2,1,0:T(8,128)(2,1)} %get-tuple-element.60.k_in, bf16[3,2304,128]{2,1,0:T(8,128)(2,1)} %get-tuple-element.61.v_in, ...), custom_call_target="tpu_custom_call" | custom-call | flops 20384317440 | bytes 17694720 | tf_op jit(solution)/shard_map/back/pallas_call | solution.py:658
  284.0 6.2 %unpack.1 = (f32[768,768]{1,0:T(8,128)}, f32[768,768]{1,0:T(8,128)}, f32[192,768]{1,0:T(8,128)}, f32[576,768]{1,0:T(8,128)}, f32[576,768]{1,0:T(8,128)}, /*index...) custom-call(bf16[8,72,768]{2,1,0:T(8,128)(2,1)} %get-tuple-element.8, ...), custom_call_target="tpu_custom_call" | custom-call | tf_op jit(solution)/shard_map/unpack/pallas_call | solution.py:780
